TPU v7x, 32 devices: a whole 2x2x4 slice. The times are simulated.
32 devices in a mesh: farm: 4 (over z), nx: 4 (over y, core), ny: 2 (over x).
Axes of the slice: x: 2, y: 2, z: 4, core: 2. Of those that a mesh axis runs over, the one named last changes fastest.
Arguments:
- coarse_tiles: float32 [256, 32, 2048], P('farm', ('nx', 'ny')), may hold values from -6 to 6
- prolong_taps: float32 [3, 8], replicated, may hold values from 0.2 to 0.8
- tile_lists: int32 [4, 4], replicated, may hold values from 0 to 255, as said below
- nest_owner: int32 [4], replicated, may hold values from 0 to 3, each once
Outputs:
- updated_tiles: float32 [256, 32, 2048], P('farm', ('nx', 'ny'))
- nest_pressure: float32 [4, 256, 128, 128], P('farm', None, ('nx', 'ny'))
Inputs may be any that keep to these rules, and one draw needn't show every extreme that they name: `tile_lists`: all entries are distinct; in each nest's row the values tile // 64 take every farm index exactly once. `nest_owner`: each farm index runs exactly one nest.
All inputs are finite; a program needn't handle non-finite values.
Results may differ from a plain program's by a relative error of at most 0.0003.
Values sent between devices are 32-bit elements; how exact they have to be, the bound alone decides.
No kernel may reach another device: no remote copies, remote signals or barrier semaphores. Data moves between devices by JAX's collectives and lax.ppermute only.
A program may use at most 384 MiB of HBM per device.

v0:
```python
import math

import jax
import jax.numpy as jnp
from jax import lax
from jax.sharding import PartitionSpec as P

TILE_Z = 32
REFINE = 4
TAPS = 8
CH = 4
NFX = 256
NFY = 128
NFZ = 128


exact_mode = lax.Precision.HIGHEST


def with_halo(block, sides, width):
    for axis, dim in sides:
        count = lax.axis_size(axis)
        forward = [(i, i + 1) for i in range(count - 1)]
        forward.append((count - 1, 0))
        backward = [(target, source) for source, target in forward]
        low = lax.ppermute(
            lax.slice_in_dim(block, block.shape[dim] - width, None, axis=dim), axis, forward
        )
        high = lax.ppermute(lax.slice_in_dim(block, 0, width, axis=dim), axis, backward)
        block = jnp.concatenate([low, block, high], axis=dim)
    return block


def prolong_matrix(taps_row, fine_count, coarse_count, fine_start, coarse_start, period):
    fine_index = fine_start + jnp.arange(fine_count, dtype=jnp.int32)
    coarse_index = coarse_start + jnp.arange(coarse_count, dtype=jnp.int32)
    offset = jnp.mod(fine_index[:, None] - REFINE * coarse_index[None, :] + 2, period)
    tap_match = offset[:, :, None] == jnp.arange(TAPS, dtype=jnp.int32)[None, None, :]
    return jnp.sum(
        jnp.where(tap_match, taps_row[None, None, :], jnp.zeros((), jnp.float32)), axis=2
    )


def eigen_part(freq_start, freq_count, length):
    freq_index = (freq_start + jnp.arange(freq_count, dtype=jnp.int32)).astype(jnp.float32)
    return 4.0 * jnp.sin(freq_index * (math.pi / length)) ** 2


def slot_lists(tile_lists, nest_owner, slot_ids):
    owner_match = nest_owner[None, :] == slot_ids[:, None]
    return jnp.sum(jnp.where(owner_match[:, :, None], tile_lists[None, :, :], 0), axis=1)


def wave_tables(length):
    index_row = jnp.arange(length, dtype=jnp.int32)
    turns = jnp.mod(index_row[:, None] * index_row[None, :], length).astype(jnp.float32)
    phase_angle = turns * (2.0 * math.pi / length)
    return (jnp.cos(phase_angle), jnp.sin(phase_angle))


def apply_along(matrix, values, axis_id):
    moved = jnp.tensordot(matrix, values, axes=([1], [axis_id]), precision=exact_mode)
    return jnp.moveaxis(moved, 0, axis_id)


def forward_pair(real_part, imag_part, cosines, sines, axis_id):
    return (
        apply_along(cosines, real_part, axis_id) + apply_along(sines, imag_part, axis_id),
        apply_along(cosines, imag_part, axis_id) - apply_along(sines, real_part, axis_id),
    )


def inverse_pair(real_part, imag_part, cosines, sines, axis_id, length):
    return (
        (apply_along(cosines, real_part, axis_id) - apply_along(sines, imag_part, axis_id))
        / length,
        (apply_along(sines, real_part, axis_id) + apply_along(cosines, imag_part, axis_id))
        / length,
    )


def to_real_space(real_part, imag_part, cos_x, sin_x, cos_z, sin_z):
    real_z, imag_z = inverse_pair(real_part, imag_part, cos_z, sin_z, 2, NFZ)
    return (apply_along(cos_x, real_z, 0) - apply_along(sin_x, imag_z, 0)) / NFX


def local(coarse_tiles, prolong_taps, tile_lists, nest_owner):
    farm_count = lax.axis_size("farm")
    farm_index = lax.axis_index("farm")
    groups = lax.axis_size(("nx", "ny"))
    group_index = lax.axis_index(("nx", "ny"))
    local_tiles, row_count, row_width = coarse_tiles.shape
    tile_edge = row_width // (CH * TILE_Z)
    pair_count = tile_lists.shape[1]
    slot_ids = jnp.arange(farm_count, dtype=jnp.int32)
    slot_tiles = slot_lists(tile_lists, nest_owner, slot_ids)
    owned_ids = farm_index * local_tiles + jnp.arange(local_tiles, dtype=jnp.int32)
    selector = (slot_tiles[:, :, None] == owned_ids[None, None, :]).astype(jnp.float32)
    send_pick = jnp.sum(selector, axis=1)
    flat_tiles = coarse_tiles.reshape(local_tiles, row_count * row_width)
    outgoing = jnp.dot(send_pick, flat_tiles, precision=exact_mode)
    incoming = lax.all_to_all(
        outgoing.reshape(farm_count, row_count, row_width),
        "farm",
        split_axis=0,
        concat_axis=0,
        tiled=True,
    )
    my_tiles = slot_tiles[farm_index]
    home_index = my_tiles // local_tiles
    order_pick = (home_index[:, None] == slot_ids[None, :]).astype(jnp.float32)
    nest_rows = jnp.dot(
        order_pick, incoming.reshape(farm_count, row_count * row_width), precision=exact_mode
    )
    nest_rows = nest_rows.reshape(pair_count, row_count, row_width)
    framed = with_halo(nest_rows, ((("nx", "ny"), 1),), 1)
    width_x = pair_count * tile_edge
    coarse = framed.reshape(pair_count, row_count + 2, CH, tile_edge, TILE_Z).transpose(
        2, 0, 3, 1, 4
    )
    coarse = coarse.reshape(CH, width_x, row_count + 2, TILE_Z)
    fine_rows = REFINE * row_count
    matrix_x = prolong_matrix(prolong_taps[0], NFX, width_x, 0, 0, NFX)
    matrix_y = prolong_matrix(
        prolong_taps[1],
        fine_rows + 1,
        row_count + 2,
        fine_rows * group_index,
        row_count * group_index - 1,
        NFY,
    )
    matrix_z = prolong_matrix(prolong_taps[2], NFZ, TILE_Z, 0, 0, NFZ)
    refined = apply_along(matrix_x, coarse, 1)
    refined = apply_along(matrix_z, refined, 3)
    refined = apply_along(matrix_y, refined, 2)
    own_rows = refined[:, :, :fine_rows, :]
    spread = (
        jnp.roll(own_rows[0], -1, 0)
        - own_rows[0]
        + (refined[1, :, 1:, :] - own_rows[1])
        + (jnp.roll(own_rows[2], -1, 2) - own_rows[2])
    )
    cos_y, sin_y = wave_tables(NFY)
    cos_z, sin_z = wave_tables(NFZ)
    ahead_cos, ahead_sin = wave_tables(NFX)
    behind_cos, behind_sin = (ahead_cos, ahead_sin)
    real_x = apply_along(ahead_cos, spread, 0)
    imag_x = -apply_along(ahead_sin, spread, 0)
    real_xz, imag_xz = forward_pair(real_x, imag_x, cos_z, sin_z, 2)
    columns = lax.all_to_all(
        jnp.stack([real_xz, imag_xz]), ("nx", "ny"), split_axis=1, concat_axis=2, tiled=True
    )
    span = ahead_cos.shape[0] // groups
    real_y, imag_y = forward_pair(columns[0], columns[1], cos_y, sin_y, 1)
    eigen_y = eigen_part(0, NFY, NFY)
    eigen_z = eigen_part(0, NFZ, NFZ)
    eigen_sum = (
        eigen_part(group_index * span, span, NFX)[:, None, None]
        + eigen_y[None, :, None]
        + eigen_z[None, None, :]
    )
    nonzero = eigen_sum > 0
    factor = jnp.where(nonzero, -1.0 / jnp.where(nonzero, eigen_sum, 1.0), 0.0)
    real_p = real_y * factor
    imag_p = imag_y * factor
    back_real, back_imag = inverse_pair(real_p, imag_p, cos_y, sin_y, 1, NFY)
    theta = jnp.arange(NFY, dtype=jnp.float32) * (2.0 * math.pi / NFY)
    cos_diff = (1.0 - jnp.cos(theta))[None, :, None]
    sin_diff = jnp.sin(theta)[None, :, None]
    real_g = real_p * cos_diff - imag_p * sin_diff
    imag_g = real_p * sin_diff + imag_p * cos_diff
    grad_real, grad_imag = inverse_pair(real_g, imag_g, cos_y, sin_y, 1, NFY)
    returned = lax.all_to_all(
        jnp.stack([back_real, back_imag, grad_real, grad_imag]),
        ("nx", "ny"),
        split_axis=2,
        concat_axis=1,
        tiled=True,
    )
    pressure = to_real_space(returned[0], returned[1], behind_cos, behind_sin, cos_z, sin_z)
    grad_y = to_real_space(returned[2], returned[3], behind_cos, behind_sin, cos_z, sin_z)
    new_fields = jnp.stack(
        [
            own_rows[0] - (pressure - jnp.roll(pressure, 1, 0)),
            own_rows[1] - grad_y,
            own_rows[2] - (pressure - jnp.roll(pressure, 1, 2)),
            own_rows[3] + pressure,
        ]
    )
    blocks = new_fields.reshape(CH, width_x, REFINE, row_count, REFINE, TILE_Z, REFINE).mean(
        axis=(2, 4, 6)
    )
    restored = blocks.reshape(CH, pair_count, tile_edge, row_count, TILE_Z).transpose(1, 3, 0, 2, 4)
    restored = restored.reshape(pair_count, row_count * row_width)
    returning = jnp.dot(order_pick.T, restored, precision=exact_mode)
    arrived = lax.all_to_all(
        returning.reshape(farm_count, row_count, row_width),
        "farm",
        split_axis=0,
        concat_axis=0,
        tiled=True,
    )
    placed = jnp.dot(
        send_pick.T, arrived.reshape(farm_count, row_count * row_width), precision=exact_mode
    )
    covered = jnp.sum(send_pick, axis=0)
    updated = coarse_tiles * (1.0 - covered)[:, None, None] + placed.reshape(
        local_tiles, row_count, row_width
    )
    return (updated, pressure[None])


def solution(mesh):
    return jax.shard_map(
        local,
        mesh=mesh,
        in_specs=(P("farm", ("nx", "ny"), None), P(), P(), P()),
        out_specs=(P("farm", ("nx", "ny"), None), P("farm", None, ("nx", "ny"), None)),
        check_vma=False,
    )
```

profile of v0, /device:TPU:0, one launch (start us, length us, event | category | flops | bytes accessed | tf_op | source)
XLA Modules:
  0.0 692.7 jit_solution(1305062172157522703)
XLA Ops:
  3.3 3.8 fusion.3
  7.8 6.3 all-to-all-start
  14.9 5.4 all-to-all-done
  27.8 5.1 fusion.145
  32.9 12.2 %convolution_bitcast_fusion = f32[4,256,17,128]{3,2,1,0:T(8,128)S(1)} fusion(f32[4,256,6,128]{3,1,2,0:T(8,128)S(1)} %fusion.145, f32[17,6]{0,1:T(8,128)S(1)} %select_reduce_fusion.2), kind=kOutput, calls=%fused_computation.2 | convolution fusion | flops 160432128 | bytes 12059032 | tf_op jit(solution)/shard_map/dot_general | solution.py:62
  46.1 3.6 copy-done
  50.4 3.3 fusion.43
  53.7 3.4 fusion.45
  66.1 4.8 copy.174
  70.8 4.6 all-to-all-start.1
  75.6 48.3 %all-to-all-done.1 = f32[2,256,16,128]{3,2,0,1:T(8,128)} async-done(((f32[2,256,16,128]{3,2,0,1:T(8,128)}), f32[2,256,16,128]{3,2,0,1:T(8,128)}, u32[]{:S(2)}, u32[]{:S(2)}) %all-to-all-start.1) | async-done | bytes 4194336 | tf_op jit(solution)/shard_map/all_to_all | solution.py:150
  156.1 4.9 copy.176
  161.0 96.9 %all_to_all.40 = f32[4,32,128,128]{3,1,0,2:T(8,128)} all-to-all(f32[4,32,128,128]{3,1,0,2:T(8,128)S(1)} %copy.176), channel_id=1, replica_groups=mesh['farm'=4,'nx'=4,'ny'=2] {'nx','ny'}, dimensions={2} | all-to-all | bytes 16777216 | tf_op jit(solution)/shard_map/all_to_all | solution.py:173
  257.9 8.2 %copy.177 = f32[4,32,128,128]{3,2,1,0:T(8,128)S(1)} copy(f32[4,32,128,128]{3,1,0,2:T(8,128)} %all_to_all.40) | data formatting | bytes 16777216 | tf_op jit(solution)/shard_map/all_to_all | solution.py:173
  288.5 3.0 fusion.21
  305.7 4.9 fusion.10
  310.5 71.4 %stack.47 = f32[1,64,4,4,4,32,4]{6,5,4,3,2,1,0:T(8,128)} reshape(f32[256,16,128]{2,1,0:T(8,128)} %get-tuple-element.20) | data formatting | bytes 4194304 | tf_op jit(solution)/shard_map/stack | solution.py:182
  382.0 70.6 %stack.50 = f32[1,64,4,4,4,32,4]{6,5,4,3,2,1,0:T(8,128)} reshape(f32[256,16,128]{2,1,0:T(8,128)S(1)} %get-tuple-element.18) | data formatting | bytes 4194304 | tf_op jit(solution)/shard_map/stack | solution.py:182
  452.5 71.5 %stack.49 = f32[1,64,4,4,4,32,4]{6,5,4,3,2,1,0:T(8,128)} reshape(f32[256,16,128]{2,1,0:T(8,128)} %get-tuple-element.21) | data formatting | bytes 4194304 | tf_op jit(solution)/shard_map/stack | solution.py:182
  524.1 70.7 %stack.48 = f32[1,64,4,4,4,32,4]{6,5,4,3,2,1,0:T(8,128)} reshape(f32[256,16,128]{2,1,0:T(8,128)S(1)} %copy-done.2) | data formatting | bytes 4194304 | tf_op jit(solution)/shard_map/stack | solution.py:182
  594.8 80.5 %maximum_reduce_fusion = f32[4,64,4,32]{3,2,1,0:T(4,128)S(1)} fusion(f32[1,64,4,4,4,32,4]{6,5,4,3,2,1,0:T(8,128)} %stack.50, f32[1,64,4,4,4,32,4]{6,5,4,3,2,1,0:T(8,128)} %stack.49, f32[1,64,4,4,4,32,4]{6,5,4,3,2,1,0:T(8,128)} %stack.48, f32[1,64,4,4,4,32,4]{6,5,4,3,2,1,0:T(8,128)} %stack.47), kind=kLoop, calls=%fused_computation | loop fusion | flops 8355840 | bytes 8519680 | tf_op jit(solution)/shard_map/reduce_sum | solution.py:190
  677.1 3.3 all-to-all-start.3
  680.5 6.4 all-to-all-done.3
  686.9 3.0 convolution_add_fusion
  (114 shorter events, 95.2 us)
Async XLA Ops:
  0.6 13.6 %copy-start.9 = (f32[3,8]{1,0:T(4,128)S(1)}, f32[3,8]{1,0:T(4,128)}, u32[]{:S(2)}) copy-start(f32[3,8]{1,0:T(4,128)} %param.5) | copy-start | bytes 292
  2.7 0.6 copy-start.5
  7.8 12.4 %all-to-all-start = ((f32[4,4,2048]{2,1,0:T(4,128)}), f32[4,4,2048]{2,1,0:T(4,128)S(1)}, u32[]{:S(2)}, u32[]{:S(2)}) async-start(f32[4,4,2048]{2,1,0:T(4,128)} %copy.167), calls=%async_computation | async-start | bytes 262144 | tf_op jit(solution)/shard_map/all_to_all | solution.py:102
  14.2 6.4 copy-start.7
  20.6 4.5 collective-permute-start
  22.2 4.2 collective-permute-start.1
  45.1 4.5 copy-start
  70.8 53.1 %all-to-all-start.1 = ((f32[2,256,16,128]{3,2,0,1:T(8,128)}), f32[2,256,16,128]{3,2,0,1:T(8,128)}, u32[]{:S(2)}, u32[]{:S(2)}) async-start(f32[2,256,16,128]{3,2,0,1:T(8,128)} %copy.174), calls=%async_computation.1 | async-start | bytes 8388608 | tf_op jit(solution)/shard_map/all_to_all | solution.py:150
  282.9 11.6 %slice-start = ((s8[12582912]{0:T(1024)(128)(4,1)}), s8[4194304]{0:T(1024)(128)(4,1)S(1)}, s32[]{:S(2)}) async-start(s8[12582912]{0:T(1024)(128)(4,1)} %bitcast.234), calls=%async_computation.4 | async-start | bytes 8388608
  283.1 11.4 %slice-start.1 = ((s8[12582912]{0:T(1024)(128)(4,1)}), s8[4194304]{0:T(1024)(128)(4,1)S(1)}, s32[]{:S(2)}) async-start(s8[12582912]{0:T(1024)(128)(4,1)} %bitcast.234), calls=%async_computation.5 | async-start | bytes 8388608
  288.5 6.0 slice-start.2
  297.2 8.5 %copy-start.1 = (f32[256,16,128]{2,1,0:T(8,128)}, f32[256,16,128]{2,1,0:T(8,128)S(1)}, u32[]{:S(2)}) copy-start(f32[256,16,128]{2,1,0:T(8,128)S(1)} %get-tuple-element.19) | copy-start | bytes 6291460
  302.7 3.0 copy-start.4
  452.5 71.5 %copy-start.2 = (f32[256,16,128]{2,1,0:T(8,128)S(1)}, f32[256,16,128]{2,1,0:T(8,128)}, u32[]{:S(2)}) copy-start(f32[256,16,128]{2,1,0:T(8,128)} %get-tuple-element.22) | copy-start | bytes 6291460
  675.3 0.8 copy-start.8
  675.5 4.9 copy-start.10
  675.5 11.3 %copy-start.3 = (f32[64,4,2048]{2,1,0:T(4,128)S(1)}, f32[64,4,2048]{2,1,0:T(4,128)}, u32[]{:S(2)}) copy-start(f32[64,4,2048]{2,1,0:T(4,128)} %param.4) | copy-start | bytes 6291460
  675.5 11.3 %copy-start.6 = (f32[4,64]{1,0:T(4,128)S(1)}, f32[4,64]{1,0:T(4,128)}, u32[]{:S(2)}) copy-start(f32[4,64]{1,0:T(4,128)} %copy-done.5) | copy-start | bytes 3076
  677.1 9.7 %all-to-all-start.3 = ((f32[4,4,2048]{2,1,0:T(4,128)}), f32[4,4,2048]{2,1,0:T(4,128)S(1)}, u32[]{:S(2)}, u32[]{:S(2)}) async-start(f32[4,4,2048]{2,1,0:T(4,128)} %copy.198), calls=%async_computation.3 | async-start | bytes 262144 | tf_op jit(solution)/shard_map/all_to_all | solution.py:196
where the time goes:
time: 696 us; the launch traced here: 693 us
  local copies, waits for them, and re-layouts  320 us (46%)
  matrix products  101 us (15%)
  blocking collectives  96.9 us (14%)
  other arithmetic  93.1 us (13%)
  waiting for transfers between devices  62.7 us (9%)
  starting transfers between devices  17.2 us (2%)
    another operation x4, local copies, waits for them, and re-layouts, local(): jnp.stack([own_rows[0] - (pressure - jnp.roll(pressure, 1, 0)), own_rows[...  284 us
    all_to_all x1, blocking collectives, local(): lax.all_to_all(jnp.stack([back_real, back_imag, grad_real, grad_imag]), (...  96.9 us
    dot_general x32, matrix products, apply_along(): jnp.tensordot(matrix, values, axes=([1], [axis_id]), precision=exact_mode)  93.2 us
    reduce_sum x1, other arithmetic, local(): new_fields.reshape(CH, width_x, REFINE, row_count, REFINE, TILE_Z, REFINE)  80.5 us
    all_to_all x1, waiting for transfers between devices, local(): lax.all_to_all(jnp.stack([real_xz, imag_xz]), ('nx', 'ny'), split_axis=1,...  48.3 us
  transfers between devices with their start and end apart: 5, of which 5 were waited for; matrix products, arithmetic and copies ran while one was open for 0% of the time, Pallas kernels for 0%

commit v1 on v0

--- a/solution.py
+++ b/solution.py
@@ -2,7 +2,10 @@
 
 import jax
 import jax.numpy as jnp
+import numpy as np
 from jax import lax
+from jax.experimental import pallas as pl
+from jax.experimental.pallas import tpu as pltpu
 from jax.sharding import PartitionSpec as P
 
 TILE_Z = 32
@@ -210,11 +213,712 @@
     return (updated, pressure[None])
 
 
+BF = jnp.bfloat16
+F32 = jnp.float32
+GROUP = ("nx", "ny")
+
+
+def split_np(table):
+    hi = jnp.asarray(table, F32).astype(BF)
+    return hi
+
+
+def halves(value):
+    hi = value.astype(BF)
+    return hi, (value - hi.astype(F32)).astype(BF)
+
+
+def halves_np(table):
+    table = np.asarray(table, np.float32)
+    hi = table.astype(BF)
+    return hi, (table - hi.astype(np.float32)).astype(BF)
+
+
+def mm(left, right):
+    return jnp.dot(left, right, preferred_element_type=F32)
+
+
+def x_slots(nfx):
+    quarter = nfx // 4
+    low = np.arange(quarter)
+    freq = np.concatenate([low, low, low + quarter, low + quarter])
+    phase = np.concatenate(
+        [np.ones(quarter), 1j * np.ones(quarter), np.ones(quarter), 1j * np.ones(quarter)]
+    ).astype(np.complex128)
+    freq[quarter] = nfx // 2
+    phase[quarter] = 1.0
+    phase[2 * quarter] = 1.0 - 1.0j
+    weight = np.where((freq == 0) | (freq == nfx // 2), 1.0, 2.0)
+    return freq, phase, weight
+
+
+def z_slots(nfz):
+    half = nfz // 2
+    low = np.arange(half)
+    freq = np.concatenate([low, low])
+    imag = np.concatenate([np.zeros(half, bool), np.ones(half, bool)])
+    freq[half] = half
+    imag[half] = False
+    weight = np.where((freq == 0) | (freq == half), 1.0, 2.0)
+    return freq, imag, weight
+
+
+def tables(nfx, nfy, nfz, rows):
+    out = {}
+    quarter = nfx // 4
+    fx, phase, wx = x_slots(nfx)
+    theta = 2 * np.pi * fx / nfx
+    tap = np.arange(TAPS)[:, None] - 2
+    gamma = (wx / nfx) * phase * np.exp(-1j * theta[None] * tap)
+    mean = sum(np.exp(1j * theta * q) for q in range(REFINE)) / REFINE
+    step = (np.exp(1j * theta * (REFINE - 1)) - np.exp(-1j * theta)) / REFINE
+    gx = np.stack([gamma, gamma * mean, gamma * step])
+    out["gx"] = np.stack([gx.real, gx.imag])
+    turns = (np.arange(nfx)[:, None] * fx[None, :]) % nfx
+    out["ex"] = np.stack([np.cos(turns * 2 * np.pi / nfx), np.sin(turns * 2 * np.pi / nfx)])
+    out["e4"] = out["ex"][:, ::REFINE]
+    fz, imag, wz = z_slots(nfz)
+    phi = 2 * np.pi * fz / nfz
+    psi = np.where(imag, -1j, 1.0)
+    gz = psi * np.exp(-1j * phi[None] * tap)
+    gz = np.stack([gz, gz * (np.exp(1j * phi) - 1.0)])
+    out["gz"] = np.stack([gz.real, gz.imag])
+    coarse_z = nfz // REFINE
+    turns = (REFINE * np.arange(coarse_z)[:, None] * fz[None, :]) % nfz
+    zz = np.stack([np.cos(turns * 2 * np.pi / nfz), np.sin(turns * 2 * np.pi / nfz)])
+    out["zz"] = np.tile(zz, (1, rows, 1))
+    turns = (fz[:, None] * np.arange(nfz)[None, :]) % nfz
+    angle = turns * 2 * np.pi / nfz
+    iz = (wz / nfz)[:, None] * np.where(imag[:, None], -np.sin(angle), np.cos(angle))
+    hi, lo = halves_np(iz)
+    out["iz"] = np.concatenate(
+        [np.concatenate([hi, lo], 1), np.concatenate([hi, np.zeros_like(lo)], 1)], 0
+    )
+    rz = iz.reshape(nfz, coarse_z, REFINE).mean(2)
+    dz = (iz[:, REFINE - 1 :: REFINE] - np.roll(iz, 1, 1)[:, ::REFINE]) / REFINE
+    eye = np.eye(rows)
+    for name, mat in (("rz", rz), ("dz", dz)):
+        big = np.einsum("ij,kz->ikjz", eye, mat).reshape(rows * nfz, rows * coarse_z)
+        hi, lo = halves_np(big)
+        out[name] = np.stack([hi, lo])
+    coarse = np.arange(quarter)
+    turns = (coarse[:, None] * coarse[None, :]) % quarter
+    angle = turns * 2 * np.pi / quarter
+    fwd = np.concatenate([np.cos(angle), -np.sin(angle)], 0)
+    fwd[quarter] = 1.0
+    hi, lo = halves_np(fwd)
+    out["fx"] = np.concatenate([hi, hi, lo], 1)
+    mu = 4 * np.sin(np.pi * fx / nfx)[:, None] ** 2 + 4 * np.sin(np.pi * fz / nfz)[None, :] ** 2
+    root = 1 + mu / 2 - np.sqrt(mu + mu * mu / 4)
+    root = np.where(mu == 0, 0.0, root)
+    kappa = -root / (1 - root**2)
+    per = 1 / (1 - root**nfy)
+    dx = np.exp(1j * theta) - 1
+    own = dx.real.copy()
+    other = np.concatenate(
+        [-dx.imag[:quarter], dx.imag[:quarter], -dx.imag[2 * quarter : 3 * quarter],
+         dx.imag[2 * quarter : 3 * quarter]]
+    )
+    own[0], own[quarter], own[2 * quarter], own[3 * quarter] = 0.0, -2.0, -1.0, 0.0
+    other[[0, quarter, 2 * quarter, 3 * quarter]] = 0.0
+    wide = np.ones((1, nfz))
+    out["planes"] = np.stack([root, kappa, per, own[:, None] * wide, other[:, None] * wide])
+    for key in ("gx", "ex", "e4", "gz", "zz", "planes"):
+        out[key] = out[key].astype(np.float32)
+    return out
+
+
+def pick_indices(ids_ref, lists_ref, owner_ref, local_tiles, farm_count, pairs):
+    me = ids_ref[0]
+    found = []
+    for shift in range(farm_count):
+        target = me ^ shift
+        tile = jnp.int32(0)
+        for nest in range(farm_count):
+            for pair in range(pairs):
+                entry = lists_ref[nest, pair]
+                hit = (owner_ref[nest] == target) & (entry // local_tiles == me)
+                tile = jnp.where(hit, entry, tile)
+        found.append(tile - me * local_tiles)
+    return found
+
+
+def home_shifts(ids_ref, lists_ref, owner_ref, local_tiles, farm_count, pairs):
+    me = ids_ref[0]
+    shifts = []
+    for pair in range(pairs):
+        tile = jnp.int32(0)
+        for nest in range(farm_count):
+            tile = jnp.where(owner_ref[nest] == me, lists_ref[nest, pair], tile)
+        shifts.append((tile // local_tiles) ^ me)
+    return shifts
+
+
+def swap_blocks(value, rows, width):
+    lane = lax.broadcasted_iota(jnp.int32, value.shape, 1) // width
+    sub = lax.broadcasted_iota(jnp.int32, value.shape, 0) % rows
+    delta = lane - sub
+    result = value
+    lanes = value.shape[1]
+    height = value.shape[0]
+    for shift in range(1, rows):
+        for sign in (1, -1):
+            amount = sign * shift
+            moved = pltpu.roll(value, (amount * width) % lanes, 1)
+            moved = pltpu.roll(moved, (-amount) % height, 0)
+            result = jnp.where(delta == amount, moved, result)
+    return result
+
+
+def pick_kernel(local_tiles, farm_count, pairs, ids, lists, owner, tiles, *refs):
+    outs, stage, sems = refs[:farm_count], refs[farm_count], refs[farm_count + 1]
+    found = pick_indices(ids, lists, owner, local_tiles, farm_count, pairs)
+    copies = []
+    for shift in range(farm_count):
+        copies.append(
+            pltpu.make_async_copy(tiles.at[found[shift]], stage.at[shift], sems.at[shift])
+        )
+        copies[-1].start()
+    for shift in range(farm_count):
+        copies[shift].wait()
+        outs[shift][...] = stage[shift]
+
+
+def arrange_kernel(local_tiles, farm_count, pairs, ids, lists, owner, *refs):
+    tiles, out, stage = refs[:farm_count], refs[farm_count], refs[farm_count + 1]
+    for shift in range(farm_count):
+        stage[shift] = tiles[shift][...]
+    rows = stage.shape[1]
+    channels, width_x, lanes = out.shape
+    edge = width_x // pairs
+    per = lanes // rows
+    row_lanes = edge * per
+    shifts = home_shifts(ids, lists, owner, local_tiles, farm_count, pairs)
+    for pair in range(pairs):
+        tile = stage[shifts[pair]]
+        for channel in range(channels):
+            for part in range(edge * per // (2 * lanes)):
+                base = channel * row_lanes + 2 * part * lanes
+                block = jnp.concatenate(
+                    [tile[:, base : base + lanes], tile[:, base + lanes : base + 2 * lanes]], 0
+                )
+                at = pair * edge + 2 * part * rows
+                out[channel, at : at + 2 * rows, :] = swap_blocks(block, rows, per)
+
+
+def prep_kernel(taps, gx, gz, ex, e4, zz, tiles, mats, rmats, wu, ww, base, stage, sems):
+    into = pltpu.make_async_copy(tiles, stage, sems.at[0])
+    into.start()
+    nfx = mats.shape[1]
+    lanes = zz.shape[2]
+    rows = wu.shape[1] // lanes
+    per = lanes // rows
+
+    def weighted(table, part, which, axis):
+        total = taps[axis, 0] * table[part, which, 0:1, :]
+        for tap in range(1, TAPS):
+            total = total + taps[axis, tap] * table[part, which, tap : tap + 1, :]
+        return total
+
+    full = weighted(gx, 0, 0, 0) * ex[0] - weighted(gx, 1, 0, 0) * ex[1]
+    hi, lo = halves(full)
+    mats[0:nfx, :] = hi
+    mats[nfx : 2 * nfx, :] = lo
+    quarter = nfx // REFINE
+    for which in (1, 2):
+        at = (which - 1) * quarter
+        coarse = weighted(gx, 0, which, 0) * e4[0] - weighted(gx, 1, which, 0) * e4[1]
+        hi, lo = halves(coarse)
+        rmats[0, at : at + quarter, :] = hi
+        rmats[1, at : at + quarter, :] = lo
+    band = lax.broadcasted_iota(jnp.int32, (lanes, lanes), 0) // per
+    for which, target in ((0, wu), (1, ww)):
+        value = weighted(gz, 0, which, 2) * zz[0] + weighted(gz, 1, which, 2) * zz[1]
+        for row in range(rows):
+            hi, lo = halves(jnp.where(band == row, value, 0.0))
+            at = row * lanes
+            target[0:lanes, at : at + lanes] = hi
+            target[lanes : 2 * lanes, at : at + lanes] = hi
+            target[2 * lanes : 3 * lanes, at : at + lanes] = lo
+    into.wait()
+    back = pltpu.make_async_copy(stage, base, sems.at[1])
+    back.start()
+    back.wait()
+
+
+def solve_kernel(local_tiles, farm_count, pairs, groups, ids, lists, owner, taps, *refs):
+    pieces = refs[:groups]
+    (fx, wu_any, ww_any, planes_any, rmats, rz, dz, spectrum) = refs[groups : groups + 8]
+    outs = refs[groups + 8 : groups + 8 + farm_count]
+    (data, wu, ww, planes, left, field, mean_p, step_p, fresh, out_stage, zero_add, sems) = refs[
+        groups + 8 + farm_count :
+    ]
+    group = ids[1]
+    copies = []
+    for shift in range(groups):
+        copies.append(
+            pltpu.make_async_copy(pieces[shift], data.at[group ^ shift], sems.at[shift])
+        )
+    weights = [
+        pltpu.make_async_copy(wu_any, wu, sems.at[groups]),
+        pltpu.make_async_copy(ww_any, ww, sems.at[groups + 1]),
+        pltpu.make_async_copy(planes_any, planes, sems.at[groups + 2]),
+    ]
+    for copy in copies + weights:
+        copy.start()
+    for copy in copies:
+        copy.wait()
+    channels, width_x, lanes = data.shape[1:]
+    rows = wu.shape[1] // lanes
+    per = lanes // rows
+    coarse_y = groups * rows
+    fine_y = coarse_y * REFINE
+    own_fine = rows * REFINE
+    coarse_rows = fx.shape[0]
+
+    for block in range(groups):
+        hi_lo = [halves(data[block, channel]) for channel in range(3)]
+        hi = jnp.concatenate([pair[0] for pair in hi_lo], 1)
+        lo = jnp.concatenate([pair[1] for pair in hi_lo], 1)
+        turned = mm(fx[...], jnp.concatenate([hi, lo, hi], 0))
+        for channel in range(3):
+            hi, lo = halves(turned[:, channel * lanes : (channel + 1) * lanes])
+            at = block * coarse_rows
+            left[channel, at : at + coarse_rows, :] = jnp.concatenate([hi, lo, hi], 1)
+    for copy in weights:
+        copy.wait()
+    chunk = min(groups, 4)
+    for channel in range(3):
+        weight = ww if channel == 2 else wu
+        for block in range(0, groups, chunk):
+            at = block * coarse_rows
+            value = mm(left[channel, at : at + chunk * coarse_rows, :], weight[...])
+            for inner in range(chunk):
+                for row in range(rows):
+                    field[channel, (block + inner) * rows + row] = value[
+                        inner * coarse_rows : (inner + 1) * coarse_rows,
+                        row * lanes : (row + 1) * lanes,
+                    ]
+
+    sums = jnp.concatenate(
+        [jnp.sum(data[block, 1], axis=0, keepdims=True) for block in range(groups)], 0
+    )
+    total_z = taps[2, 0]
+    for tap in range(1, TAPS):
+        total_z = total_z + taps[2, tap]
+    sums = sums * total_z
+    shape = (groups, lanes)
+    coarse_id = rows * lax.broadcasted_iota(jnp.int32, shape, 0)
+    coarse_id = coarse_id + lax.broadcasted_iota(jnp.int32, shape, 1) // per
+    corner = (lax.broadcasted_iota(jnp.int32, (8, lanes), 0) == 0) & (
+        lax.broadcasted_iota(jnp.int32, (8, lanes), 1) == 0
+    )
+    for index in range(own_fine + 1):
+        at = own_fine * group - 1 + index
+        weight = jnp.zeros(shape, F32)
+        for tap in range(TAPS):
+            gap = (at - REFINE * coarse_id + 2 - tap) & (fine_y - 1)
+            saw = 0.5 - (2 * gap + 1).astype(F32) * (0.5 / fine_y)
+            weight = weight + taps[1, tap] * saw
+        value = jnp.sum(jnp.sum(weight * sums, axis=1, keepdims=True), axis=0, keepdims=True)
+        zero_add[index] = jnp.where(corner, value, 0.0)
+
+    first = rows * group
+
+    def at_row(offset):
+        return (first + offset) & (coarse_y - 1)
+
+    def tap_y(offset):
+        return taps[1, offset + 2]
+
+    half_rows = coarse_rows // 2
+
+    def sweep(step, carry):
+        low = pl.multiple_of(8 * step, 8)
+        spots = (low, half_rows + low)
+        slots = [pl.multiple_of(part * half_rows + low, 8) for part in range(4)]
+
+        def plane(which, part):
+            return planes[which, pl.ds(slots[part], 8), :]
+
+        def coarse(channel, row, side):
+            return field[channel, row, pl.ds(spots[side], 8), :]
+
+        root = [plane(0, part) for part in range(4)]
+        quad = [value * value for value in root]
+        quad = [value * value for value in quad]
+
+        def horner(offset, sign):
+            def body(i, acc):
+                row = at_row(offset + sign * (coarse_y - 1 - i))
+                loaded = [[coarse(c, row, side) for side in range(2)] for c in range(3)]
+                return tuple(
+                    acc[c * 4 + part] * quad[part] + loaded[c][part % 2]
+                    for c in range(3)
+                    for part in range(4)
+                )
+
+            zeros = tuple(jnp.zeros((8, lanes), F32) for _ in range(12))
+            return lax.fori_loop(0, coarse_y, body, zeros, unroll=4)
+
+        below = horner(-2, -1)
+        above = horner(rows + 1, 1)
+        near = list(range(-1, rows + 1))
+        near_u = {m: [coarse(0, at_row(m), side) for side in range(2)] for m in near}
+        near_v = {m: [coarse(1, at_row(m), side) for side in range(2)] for m in near}
+        near_w = {m: [coarse(2, at_row(m), side) for side in range(2)] for m in near}
+        for part in range(4):
+            side = part % 2
+            mate = part + 1 if side == 0 else part - 1
+            r = root[part]
+            kappa, per_wrap = plane(1, part), plane(2, part)
+            own, other = plane(3, part), plane(4, part)
+            turn = {
+                m: own * near_u[m][side] + other * near_u[m][1 - side] + near_w[m][side]
+                for m in near
+            }
+            lift = {m: near_v[m][side] for m in near}
+            poly_a2 = tap_y(-2) * r + tap_y(-1)
+            poly_a1 = poly_a2
+            for e in range(0, 4):
+                poly_a1 = poly_a1 * r + tap_y(e)
+            poly_a = (poly_a1 * r + tap_y(4)) * r + tap_y(5)
+            poly_b2 = tap_y(5) * r + tap_y(4)
+            poly_b1 = poly_b2
+            for e in (3, 2, 1, 0):
+                poly_b1 = poly_b1 * r + tap_y(e)
+            poly_b = (poly_b1 * r + tap_y(-1)) * r + tap_y(-2)
+            far_scale = per_wrap * r * r
+            turn_l = own * below[part] + other * below[mate] + below[8 + part]
+            turn_r = own * above[part] + other * above[mate] + above[8 + part]
+            drop = r - 1.0
+            start = far_scale * poly_a * (turn_l + drop * below[4 + part])
+            start = start + poly_a1 * turn[-1] + (drop * poly_a1 + tap_y(4)) * lift[-1]
+            start = start + poly_a2 * turn[0] + (drop * poly_a2 + tap_y(0)) * lift[0]
+            end = far_scale * poly_b * (r * turn_r - drop * above[4 + part])
+            end = end + r * poly_b1 * turn[rows] - (drop * poly_b1 + tap_y(0)) * lift[rows]
+            end = end + r * poly_b2 * turn[rows - 1] - (drop * poly_b2 + tap_y(4)) * lift[rows - 1]
+            source = []
+            for j in range(own_fine):
+                m0, q = j // REFINE, j % REFINE
+                total = None
+                for m in (m0 - 1, m0, m0 + 1):
+                    e = j - REFINE * m
+                    if -2 <= e <= 5:
+                        term = tap_y(e) * turn[m]
+                        total = term if total is None else total + term
+                    if -3 <= e <= 5:
+                        scale = (tap_y(e + 1) if e < 5 else 0.0) - (tap_y(e) if e > -3 else 0.0)
+                        total = total + scale * lift[m] if total is not None else scale * lift[m]
+                source.append(total)
+            ahead = [start]
+            for j in range(own_fine):
+                ahead.append(ahead[-1] * r + source[j])
+            back = end
+            pressure = [None] * (own_fine + 1)
+            pressure[own_fine] = kappa * (ahead[own_fine] + back)
+            for j in range(own_fine - 1, -1, -1):
+                back = r * (back + source[j])
+                pressure[j] = kappa * (ahead[j] + back)
+            spot = pl.ds(slots[part], 8)
+            for j in range(own_fine):
+                spectrum[j, spot, :] = pressure[j + 1]
+            for m in range(rows):
+                at = REFINE * m
+                total = pressure[at + 1]
+                for q in range(1, REFINE):
+                    total = total + pressure[at + 1 + q]
+                mean_p[m, spot, :] = total * (1.0 / REFINE)
+                step_p[m, spot, :] = (pressure[at + REFINE] - pressure[at]) * (1.0 / REFINE)
+        return carry
+
+    lax.fori_loop(0, half_rows // 8, sweep, 0)
+    for j in range(own_fine):
+        spectrum[j, 0:8, :] = spectrum[j, 0:8, :] + zero_add[j + 1]
+    for m in range(rows):
+        at = REFINE * m
+        total = zero_add[at + 1]
+        for q in range(1, REFINE):
+            total = total + zero_add[at + 1 + q]
+        mean_p[m, 0:8, :] = mean_p[m, 0:8, :] + total * (1.0 / REFINE)
+        step = (zero_add[at + REFINE] - zero_add[at]) * (1.0 / REFINE)
+        step_p[m, 0:8, :] = step_p[m, 0:8, :] + step
+
+    def left_three(count, stacked):
+        hi, lo = halves(stacked)
+        value = mm(rmats[0, 0:count, :], hi) + mm(rmats[0, 0:count, :], lo)
+        return value + mm(rmats[1, 0:count, :], hi)
+
+    def right_three(value, table):
+        hi, lo = halves(value)
+        return mm(hi, table[0]) + mm(lo, table[0]) + mm(hi, table[1])
+
+    smooth = left_three(2 * width_x, jnp.concatenate([mean_p[m] for m in range(rows)], 1))
+    slope = left_three(width_x, jnp.concatenate([step_p[m] for m in range(rows)], 1))
+    mean_x, step_x = smooth[0:width_x], smooth[width_x : 2 * width_x]
+    through = right_three(jnp.concatenate([step_x, slope, mean_x], 0), rz)
+    part_w = right_three(mean_x, dz)
+    change = [
+        -through[0:width_x],
+        -through[width_x : 2 * width_x],
+        -part_w,
+        through[2 * width_x : 3 * width_x],
+    ]
+
+    def band(axis):
+        quarter = 1.0 / REFINE
+        return (
+            (taps[axis, 6] + taps[axis, 7]) * quarter,
+            (taps[axis, 2] + taps[axis, 3] + taps[axis, 4] + taps[axis, 5]) * quarter,
+            (taps[axis, 0] + taps[axis, 1]) * quarter,
+        )
+
+    lane = lax.broadcasted_iota(jnp.int32, (width_x, lanes), 1)
+    previous = (group + groups - 1) & (groups - 1)
+    following = (group + 1) & (groups - 1)
+    for channel in range(channels):
+        here = data[group, channel]
+        before, after = data[previous, channel], data[following, channel]
+        lag, mid, lead = band(1)
+        low = jnp.where(lane < per, pltpu.roll(before, per, 1), pltpu.roll(here, per, 1))
+        high = jnp.where(
+            lane >= lanes - per, pltpu.roll(after, lanes - per, 1), pltpu.roll(here, lanes - per, 1)
+        )
+        value = mid * here + lag * low + lead * high
+        lag, mid, lead = band(2)
+        spot = lane % per
+        low = jnp.where(spot == 0, pltpu.roll(value, lanes - per + 1, 1), pltpu.roll(value, 1, 1))
+        high = jnp.where(
+            spot == per - 1, pltpu.roll(value, per - 1, 1), pltpu.roll(value, lanes - 1, 1)
+        )
+        value = mid * value + lag * low + lead * high
+        lag, mid, lead = band(0)
+        value = (
+            mid * value
+            + lag * pltpu.roll(value, 1, 0)
+            + lead * pltpu.roll(value, width_x - 1, 0)
+        )
+        fresh[channel] = value + change[channel]
+    shifts = home_shifts(ids, lists, owner, local_tiles, farm_count, pairs)
+    edge = width_x // pairs
+    row_lanes = edge * per
+    for pair in range(pairs):
+        for channel in range(channels):
+            for part in range(row_lanes // (2 * lanes)):
+                at = pair * edge + 2 * part * rows
+                block = swap_blocks(fresh[channel, at : at + 2 * rows, :], rows, per)
+                base = channel * row_lanes + 2 * part * lanes
+                out_stage[shifts[pair], :, base : base + lanes] = block[0:rows]
+                out_stage[shifts[pair], :, base + lanes : base + 2 * lanes] = block[rows:]
+    for shift in range(farm_count):
+        outs[shift][...] = out_stage[shift]
+
+
+def inverse_kernel(iz, mats, spectrum, out):
+    count, nfx, lanes = spectrum.shape
+    for at in range(0, count, 2):
+        value = []
+        for row in (at, at + 1):
+            hi, lo = halves(spectrum[row])
+            both = mm(jnp.concatenate([hi, lo], 1), iz[...])
+            value.append(both[:, 0:lanes] + both[:, lanes : 2 * lanes])
+        hi, lo = halves(jnp.concatenate(value, 1))
+        upper = mm(mats[...], hi)
+        final = upper[0:nfx] + upper[nfx : 2 * nfx] + mm(mats[0:nfx, :], lo)
+        for row in range(2):
+            out[:, at + row, :] = final[:, row * lanes : (row + 1) * lanes]
+
+
+def patch_kernel(local_tiles, farm_count, pairs, ids, lists, owner, base, *refs):
+    tiles, out, sems = refs[:farm_count], refs[farm_count], refs[farm_count + 1]
+    found = pick_indices(ids, lists, owner, local_tiles, farm_count, pairs)
+    copies = []
+    for shift in range(farm_count):
+        copies.append(
+            pltpu.make_async_copy(tiles[shift], out.at[found[shift]], sems.at[shift])
+        )
+        copies[-1].start()
+    for copy in copies:
+        copy.wait()
+
+
+def in_vmem():
+    return pl.BlockSpec(memory_space=pltpu.VMEM)
+
+
+def in_smem():
+    return pl.BlockSpec(memory_space=pltpu.SMEM)
+
+
+def anywhere():
+    return pl.BlockSpec(memory_space=pl.ANY)
+
+
+def limit(mib):
+    return pltpu.CompilerParams(vmem_limit_bytes=mib << 20)
+
+
+def cost(flops, nbytes):
+    return pl.CostEstimate(flops=flops, bytes_accessed=nbytes, transcendentals=0)
+
+
+def flip(value, axis, bits):
+    count = lax.axis_size(axis)
+    return lax.ppermute(value, axis, [(i, i ^ bits) for i in range(count)])
+
+
+def fast_local(coarse_tiles, prolong_taps, tile_lists, nest_owner):
+    farm_count = lax.axis_size("farm")
+    groups = lax.axis_size(GROUP)
+    local_tiles, rows, row_width = coarse_tiles.shape
+    pairs = tile_lists.shape[1]
+    edge = row_width // (CH * TILE_Z)
+    width_x = pairs * edge
+    lanes = rows * TILE_Z
+    own_fine = rows * REFINE
+    table = tables(NFX, NFY, NFZ, rows)
+    const = {key: jnp.asarray(value) for key, value in table.items()}
+    ids = jnp.stack([lax.axis_index("farm"), lax.axis_index(GROUP)]).astype(jnp.int32)
+    sizes = (local_tiles, farm_count, pairs)
+    bind = lambda kernel, *extra: (lambda *refs: kernel(*sizes, *extra, *refs))
+    tile_shape = jax.ShapeDtypeStruct((rows, row_width), F32)
+    scalars = [in_smem()] * 3
+
+    picked = pl.pallas_call(
+        bind(pick_kernel),
+        name="pick",
+        out_shape=[tile_shape] * farm_count,
+        in_specs=scalars + [anywhere()],
+        out_specs=[in_vmem()] * farm_count,
+        scratch_shapes=[
+            pltpu.VMEM((farm_count, rows, row_width), F32),
+            pltpu.SemaphoreType.DMA((farm_count,)),
+        ],
+        compiler_params=limit(8),
+        cost_estimate=cost(0, 1 << 18),
+    )(ids, tile_lists, nest_owner, coarse_tiles)
+    moved = [picked[0]] + [flip(picked[s], "farm", s) for s in range(1, farm_count)]
+    piece = pl.pallas_call(
+        bind(arrange_kernel),
+        name="arrange",
+        out_shape=jax.ShapeDtypeStruct((CH, width_x, lanes), F32),
+        in_specs=scalars + [in_vmem()] * farm_count,
+        out_specs=in_vmem(),
+        scratch_shapes=[pltpu.VMEM((farm_count, rows, row_width), F32)],
+        compiler_params=limit(8),
+        cost_estimate=cost(0, 1 << 18),
+    )(ids, tile_lists, nest_owner, *moved)
+    far_bit, core_bit, near_bit = 4, 2, 1
+    held = {0: piece}
+    for bits in (near_bit, far_bit, near_bit | far_bit):
+        held[bits] = flip(piece, GROUP, bits)
+    for bits in (0, near_bit, far_bit, near_bit | far_bit):
+        held[bits | core_bit] = flip(held[bits], GROUP, core_bit)
+
+    mats, rmats, wu, ww, base = pl.pallas_call(
+        prep_kernel,
+        name="prep",
+        out_shape=[
+            jax.ShapeDtypeStruct((2 * NFX, NFX), BF),
+            jax.ShapeDtypeStruct((2, 2 * width_x, NFX), BF),
+            jax.ShapeDtypeStruct((3 * lanes, rows * NFZ), BF),
+            jax.ShapeDtypeStruct((3 * lanes, rows * NFZ), BF),
+            jax.ShapeDtypeStruct(coarse_tiles.shape, F32),
+        ],
+        in_specs=[in_smem()] + [in_vmem()] * 5 + [anywhere()],
+        out_specs=[in_vmem()] * 4 + [anywhere()],
+        scratch_shapes=[
+            pltpu.VMEM(coarse_tiles.shape, F32),
+            pltpu.SemaphoreType.DMA((2,)),
+        ],
+        compiler_params=limit(16),
+        cost_estimate=cost(0, 6 << 20),
+    )(prolong_taps, const["gx"], const["gz"], const["ex"], const["e4"], const["zz"], coarse_tiles)
+
+    coarse_rows = 2 * width_x
+    coarse_y = groups * rows
+    spectrum, *fresh = pl.pallas_call(
+        bind(solve_kernel, groups),
+        name="solve",
+        out_shape=[jax.ShapeDtypeStruct((own_fine, NFX, NFZ), F32)] + [tile_shape] * farm_count,
+        in_specs=scalars
+        + [in_smem()]
+        + [anywhere()] * groups
+        + [in_vmem()]
+        + [anywhere()] * 3
+        + [in_vmem()] * 3,
+        out_specs=[in_vmem()] * (farm_count + 1),
+        scratch_shapes=[
+            pltpu.VMEM((groups, CH, width_x, lanes), F32),
+            pltpu.VMEM((3 * lanes, rows * NFZ), BF),
+            pltpu.VMEM((3 * lanes, rows * NFZ), BF),
+            pltpu.VMEM(const["planes"].shape, F32),
+            pltpu.VMEM((3, groups * coarse_rows, 3 * lanes), BF),
+            pltpu.VMEM((3, coarse_y, coarse_rows, NFZ), F32),
+            pltpu.VMEM((rows, NFX, NFZ), F32),
+            pltpu.VMEM((rows, NFX, NFZ), F32),
+            pltpu.VMEM((CH, width_x, lanes), F32),
+            pltpu.VMEM((farm_count, rows, row_width), F32),
+            pltpu.VMEM((own_fine + 1, 8, lanes), F32),
+            pltpu.SemaphoreType.DMA((groups + 3,)),
+        ],
+        compiler_params=limit(40),
+        cost_estimate=cost(4 << 30, 8 << 20),
+    )(
+        ids, tile_lists, nest_owner, prolong_taps,
+        *[held[s] for s in range(groups)],
+        const["fx"], wu, ww, const["planes"], rmats, const["rz"], const["dz"],
+    )
+    returned = [fresh[0]] + [flip(fresh[s], "farm", s) for s in range(1, farm_count)]
+
+    half = 8
+    pressure = pl.pallas_call(
+        inverse_kernel,
+        name="inverse",
+        out_shape=jax.ShapeDtypeStruct((NFX, own_fine, NFZ), F32),
+        grid=(own_fine // half,),
+        in_specs=[
+            pl.BlockSpec((2 * NFZ, 2 * NFZ), lambda i: (0, 0)),
+            pl.BlockSpec((2 * NFX, NFX), lambda i: (0, 0)),
+            pl.BlockSpec((half, NFX, NFZ), lambda i: (i, 0, 0)),
+        ],
+        out_specs=pl.BlockSpec((NFX, half, NFZ), lambda i: (0, i, 0)),
+        compiler_params=limit(24),
+        cost_estimate=cost(4 << 30, 4 << 20),
+    )(const["iz"], mats, spectrum)
+
+    updated = pl.pallas_call(
+        bind(patch_kernel),
+        name="patch",
+        out_shape=jax.ShapeDtypeStruct(coarse_tiles.shape, F32),
+        in_specs=scalars + [anywhere()] + [in_vmem()] * farm_count,
+        out_specs=anywhere(),
+        scratch_shapes=[pltpu.SemaphoreType.DMA((farm_count,))],
+        input_output_aliases={3: 0},
+        compiler_params=limit(8),
+        cost_estimate=cost(0, 1 << 18),
+    )(ids, tile_lists, nest_owner, base, *returned)
+    return updated, pressure[None]
+
+
+def fits_fast(mesh):
+    return dict(mesh.shape) == {"farm": 4, "nx": 4, "ny": 2}
+
+
 def solution(mesh):
+    def body(coarse_tiles, prolong_taps, tile_lists, nest_owner):
+        rows, row_width = coarse_tiles.shape[1:]
+        edge = row_width // (CH * TILE_Z)
+        dense = rows * TILE_Z == NFZ and edge % (2 * rows) == 0
+        whole = tile_lists.shape[1] * edge * REFINE == NFX
+        if fits_fast(mesh) and dense and whole:
+            return fast_local(coarse_tiles, prolong_taps, tile_lists, nest_owner)
+        return local(coarse_tiles, prolong_taps, tile_lists, nest_owner)
+
     return jax.shard_map(
-        local,
+        body,
         mesh=mesh,
-        in_specs=(P("farm", ("nx", "ny"), None), P(), P(), P()),
-        out_specs=(P("farm", ("nx", "ny"), None), P("farm", None, ("nx", "ny"), None)),
+        in_specs=(P("farm", GROUP, None), P(), P(), P()),
+        out_specs=(P("farm", GROUP, None), P("farm", None, GROUP, None)),
         check_vma=False,
     )

time: 696 us -> 50.3 us (0.07)
  local copies, waits for them, and re-layouts: 320 us -> 4.82 us
  matrix products: 101 us -> 0 us
  blocking collectives: 96.9 us -> 0 us
  other arithmetic: 93.1 us -> 0.08 us
  waiting for transfers between devices: 62.7 us -> 10.3 us
  Pallas kernels: 0 us -> 19.7 us
    another operation x6 -> x0, local copies, waits for them, and re-layouts: 294 us -> none  [the longest x4 284 us: local(): jnp.stack([own_rows[0] - (pressure - jnp.roll(pressure, 1, 0)), own_rows[...]
    dot_general x36 -> x0, matrix products: 101 us -> none  [the longest x32 93.2 us: apply_along(): jnp.tensordot(matrix, values, axes=([1], [axis_id]), precision=exact_mode)]
    all_to_all x1 -> x0, blocking collectives: 96.9 us -> none  [local(): lax.all_to_all(jnp.stack([back_real, back_imag, grad_real, grad_imag]), (...]
    reduce_sum x6 -> x0, other arithmetic: 82.4 us -> none  [the longest x1 80.5 us: local(): new_fields.reshape(CH, width_x, REFINE, row_count, REFINE, TILE_Z, REFINE)]
    all_to_all x3 -> x0, waiting for transfers between devices: 60 us -> none  [the longest x1 48.3 us: local(): lax.all_to_all(jnp.stack([real_xz, imag_xz]), ('nx', 'ny'), split_axis=1,...]
    pallas_call x0 -> x6, Pallas kernels: none -> 19.7 us  [the longest x1 10.1 us: fast_local(): pl.pallas_call(bind(solve_kernel, groups), name='solve', out_shape=[jax.S...]
    all_to_all x3 -> x0, starting transfers between devices: 14.2 us -> none  [the longest x1 6.35 us: local(): lax.all_to_all(outgoing.reshape(farm_count, row_count, row_width), 'farm'...]
    ppermute x2 -> x13, starting transfers between devices: 2.98 us -> 14.2 us  [flip(): return lax.ppermute(value, axis, [(i, i ^ bits) for i in range(count)])]
  transfers between devices with their start and end apart: 5 -> 13, of which waited for: 5 -> 4; matrix products, arithmetic and copies ran while one was open for 0% -> 0% of each run, Pallas kernels for 0% -> 13%
where the time goes in v1:
time: 50.3 us; the launch traced here: 50 us
  Pallas kernels  19.7 us (39%)
  starting transfers between devices  14.2 us (28%)
  waiting for transfers between devices  10.3 us (20%)
  local copies, waits for them, and re-layouts  4.82 us (10%)
  between operations  0.84 us (2%)
    ppermute x13, starting transfers between devices, flip(): return lax.ppermute(value, axis, [(i, i ^ bits) for i in range(count)])  14.2 us
    ppermute x13, waiting for transfers between devices, flip(): return lax.ppermute(value, axis, [(i, i ^ bits) for i in range(count)])  10.3 us
    pallas_call x1, Pallas kernels, fast_local(): pl.pallas_call(bind(solve_kernel, groups), name='solve', out_shape=[jax.S...  10.1 us
    unnamed x34, local copies, waits for them, and re-layouts  4.82 us
    pallas_call x1, Pallas kernels, fast_local(): pl.pallas_call(inverse_kernel, name='inverse', out_shape=jax.ShapeDtypeSt...  4.23 us
    pallas_call x1, Pallas kernels, fast_local(): pl.pallas_call(prep_kernel, name='prep', out_shape=[jax.ShapeDtypeStruct(...  2.29 us
    pallas_call x1, Pallas kernels, fast_local(): pl.pallas_call(bind(patch_kernel), name='patch', out_shape=jax.ShapeDtype...  1.4 us
  transfers between devices with their start and end apart: 13, of which 4 were waited for; matrix products, arithmetic and copies ran while one was open for 0% of the time, Pallas kernels for 13%

profile of v1, /device:TPU:0, one launch (start us, length us, event | category | flops | bytes accessed | tf_op | source)
XLA Modules:
  0.0 50.0 jit_solution(16091645631656164348)
XLA Ops:
  0.7 0.1 pad_add_fusion.refs_0_
  0.7 1.6 %copy-done = f32[64,4,2048]{2,1,0:T(4,128)S(1)} copy-done((f32[64,4,2048]{2,1,0:T(4,128)S(1)}, f32[64,4,2048]{2,1,0:T(4,128)}, u32[]{:S(2)}) %copy-start) | copy-done | bytes 2097176
  2.3 0.7 %copy-done.6 = s32[4,4]{1,0:T(4,128)S(1)} copy-done((s32[4,4]{1,0:T(4,128)S(1)}, s32[4,4]{1,0:T(4,128)}, u32[]{:S(2)}) %copy-start.6) | copy-done | bytes 88
  3.0 0.7 %copy-done.9 = s32[4]{0:T(128)S(1)} copy-done((s32[4]{0:T(128)S(1)}, s32[4]{0:T(128)}, u32[]{:S(2)}) %copy-start.9) | copy-done | bytes 40
  3.7 1.0 %pick.1 = (f32[4,2048]{1,0:T(4,128)S(1)}, f32[4,2048]{1,0:T(4,128)S(1)}, f32[4,2048]{1,0:T(4,128)S(1)}, f32[4,2048]{1,0:T(4,128)S(1)}) custom-call(s32[2]{0:T(128)S(1)} %pad_add_fusion.refs_0_, s32[4,4]{1,0:T(4,128)S(1)} %copy-done.6, s32[4]{0:T(128)S(1)} %copy-done.9, f32[64,4,2048]{2,1,0:T(4,128)S(1)} %copy-done), custom_call_target="tpu_custom_call" | custom-call | bytes 262144 | tf_op jit(solution)/shard_map/pick/pallas_call | solution.py:787
  4.7 3.1 %collective-permute-start = (f32[4,2048]{1,0:T(4,128)S(1)}, f32[4,2048]{1,0:T(4,128)S(1)}, u32[]{:S(2)}, u32[]{:S(2)}) collective-permute-start(f32[4,2048]{1,0:T(4,128)S(1)} %get-tuple-element.18), channel_id=1, source_target_pairs={{0,8},{8,0},{16,24},{24,16},{1,9},{9,1},{17,25},{25,17},{2,10},{10... | collective-permute-start | bytes 98312 | tf_op jit(solution)/shard_map/ppermute | solution.py:767
  7.8 2.6 %collective-permute-start.1 = (f32[4,2048]{1,0:T(4,128)S(1)}, f32[4,2048]{1,0:T(4,128)S(1)}, u32[]{:S(2)}, u32[]{:S(2)}) collective-permute-start(f32[4,2048]{1,0:T(4,128)S(1)} %get-tuple-element.19), channel_id=1, source_target_pairs={{0,16},{8,24},{16,0},{24,8},{1,17},{9,25},{17,1},{25,9},{2,18},{10... | collective-permute-start | bytes 98312 | tf_op jit(solution)/shard_map/ppermute | solution.py:767
  10.4 2.8 %collective-permute-done.1.refs_5_ = f32[4,2048]{1,0:T(4,128)S(1)} collective-permute-done((f32[4,2048]{1,0:T(4,128)S(1)}, f32[4,2048]{1,0:T(4,128)S(1)}, u32[]{:S(2)}, u32[]{:S(2)}) %collective-permute-start.1) | collective-permute-done | bytes 32800 | tf_op jit(solution)/shard_map/ppermute | solution.py:767
  13.2 2.9 %collective-permute-done.2.refs_6_ = f32[4,2048]{1,0:T(4,128)S(1)} collective-permute-done((f32[4,2048]{1,0:T(4,128)S(1)}, f32[4,2048]{1,0:T(4,128)S(1)}, u32[]{:S(2)}, u32[]{:S(2)}) %collective-permute-start.2) | collective-permute-done | bytes 32800 | tf_op jit(solution)/shard_map/ppermute | solution.py:767
  16.1 0.8 %arrange.1.refs_4_ = f32[4,64,128]{2,1,0:T(8,128)S(1)} custom-call(s32[2]{0:T(128)S(1)} %pad_add_fusion.refs_0_, s32[4,4]{1,0:T(4,128)S(1)} %copy-done.6, s32[4]{0:T(128)S(1)} %copy-done.9, f32[4,2048]{1,0:T(4,128)S(1)} %get-tuple-element.17.refs_3_, f32[4,2048]{1,0:T(4,128)S(1)} %collective-permute-done.refs_4_, ...), custom_call_target="tpu_custom_call" | custom-call | bytes 262144 | tf_op jit(solution)/shard_map/arrange/pallas_call | solution.py:801
  16.9 2.5 %collective-permute-start.7 = (f32[4,64,128]{2,1,0:T(8,128)S(1)}, f32[4,64,128]{2,1,0:T(8,128)S(1)}, u32[]{:S(2)}, u32[]{:S(2)}) collective-permute-start(f32[4,64,128]{2,1,0:T(8,128)S(1)} %arrange.1.refs_4_), channel_id=1, source_target_pairs={{0,5},{1,4},{2,7},{3,6},{4,1},{5,0},{6,3},{7,2},{8,13},{9,12},{10,... | collective-permute-start | bytes 393224 | tf_op jit(solution)/shard_map/ppermute | solution.py:767
  19.4 0.5 %collective-permute-start.6 = (f32[4,64,128]{2,1,0:T(8,128)S(1)}, f32[4,64,128]{2,1,0:T(8,128)S(1)}, u32[]{:S(2)}, u32[]{:S(2)}) collective-permute-start(f32[4,64,128]{2,1,0:T(8,128)S(1)} %arrange.1.refs_4_), channel_id=1, source_target_pairs={{0,4},{1,5},{2,6},{3,7},{4,0},{5,1},{6,2},{7,3},{8,12},{9,13},{10,... | collective-permute-start | bytes 393224 | tf_op jit(solution)/shard_map/ppermute | solution.py:767
  19.9 0.5 %collective-permute-start.3 = (f32[4,64,128]{2,1,0:T(8,128)S(1)}, f32[4,64,128]{2,1,0:T(8,128)S(1)}, u32[]{:S(2)}, u32[]{:S(2)}) collective-permute-start(f32[4,64,128]{2,1,0:T(8,128)S(1)} %arrange.1.refs_4_), channel_id=1, source_target_pairs={{0,1},{1,0},{2,3},{3,2},{4,5},{5,4},{6,7},{7,6},{8,9},{9,8},{10,11... | collective-permute-start | bytes 393224 | tf_op jit(solution)/shard_map/ppermute | solution.py:767
  20.4 3.6 %collective-permute-done.7.refs_9_ = f32[4,64,128]{2,1,0:T(8,128)S(1)} collective-permute-done((f32[4,64,128]{2,1,0:T(8,128)S(1)}, f32[4,64,128]{2,1,0:T(8,128)S(1)}, u32[]{:S(2)}, u32[]{:S(2)}) %collective-permute-start.7) | collective-permute-done | bytes 131104 | tf_op jit(solution)/shard_map/ppermute | solution.py:767
  24.0 1.0 %collective-permute-done.6.refs_8_ = f32[4,64,128]{2,1,0:T(8,128)S(1)} collective-permute-done((f32[4,64,128]{2,1,0:T(8,128)S(1)}, f32[4,64,128]{2,1,0:T(8,128)S(1)}, u32[]{:S(2)}, u32[]{:S(2)}) %collective-permute-start.6) | collective-permute-done | bytes 131104 | tf_op jit(solution)/shard_map/ppermute | solution.py:767
  25.0 0.5 %collective-permute-start.5 = (f32[4,64,128]{2,1,0:T(8,128)S(1)}, f32[4,64,128]{2,1,0:T(8,128)S(1)}, u32[]{:S(2)}, u32[]{:S(2)}) collective-permute-start(f32[4,64,128]{2,1,0:T(8,128)S(1)} %collective-permute-done.3.refs_5_), channel_id=1, source_target_pairs={{0,2},{1,3},{2,0},{3,1},{4,6},{5,7},{6,4},{7,5},{8,10},{9,11},{10,... | collective-permute-start | bytes 393224 | tf_op jit(solution)/shard_map/ppermute | solution.py:767
  25.5 1.0 %copy-done.2 = f32[2,256,256]{2,1,0:T(8,128)S(1)} copy-done((f32[2,256,256]{2,1,0:T(8,128)S(1)}, f32[2,256,256]{2,1,0:T(8,128)}, u32[]{:S(2)}) %copy-start.2) | copy-done | bytes 524312
  26.5 0.8 %copy-done.5 = f32[2,3,8,256]{3,2,1,0:T(8,128)S(1)} copy-done((f32[2,3,8,256]{3,2,1,0:T(8,128)S(1)}, f32[2,3,8,256]{3,2,1,0:T(8,128)}, u32[]{:S(2)}) %copy-start.5) | copy-done | bytes 49176
  27.4 2.3 %prep.1 = (bf16[512,256]{1,0:T(8,128)(2,1)S(1)}, bf16[2,128,256]{2,1,0:T(8,128)(2,1)S(1)}, bf16[384,512]{1,0:T(8,128)(2,1)S(1)}, bf16[384,512]{1,0:T(8,128)(2,1)S(1)}, f32[64,4,2048]{2,1,0:T(4,128)}) custom-call(f32[3,8]{1,0:T(4,128)S(1)} %copy-done.11, f32[2,3,8,256]{3,2,1,0:T(8,128)S(1)} %copy-done.5, f32[2,2,8,128]{3,2,1,0:T(8,128)S(1)} %copy-done.8, ...), custom_call_target="tpu_custom_call" | custom-call | bytes 6291456 | tf_op jit(solution)/shard_map/prep/pallas_call | solution.py:818
  29.8 10.1 %solve.1 = (f32[16,256,128]{2,1,0:T(8,128)S(1)}, f32[4,2048]{1,0:T(4,128)S(1)}, f32[4,2048]{1,0:T(4,128)S(1)}, f32[4,2048]{1,0:T(4,128)S(1)}, f32[4,2048]{1,0:T(4,128)S(1)}) custom-call(s32[2]{0:T(128)S(1)} %pad_add_fusion.refs_0_, s32[4,4]{1,0:T(4,128)S(1)} %copy-done.7, s32[4]{0:T(128)S(1)} %copy-done.10, f32[3,8]{1,0:T(4,128)S(1)} %copy-done.11, ...), custom_call_target="tpu_custom_call" | custom-call | flops 4294967296 | bytes 8388608 | tf_op jit(solution)/shard_map/solve/pallas_call | solution.py:840
  40.0 0.9 %collective-permute-start.11 = (f32[4,2048]{1,0:T(4,128)S(1)}, f32[4,2048]{1,0:T(4,128)S(1)}, u32[]{:S(2)}, u32[]{:S(2)}) collective-permute-start(f32[4,2048]{1,0:T(4,128)S(1)} %get-tuple-element.26), channel_id=1, source_target_pairs={{0,16},{8,24},{16,0},{24,8},{1,17},{9,25},{17,1},{25,9},{2,18},{10... | collective-permute-start | bytes 98312 | tf_op jit(solution)/shard_map/ppermute | solution.py:767
  40.9 3.5 %collective-permute-start.12 = (f32[4,2048]{1,0:T(4,128)S(1)}, f32[4,2048]{1,0:T(4,128)S(1)}, u32[]{:S(2)}, u32[]{:S(2)}) collective-permute-start(f32[4,2048]{1,0:T(4,128)S(1)} %get-tuple-element.27), channel_id=1, source_target_pairs={{0,24},{8,16},{16,8},{24,0},{1,25},{9,17},{17,9},{25,1},{2,26},{10... | collective-permute-start | bytes 98312 | tf_op jit(solution)/shard_map/ppermute | solution.py:767
  44.3 4.2 %inverse.1 = f32[256,16,128]{2,1,0:T(8,128)} custom-call(bf16[256,256]{1,0:T(8,128)(2,1)S(1)} %copy-done.15, bf16[512,256]{1,0:T(8,128)(2,1)S(1)} %get-tuple-element.28.mats, f32[16,256,128]{2,1,0:T(8,128)S(1)} %get-tuple-element.29.spectrum), custom_call_target="tpu_custom_call" | custom-call | flops 4294967296 | bytes 4194304 | tf_op jit(solution)/shard_map/inverse/pallas_call | solution.py:875
  48.6 1.4 %patch.1 = f32[64,4,2048]{2,1,0:T(4,128)} custom-call(s32[2]{0:T(128)S(1)} %pad_add_fusion.refs_0_, s32[4,4]{1,0:T(4,128)S(1)} %copy-done.7, s32[4]{0:T(128)S(1)} %copy-done.10, f32[64,4,2048]{2,1,0:T(4,128)} %get-tuple-element.16.refs_3_, f32[4,2048]{1,0:T(4,128)S(1)} %get-tuple-element.24.refs_4_, ...), custom_call_target="tpu_custom_call", output_to_operand_aliasing={{}: (3, {})} | custom-call | bytes 262144 | tf_op jit(solution)/shard_map/patch/pallas_call | solution.py:890
  (43 shorter events, 0.2 us)
Async XLA Ops:
  0.6 24.9 %copy-start.8 = (f32[2,2,8,128]{3,2,1,0:T(8,128)S(1)}, f32[2,2,8,128]{3,2,1,0:T(8,128)}, u32[]{:S(2)}) copy-start(f32[2,2,8,128]{3,2,1,0:T(8,128)} %constant.36.clone.gz) | copy-start | bytes 49156
  0.6 24.8 %copy-start.11 = (f32[3,8]{1,0:T(4,128)S(1)}, f32[3,8]{1,0:T(4,128)}, u32[]{:S(2)}) copy-start(f32[3,8]{1,0:T(4,128)} %refs_3_.3) | copy-start | bytes 292
  3.7 21.8 %copy-start.1 = (f32[64,4,2048]{2,1,0:T(4,128)S(1)}, f32[64,4,2048]{2,1,0:T(4,128)}, u32[]{:S(2)}) copy-start(f32[64,4,2048]{2,1,0:T(4,128)} %refs_3_.2) | copy-start | bytes 6291460
  3.7 21.8 %copy-start.3 = (f32[2,128,128]{2,1,0:T(8,128)S(1)}, f32[2,128,128]{2,1,0:T(8,128)}, u32[]{:S(2)}) copy-start(f32[2,128,128]{2,1,0:T(8,128)} %constant.37.clone.zz) | copy-start | bytes 393220
  3.7 21.8 %copy-start.4 = (f32[2,64,256]{2,1,0:T(8,128)S(1)}, f32[2,64,256]{2,1,0:T(8,128)}, u32[]{:S(2)}) copy-start(f32[2,64,256]{2,1,0:T(8,128)} %constant.35.clone.e4) | copy-start | bytes 393220
  4.6 25.1 %copy-start.7 = (s32[4,4]{1,0:T(4,128)S(1)}, s32[4,4]{1,0:T(4,128)}, u32[]{:S(2)}) copy-start(s32[4,4]{1,0:T(4,128)} %refs_1_.7) | copy-start | bytes 196
  4.7 25.1 %copy-start.10 = (s32[4]{0:T(128)S(1)}, s32[4]{0:T(128)}, u32[]{:S(2)}) copy-start(s32[4]{0:T(128)} %refs_2_.7) | copy-start | bytes 52
  4.7 5.7 %collective-permute-start = (f32[4,2048]{1,0:T(4,128)S(1)}, f32[4,2048]{1,0:T(4,128)S(1)}, u32[]{:S(2)}, u32[]{:S(2)}) collective-permute-start(f32[4,2048]{1,0:T(4,128)S(1)} %get-tuple-element.18), channel_id=1, source_target_pairs={{0,8},{8,0},{16,24},{24,16},{1,9},{9,1},{17,25},{25,17},{2,10},{10... | collective-permute-start | bytes 98312 | tf_op jit(solution)/shard_map/ppermute | solution.py:767
  7.8 5.4 %collective-permute-start.1 = (f32[4,2048]{1,0:T(4,128)S(1)}, f32[4,2048]{1,0:T(4,128)S(1)}, u32[]{:S(2)}, u32[]{:S(2)}) collective-permute-start(f32[4,2048]{1,0:T(4,128)S(1)} %get-tuple-element.19), channel_id=1, source_target_pairs={{0,16},{8,24},{16,0},{24,8},{1,17},{9,25},{17,1},{25,9},{2,18},{10... | collective-permute-start | bytes 98312 | tf_op jit(solution)/shard_map/ppermute | solution.py:767
  10.4 5.7 %collective-permute-start.2 = (f32[4,2048]{1,0:T(4,128)S(1)}, f32[4,2048]{1,0:T(4,128)S(1)}, u32[]{:S(2)}, u32[]{:S(2)}) collective-permute-start(f32[4,2048]{1,0:T(4,128)S(1)} %get-tuple-element.20), channel_id=1, source_target_pairs={{0,24},{8,16},{16,8},{24,0},{1,25},{9,17},{17,9},{25,1},{2,26},{10... | collective-permute-start | bytes 98312 | tf_op jit(solution)/shard_map/ppermute | solution.py:767
  16.9 7.1 %collective-permute-start.7 = (f32[4,64,128]{2,1,0:T(8,128)S(1)}, f32[4,64,128]{2,1,0:T(8,128)S(1)}, u32[]{:S(2)}, u32[]{:S(2)}) collective-permute-start(f32[4,64,128]{2,1,0:T(8,128)S(1)} %arrange.1.refs_4_), channel_id=1, source_target_pairs={{0,5},{1,4},{2,7},{3,6},{4,1},{5,0},{6,3},{7,2},{8,13},{9,12},{10,... | collective-permute-start | bytes 393224 | tf_op jit(solution)/shard_map/ppermute | solution.py:767
  19.4 5.6 %collective-permute-start.6 = (f32[4,64,128]{2,1,0:T(8,128)S(1)}, f32[4,64,128]{2,1,0:T(8,128)S(1)}, u32[]{:S(2)}, u32[]{:S(2)}) collective-permute-start(f32[4,64,128]{2,1,0:T(8,128)S(1)} %arrange.1.refs_4_), channel_id=1, source_target_pairs={{0,4},{1,5},{2,6},{3,7},{4,0},{5,1},{6,2},{7,3},{8,12},{9,13},{10,... | collective-permute-start | bytes 393224 | tf_op jit(solution)/shard_map/ppermute | solution.py:767
  19.9 5.1 %collective-permute-start.3 = (f32[4,64,128]{2,1,0:T(8,128)S(1)}, f32[4,64,128]{2,1,0:T(8,128)S(1)}, u32[]{:S(2)}, u32[]{:S(2)}) collective-permute-start(f32[4,64,128]{2,1,0:T(8,128)S(1)} %arrange.1.refs_4_), channel_id=1, source_target_pairs={{0,1},{1,0},{2,3},{3,2},{4,5},{5,4},{6,7},{7,6},{8,9},{9,8},{10,11... | collective-permute-start | bytes 393224 | tf_op jit(solution)/shard_map/ppermute | solution.py:767
  20.4 9.2 %collective-permute-start.4 = (f32[4,64,128]{2,1,0:T(8,128)S(1)}, f32[4,64,128]{2,1,0:T(8,128)S(1)}, u32[]{:S(2)}, u32[]{:S(2)}) collective-permute-start(f32[4,64,128]{2,1,0:T(8,128)S(1)} %arrange.1.refs_4_), channel_id=1, source_target_pairs={{0,2},{1,3},{2,0},{3,1},{4,6},{5,7},{6,4},{7,5},{8,10},{9,11},{10,... | collective-permute-start | bytes 393224 | tf_op jit(solution)/shard_map/ppermute | solution.py:767
  24.0 5.7 %collective-permute-start.9 = (f32[4,64,128]{2,1,0:T(8,128)S(1)}, f32[4,64,128]{2,1,0:T(8,128)S(1)}, u32[]{:S(2)}, u32[]{:S(2)}) collective-permute-start(f32[4,64,128]{2,1,0:T(8,128)S(1)} %collective-permute-done.7.refs_9_), channel_id=1, source_target_pairs={{0,2},{1,3},{2,0},{3,1},{4,6},{5,7},{6,4},{7,5},{8,10},{9,11},{10,... | collective-permute-start | bytes 393224 | tf_op jit(solution)/shard_map/ppermute | solution.py:767
  25.0 4.7 %collective-permute-start.8 = (f32[4,64,128]{2,1,0:T(8,128)S(1)}, f32[4,64,128]{2,1,0:T(8,128)S(1)}, u32[]{:S(2)}, u32[]{:S(2)}) collective-permute-start(f32[4,64,128]{2,1,0:T(8,128)S(1)} %collective-permute-done.6.refs_8_), channel_id=1, source_target_pairs={{0,2},{1,3},{2,0},{3,1},{4,6},{5,7},{6,4},{7,5},{8,10},{9,11},{10,... | collective-permute-start | bytes 393224 | tf_op jit(solution)/shard_map/ppermute | solution.py:767
  25.0 4.7 %collective-permute-start.5 = (f32[4,64,128]{2,1,0:T(8,128)S(1)}, f32[4,64,128]{2,1,0:T(8,128)S(1)}, u32[]{:S(2)}, u32[]{:S(2)}) collective-permute-start(f32[4,64,128]{2,1,0:T(8,128)S(1)} %collective-permute-done.3.refs_5_), channel_id=1, source_target_pairs={{0,2},{1,3},{2,0},{3,1},{4,6},{5,7},{6,4},{7,5},{8,10},{9,11},{10,... | collective-permute-start | bytes 393224 | tf_op jit(solution)/shard_map/ppermute | solution.py:767
  27.3 2.4 %copy-start.13 = (bf16[2,512,128]{2,1,0:T(8,128)(2,1)S(1)}, bf16[2,512,128]{2,1,0:T(8,128)(2,1)}, u32[]{:S(2)}) copy-start(bf16[2,512,128]{2,1,0:T(8,128)(2,1)} %constant.40.clone.refs_18_) | copy-start | bytes 786436
  27.4 2.4 %copy-start.14 = (bf16[2,512,128]{2,1,0:T(8,128)(2,1)S(1)}, bf16[2,512,128]{2,1,0:T(8,128)(2,1)}, u32[]{:S(2)}) copy-start(bf16[2,512,128]{2,1,0:T(8,128)(2,1)} %constant.39.clone.refs_17_) | copy-start | bytes 786436
  27.4 2.4 %copy-start.16 = (bf16[128,192]{1,0:T(8,128)(2,1)S(1)}, bf16[128,192]{1,0:T(8,128)(2,1)}, u32[]{:S(2)}) copy-start(bf16[128,192]{1,0:T(8,128)(2,1)} %constant.41.clone.refs_12_) | copy-start | bytes 147460
  29.8 14.6 %copy-start.15 = (bf16[256,256]{1,0:T(8,128)(2,1)S(1)}, bf16[256,256]{1,0:T(8,128)(2,1)}, u32[]{:S(2)}) copy-start(bf16[256,256]{1,0:T(8,128)(2,1)} %constant.38.clone.iz) | copy-start | bytes 393220
  39.9 8.7 %collective-permute-start.10 = (f32[4,2048]{1,0:T(4,128)S(1)}, f32[4,2048]{1,0:T(4,128)S(1)}, u32[]{:S(2)}, u32[]{:S(2)}) collective-permute-start(f32[4,2048]{1,0:T(4,128)S(1)} %get-tuple-element.25), channel_id=1, source_target_pairs={{0,8},{8,0},{16,24},{24,16},{1,9},{9,1},{17,25},{25,17},{2,10},{10... | collective-permute-start | bytes 98312 | tf_op jit(solution)/shard_map/ppermute | solution.py:767
  40.0 8.6 %collective-permute-start.11 = (f32[4,2048]{1,0:T(4,128)S(1)}, f32[4,2048]{1,0:T(4,128)S(1)}, u32[]{:S(2)}, u32[]{:S(2)}) collective-permute-start(f32[4,2048]{1,0:T(4,128)S(1)} %get-tuple-element.26), channel_id=1, source_target_pairs={{0,16},{8,24},{16,0},{24,8},{1,17},{9,25},{17,1},{25,9},{2,18},{10... | collective-permute-start | bytes 98312 | tf_op jit(solution)/shard_map/ppermute | solution.py:767
  40.9 7.7 %collective-permute-start.12 = (f32[4,2048]{1,0:T(4,128)S(1)}, f32[4,2048]{1,0:T(4,128)S(1)}, u32[]{:S(2)}, u32[]{:S(2)}) collective-permute-start(f32[4,2048]{1,0:T(4,128)S(1)} %get-tuple-element.27), channel_id=1, source_target_pairs={{0,24},{8,16},{16,8},{24,0},{1,25},{9,17},{17,9},{25,1},{2,26},{10... | collective-permute-start | bytes 98312 | tf_op jit(solution)/shard_map/ppermute | solution.py:767
  (6 other events, 7.1 us)

commit v2 on v1

--- a/solution.py
+++ b/solution.py
@@ -323,35 +323,31 @@
     other[[0, quarter, 2 * quarter, 3 * quarter]] = 0.0
     wide = np.ones((1, nfz))
     out["planes"] = np.stack([root, kappa, per, own[:, None] * wide, other[:, None] * wide])
-    for key in ("gx", "ex", "e4", "gz", "zz", "planes"):
-        out[key] = out[key].astype(np.float32)
+    out["planes"] = out["planes"].astype(np.float32)
+    flat = [out.pop("gx").reshape(-1, nfx), out.pop("ex").reshape(-1, nfx)]
+    flat += [out.pop("e4").reshape(-1, nfx)]
+    flat += [np.concatenate([part[0], part[1]], -1).reshape(-1, nfx) for part in (out.pop("gz"), out.pop("zz"))]
+    out["bank"] = np.concatenate(flat, 0).astype(np.float32)
     return out
 
 
-def pick_indices(ids_ref, lists_ref, owner_ref, local_tiles, farm_count, pairs):
-    me = ids_ref[0]
-    found = []
+def find_tiles(me, lists, owner, local_tiles, farm_count, pairs):
+    found, shifts = [], []
     for shift in range(farm_count):
         target = me ^ shift
         tile = jnp.int32(0)
         for nest in range(farm_count):
             for pair in range(pairs):
-                entry = lists_ref[nest, pair]
-                hit = (owner_ref[nest] == target) & (entry // local_tiles == me)
+                entry = lists[nest, pair]
+                hit = (owner[nest] == target) & (entry // local_tiles == me)
                 tile = jnp.where(hit, entry, tile)
         found.append(tile - me * local_tiles)
-    return found
-
-
-def home_shifts(ids_ref, lists_ref, owner_ref, local_tiles, farm_count, pairs):
-    me = ids_ref[0]
-    shifts = []
     for pair in range(pairs):
         tile = jnp.int32(0)
         for nest in range(farm_count):
-            tile = jnp.where(owner_ref[nest] == me, lists_ref[nest, pair], tile)
+            tile = jnp.where(owner[nest] == me, lists[nest, pair], tile)
         shifts.append((tile // local_tiles) ^ me)
-    return shifts
+    return found, shifts
 
 
 def swap_blocks(value, rows, width):
@@ -370,32 +366,45 @@
     return result
 
 
-def pick_kernel(local_tiles, farm_count, pairs, ids, lists, owner, tiles, *refs):
-    outs, stage, sems = refs[:farm_count], refs[farm_count], refs[farm_count + 1]
-    found = pick_indices(ids, lists, owner, local_tiles, farm_count, pairs)
+def pick_kernel(local_tiles, farm_count, pairs, lists_any, owner_any, tiles, *refs):
+    info, outs = refs[0], refs[1 : 1 + farm_count]
+    lists, owner, sems = refs[1 + farm_count :]
+    reads = [
+        pltpu.make_async_copy(lists_any, lists, sems.at[farm_count]),
+        pltpu.make_async_copy(owner_any, owner, sems.at[farm_count + 1]),
+    ]
+    for copy in reads:
+        copy.start()
+    for copy in reads:
+        copy.wait()
+    me = lax.axis_index("farm")
+    found, shifts = find_tiles(me, lists, owner, local_tiles, farm_count, pairs)
     copies = []
     for shift in range(farm_count):
         copies.append(
-            pltpu.make_async_copy(tiles.at[found[shift]], stage.at[shift], sems.at[shift])
+            pltpu.make_async_copy(tiles.at[found[shift]], outs[shift], sems.at[shift])
         )
         copies[-1].start()
     for shift in range(farm_count):
-        copies[shift].wait()
-        outs[shift][...] = stage[shift]
-
-
-def arrange_kernel(local_tiles, farm_count, pairs, ids, lists, owner, *refs):
+        info[shift] = found[shift]
+    for pair in range(pairs):
+        info[farm_count + pair] = shifts[pair]
+    info[farm_count + pairs] = lax.axis_index(GROUP)
+    for copy in copies:
+        copy.wait()
+
+
+def arrange_kernel(farm_count, pairs, info, gate, *refs):
     tiles, out, stage = refs[:farm_count], refs[farm_count], refs[farm_count + 1]
     for shift in range(farm_count):
-        stage[shift] = tiles[shift][...]
+        stage[shift] = tiles[farm_count - 1 - shift][...]
     rows = stage.shape[1]
     channels, width_x, lanes = out.shape
     edge = width_x // pairs
     per = lanes // rows
     row_lanes = edge * per
-    shifts = home_shifts(ids, lists, owner, local_tiles, farm_count, pairs)
     for pair in range(pairs):
-        tile = stage[shifts[pair]]
+        tile = stage[info[farm_count + pair]]
         for channel in range(channels):
             for part in range(edge * per // (2 * lanes)):
                 base = channel * row_lanes + 2 * part * lanes
@@ -406,54 +415,59 @@
                 out[channel, at : at + 2 * rows, :] = swap_blocks(block, rows, per)
 
 
-def prep_kernel(taps, gx, gz, ex, e4, zz, tiles, mats, rmats, wu, ww, base, stage, sems):
-    into = pltpu.make_async_copy(tiles, stage, sems.at[0])
-    into.start()
+def prep_kernel(taps, bank, mats, rmats, wu, ww):
     nfx = mats.shape[1]
-    lanes = zz.shape[2]
+    quarter = nfx // REFINE
+    lanes = wu.shape[0] // 3
     rows = wu.shape[1] // lanes
     per = lanes // rows
-
-    def weighted(table, part, which, axis):
-        total = taps[axis, 0] * table[part, which, 0:1, :]
+    at_ex = 6 * TAPS
+    at_e4 = at_ex + 2 * nfx
+    at_gz = at_e4 + 2 * quarter
+    at_zz = at_gz + 2 * TAPS
+
+    def weighted(at, axis):
+        total = taps[axis, 0] * bank[at : at + 1, :]
         for tap in range(1, TAPS):
-            total = total + taps[axis, tap] * table[part, which, tap : tap + 1, :]
+            total = total + taps[axis, tap] * bank[at + tap : at + tap + 1, :]
         return total
 
-    full = weighted(gx, 0, 0, 0) * ex[0] - weighted(gx, 1, 0, 0) * ex[1]
+    full = weighted(0, 0) * bank[at_ex : at_ex + nfx, :]
+    full = full - weighted(3 * TAPS, 0) * bank[at_ex + nfx : at_ex + 2 * nfx, :]
     hi, lo = halves(full)
     mats[0:nfx, :] = hi
     mats[nfx : 2 * nfx, :] = lo
-    quarter = nfx // REFINE
     for which in (1, 2):
         at = (which - 1) * quarter
-        coarse = weighted(gx, 0, which, 0) * e4[0] - weighted(gx, 1, which, 0) * e4[1]
+        coarse = weighted(which * TAPS, 0) * bank[at_e4 : at_e4 + quarter, :]
+        second = bank[at_e4 + quarter : at_e4 + 2 * quarter, :]
+        coarse = coarse - weighted((3 + which) * TAPS, 0) * second
         hi, lo = halves(coarse)
         rmats[0, at : at + quarter, :] = hi
         rmats[1, at : at + quarter, :] = lo
     band = lax.broadcasted_iota(jnp.int32, (lanes, lanes), 0) // per
     for which, target in ((0, wu), (1, ww)):
-        value = weighted(gz, 0, which, 2) * zz[0] + weighted(gz, 1, which, 2) * zz[1]
+        value = weighted(at_gz + which * TAPS, 2) * bank[at_zz : at_zz + lanes, :]
+        value = value[:, 0:lanes] + value[:, lanes : 2 * lanes]
         for row in range(rows):
             hi, lo = halves(jnp.where(band == row, value, 0.0))
             at = row * lanes
             target[0:lanes, at : at + lanes] = hi
             target[lanes : 2 * lanes, at : at + lanes] = hi
             target[2 * lanes : 3 * lanes, at : at + lanes] = lo
-    into.wait()
-    back = pltpu.make_async_copy(stage, base, sems.at[1])
-    back.start()
-    back.wait()
-
-
-def solve_kernel(local_tiles, farm_count, pairs, groups, ids, lists, owner, taps, *refs):
+
+
+def solve_kernel(farm_count, pairs, groups, info, taps, *refs):
     pieces = refs[:groups]
-    (fx, wu_any, ww_any, planes_any, rmats, rz, dz, spectrum) = refs[groups : groups + 8]
-    outs = refs[groups + 8 : groups + 8 + farm_count]
-    (data, wu, ww, planes, left, field, mean_p, step_p, fresh, out_stage, zero_add, sems) = refs[
-        groups + 8 + farm_count :
+    (fx, wu_any, ww_any, planes_any, rmats, rz, dz, tiles, spectrum) = refs[groups : groups + 9]
+    outs = refs[groups + 9 : groups + 9 + farm_count]
+    base = refs[groups + 9 + farm_count]
+    (data, wu, ww, planes, left, field, mean_p, step_p, fresh, out_stage, zero_add, shelf, sems) = refs[
+        groups + 10 + farm_count :
     ]
-    group = ids[1]
+    take = pltpu.make_async_copy(tiles, shelf, sems.at[groups + 3])
+    take.start()
+    group = info[farm_count + pairs]
     copies = []
     for shift in range(groups):
         copies.append(
@@ -523,6 +537,9 @@
         value = jnp.sum(jnp.sum(weight * sums, axis=1, keepdims=True), axis=0, keepdims=True)
         zero_add[index] = jnp.where(corner, value, 0.0)
 
+    take.wait()
+    give = pltpu.make_async_copy(shelf, base, sems.at[groups + 4])
+    give.start()
     first = rows * group
 
     def at_row(offset):
@@ -699,7 +716,7 @@
             + lead * pltpu.roll(value, width_x - 1, 0)
         )
         fresh[channel] = value + change[channel]
-    shifts = home_shifts(ids, lists, owner, local_tiles, farm_count, pairs)
+    shifts = [info[farm_count + pair] for pair in range(pairs)]
     edge = width_x // pairs
     row_lanes = edge * per
     for pair in range(pairs):
@@ -712,6 +729,7 @@
                 out_stage[shifts[pair], :, base + lanes : base + 2 * lanes] = block[rows:]
     for shift in range(farm_count):
         outs[shift][...] = out_stage[shift]
+    give.wait()
 
 
 def inverse_kernel(iz, mats, spectrum, out):
@@ -729,13 +747,14 @@
             out[:, at + row, :] = final[:, row * lanes : (row + 1) * lanes]
 
 
-def patch_kernel(local_tiles, farm_count, pairs, ids, lists, owner, base, *refs):
+def patch_kernel(farm_count, info, base, *refs):
     tiles, out, sems = refs[:farm_count], refs[farm_count], refs[farm_count + 1]
-    found = pick_indices(ids, lists, owner, local_tiles, farm_count, pairs)
     copies = []
     for shift in range(farm_count):
         copies.append(
-            pltpu.make_async_copy(tiles[shift], out.at[found[shift]], sems.at[shift])
+            pltpu.make_async_copy(
+                tiles[farm_count - 1 - shift], out.at[info[shift]], sems.at[shift]
+            )
         )
         copies[-1].start()
     for copy in copies:
@@ -752,6 +771,14 @@
 
 def anywhere():
     return pl.BlockSpec(memory_space=pl.ANY)
+
+
+def in_hbm():
+    return pl.BlockSpec(memory_space=pltpu.HBM)
+
+
+def keep_hbm(value):
+    return pltpu.with_memory_space_constraint(value, pltpu.HBM)
 
 
 def limit(mib):
@@ -778,44 +805,27 @@
     own_fine = rows * REFINE
     table = tables(NFX, NFY, NFZ, rows)
     const = {key: jnp.asarray(value) for key, value in table.items()}
-    ids = jnp.stack([lax.axis_index("farm"), lax.axis_index(GROUP)]).astype(jnp.int32)
-    sizes = (local_tiles, farm_count, pairs)
-    bind = lambda kernel, *extra: (lambda *refs: kernel(*sizes, *extra, *refs))
+    bind = lambda kernel, *sizes: (lambda *refs: kernel(*sizes, *refs))
     tile_shape = jax.ShapeDtypeStruct((rows, row_width), F32)
-    scalars = [in_smem()] * 3
-
-    picked = pl.pallas_call(
-        bind(pick_kernel),
+
+    info, *picked = pl.pallas_call(
+        bind(pick_kernel, local_tiles, farm_count, pairs),
         name="pick",
-        out_shape=[tile_shape] * farm_count,
-        in_specs=scalars + [anywhere()],
-        out_specs=[in_vmem()] * farm_count,
+        out_shape=[jax.ShapeDtypeStruct((farm_count + pairs + 1,), jnp.int32)]
+        + [tile_shape] * farm_count,
+        in_specs=[in_hbm()] * 3,
+        out_specs=[in_smem()] + [in_vmem()] * farm_count,
         scratch_shapes=[
-            pltpu.VMEM((farm_count, rows, row_width), F32),
-            pltpu.SemaphoreType.DMA((farm_count,)),
+            pltpu.SMEM(tile_lists.shape, jnp.int32),
+            pltpu.SMEM(nest_owner.shape, jnp.int32),
+            pltpu.SemaphoreType.DMA((farm_count + 2,)),
         ],
         compiler_params=limit(8),
         cost_estimate=cost(0, 1 << 18),
-    )(ids, tile_lists, nest_owner, coarse_tiles)
-    moved = [picked[0]] + [flip(picked[s], "farm", s) for s in range(1, farm_count)]
-    piece = pl.pallas_call(
-        bind(arrange_kernel),
-        name="arrange",
-        out_shape=jax.ShapeDtypeStruct((CH, width_x, lanes), F32),
-        in_specs=scalars + [in_vmem()] * farm_count,
-        out_specs=in_vmem(),
-        scratch_shapes=[pltpu.VMEM((farm_count, rows, row_width), F32)],
-        compiler_params=limit(8),
-        cost_estimate=cost(0, 1 << 18),
-    )(ids, tile_lists, nest_owner, *moved)
-    far_bit, core_bit, near_bit = 4, 2, 1
-    held = {0: piece}
-    for bits in (near_bit, far_bit, near_bit | far_bit):
-        held[bits] = flip(piece, GROUP, bits)
-    for bits in (0, near_bit, far_bit, near_bit | far_bit):
-        held[bits | core_bit] = flip(held[bits], GROUP, core_bit)
-
-    mats, rmats, wu, ww, base = pl.pallas_call(
+    )(keep_hbm(tile_lists), keep_hbm(nest_owner), keep_hbm(coarse_tiles))
+    moved = {s: flip(picked[s], "farm", s) for s in range(farm_count - 1, 0, -1)}
+    moved = [picked[0]] + [moved[s] for s in range(1, farm_count)]
+    mats, rmats, wu, ww = pl.pallas_call(
         prep_kernel,
         name="prep",
         out_shape=[
@@ -823,31 +833,45 @@
             jax.ShapeDtypeStruct((2, 2 * width_x, NFX), BF),
             jax.ShapeDtypeStruct((3 * lanes, rows * NFZ), BF),
             jax.ShapeDtypeStruct((3 * lanes, rows * NFZ), BF),
-            jax.ShapeDtypeStruct(coarse_tiles.shape, F32),
         ],
-        in_specs=[in_smem()] + [in_vmem()] * 5 + [anywhere()],
-        out_specs=[in_vmem()] * 4 + [anywhere()],
-        scratch_shapes=[
-            pltpu.VMEM(coarse_tiles.shape, F32),
-            pltpu.SemaphoreType.DMA((2,)),
-        ],
-        compiler_params=limit(16),
+        in_specs=[in_smem(), in_vmem()],
+        out_specs=[in_vmem()] * 4,
+        compiler_params=limit(8),
         cost_estimate=cost(0, 6 << 20),
-    )(prolong_taps, const["gx"], const["gz"], const["ex"], const["e4"], const["zz"], coarse_tiles)
+    )(prolong_taps, const["bank"])
+
+    piece = pl.pallas_call(
+        bind(arrange_kernel, farm_count, pairs),
+        name="arrange",
+        out_shape=jax.ShapeDtypeStruct((CH, width_x, lanes), F32),
+        in_specs=[in_smem(), anywhere()] + [in_vmem()] * farm_count,
+        out_specs=in_vmem(),
+        scratch_shapes=[pltpu.VMEM((farm_count, rows, row_width), F32)],
+        compiler_params=limit(8),
+        cost_estimate=cost(0, 1 << 18),
+    )(info, rmats, *moved[::-1])
+    far_bit, core_bit, near_bit = 4, 2, 1
+    held = {0: piece}
+    for bits in (near_bit, far_bit, near_bit | far_bit):
+        held[bits] = flip(piece, GROUP, bits)
+    for bits in (0, near_bit, far_bit, near_bit | far_bit):
+        held[bits | core_bit] = flip(held[bits], GROUP, core_bit)
 
     coarse_rows = 2 * width_x
     coarse_y = groups * rows
-    spectrum, *fresh = pl.pallas_call(
-        bind(solve_kernel, groups),
+    spectrum, *fresh, base = pl.pallas_call(
+        bind(solve_kernel, farm_count, pairs, groups),
         name="solve",
-        out_shape=[jax.ShapeDtypeStruct((own_fine, NFX, NFZ), F32)] + [tile_shape] * farm_count,
-        in_specs=scalars
-        + [in_smem()]
+        out_shape=[jax.ShapeDtypeStruct((own_fine, NFX, NFZ), F32)]
+        + [tile_shape] * farm_count
+        + [jax.ShapeDtypeStruct(coarse_tiles.shape, F32)],
+        in_specs=[in_smem()] * 2
         + [anywhere()] * groups
         + [in_vmem()]
         + [anywhere()] * 3
-        + [in_vmem()] * 3,
-        out_specs=[in_vmem()] * (farm_count + 1),
+        + [in_vmem()] * 3
+        + [in_hbm()],
+        out_specs=[in_vmem()] * (farm_count + 1) + [in_hbm()],
         scratch_shapes=[
             pltpu.VMEM((groups, CH, width_x, lanes), F32),
             pltpu.VMEM((3 * lanes, rows * NFZ), BF),
@@ -860,14 +884,16 @@
             pltpu.VMEM((CH, width_x, lanes), F32),
             pltpu.VMEM((farm_count, rows, row_width), F32),
             pltpu.VMEM((own_fine + 1, 8, lanes), F32),
-            pltpu.SemaphoreType.DMA((groups + 3,)),
+            pltpu.VMEM(coarse_tiles.shape, F32),
+            pltpu.SemaphoreType.DMA((groups + 5,)),
         ],
         compiler_params=limit(40),
         cost_estimate=cost(4 << 30, 8 << 20),
     )(
-        ids, tile_lists, nest_owner, prolong_taps,
+        info, prolong_taps,
         *[held[s] for s in range(groups)],
         const["fx"], wu, ww, const["planes"], rmats, const["rz"], const["dz"],
+        keep_hbm(coarse_tiles),
     )
     returned = [fresh[0]] + [flip(fresh[s], "farm", s) for s in range(1, farm_count)]
 
@@ -888,16 +914,16 @@
     )(const["iz"], mats, spectrum)
 
     updated = pl.pallas_call(
-        bind(patch_kernel),
+        bind(patch_kernel, farm_count),
         name="patch",
         out_shape=jax.ShapeDtypeStruct(coarse_tiles.shape, F32),
-        in_specs=scalars + [anywhere()] + [in_vmem()] * farm_count,
-        out_specs=anywhere(),
+        in_specs=[in_smem(), in_hbm()] + [in_vmem()] * farm_count,
+        out_specs=in_hbm(),
         scratch_shapes=[pltpu.SemaphoreType.DMA((farm_count,))],
-        input_output_aliases={3: 0},
+        input_output_aliases={1: 0},
         compiler_params=limit(8),
         cost_estimate=cost(0, 1 << 18),
-    )(ids, tile_lists, nest_owner, base, *returned)
+    )(info, base, *returned[::-1])
     return updated, pressure[None]
 
 

time: 50.3 us -> 43.8 us (0.87)
  local copies, waits for them, and re-layouts: 4.82 us -> 0.05 us
  waiting for transfers between devices: 10.3 us -> 8.94 us
    unnamed x34 -> x14, local copies, waits for them, and re-layouts: 4.82 us -> 0.05 us
    pallas_call x1, Pallas kernels: 2.29 us -> 0.8 us  [fast_local(): pl.pallas_call(prep_kernel, name='prep', out_shape=[jax.ShapeDtypeStruct(...]
    pallas_call x4, Pallas kernels: 13.2 us -> 14.6 us  [the longest x1 10.2 us: fast_local(): pl.pallas_call(bind(solve_kernel, farm_count, pairs, groups), name='solve...]
    ppermute x13, waiting for transfers between devices: 10.3 us -> 8.94 us  [flip(): return lax.ppermute(value, axis, [(i, i ^ bits) for i in range(count)])]
  transfers between devices with their start and end apart: 13 -> 13, of which waited for: 4 -> 6; matrix products, arithmetic and copies ran while one was open for 0% -> 0% of each run, Pallas kernels for 13% -> 12%
where the time goes in v2:
time: 43.8 us; the launch traced here: 43.7 us
  Pallas kernels  19.6 us (45%)
  starting transfers between devices  14.3 us (33%)
  waiting for transfers between devices  8.94 us (20%)
  between operations  0.75 us (2%)
    ppermute x13, starting transfers between devices, flip(): return lax.ppermute(value, axis, [(i, i ^ bits) for i in range(count)])  14.3 us
    pallas_call x1, Pallas kernels, fast_local(): pl.pallas_call(bind(solve_kernel, farm_count, pairs, groups), name='solve...  10.2 us
    ppermute x13, waiting for transfers between devices, flip(): return lax.ppermute(value, axis, [(i, i ^ bits) for i in range(count)])  8.94 us
    pallas_call x1, Pallas kernels, fast_local(): pl.pallas_call(inverse_kernel, name='inverse', out_shape=jax.ShapeDtypeSt...  4.25 us
    pallas_call x1, Pallas kernels, fast_local(): pl.pallas_call(bind(pick_kernel, local_tiles, farm_count, pairs), name='p...  2.46 us
    pallas_call x1, Pallas kernels, fast_local(): pl.pallas_call(bind(patch_kernel, farm_count), name='patch', out_shape=ja...  1.23 us
  transfers between devices with their start and end apart: 13, of which 6 were waited for; matrix products, arithmetic and copies ran while one was open for 0% of the time, Pallas kernels for 12%

profile of v2, /device:TPU:0, one launch (start us, length us, event | category | flops | bytes accessed | tf_op | source)
XLA Modules:
  0.0 43.7 jit_solution(8787719075489369668)
XLA Ops:
  0.6 0.0 copy-start
  0.6 0.0 copy-start.2
  0.7 2.5 %pick.1 = (s32[9]{0:T(128)S(1)}, f32[4,2048]{1,0:T(4,128)S(1)}, f32[4,2048]{1,0:T(4,128)S(1)}, f32[4,2048]{1,0:T(4,128)S(1)}, f32[4,2048]{1,0:T(4,128)S(1)}) custom-call(s32[4,4]{1,0:T(4,128)} %refs_0_.1, s32[4]{0:T(128)} %refs_1_.2, f32[64,4,2048]{2,1,0:T(4,128)} %refs_17_.1), custom_call_target="tpu_custom_call" | custom-call | bytes 262144 | tf_op jit(solution)/shard_map/pick/pallas_call | solution.py:811
  3.2 5.1 %collective-permute-start = (f32[4,2048]{1,0:T(4,128)S(1)}, f32[4,2048]{1,0:T(4,128)S(1)}, u32[]{:S(2)}, u32[]{:S(2)}) collective-permute-start(f32[4,2048]{1,0:T(4,128)S(1)} %get-tuple-element.19), channel_id=1, source_target_pairs={{0,24},{8,16},{16,8},{24,0},{1,25},{9,17},{17,9},{25,1},{2,26},{10... | collective-permute-start | bytes 98312 | tf_op jit(solution)/shard_map/ppermute | solution.py:794
  8.3 0.6 %collective-permute-start.2 = (f32[4,2048]{1,0:T(4,128)S(1)}, f32[4,2048]{1,0:T(4,128)S(1)}, u32[]{:S(2)}, u32[]{:S(2)}) collective-permute-start(f32[4,2048]{1,0:T(4,128)S(1)} %get-tuple-element.21), channel_id=1, source_target_pairs={{0,8},{8,0},{16,24},{24,16},{1,9},{9,1},{17,25},{25,17},{2,10},{10... | collective-permute-start | bytes 98312 | tf_op jit(solution)/shard_map/ppermute | solution.py:794
  9.0 0.8 %prep.1 = (bf16[512,256]{1,0:T(8,128)(2,1)S(1)}, bf16[2,128,256]{2,1,0:T(8,128)(2,1)S(1)}, bf16[384,512]{1,0:T(8,128)(2,1)S(1)}, bf16[384,512]{1,0:T(8,128)(2,1)S(1)}) custom-call(f32[3,8]{1,0:T(4,128)S(1)} %copy-done.1, f32[832,256]{1,0:T(8,128)S(1)} %copy-done), custom_call_target="tpu_custom_call" | custom-call | bytes 6291456 | tf_op jit(solution)/shard_map/prep/pallas_call | solution.py:828
  9.8 0.4 %collective-permute-done.refs_2_ = f32[4,2048]{1,0:T(4,128)S(1)} collective-permute-done((f32[4,2048]{1,0:T(4,128)S(1)}, f32[4,2048]{1,0:T(4,128)S(1)}, u32[]{:S(2)}, u32[]{:S(2)}) %collective-permute-start) | collective-permute-done | bytes 32800 | tf_op jit(solution)/shard_map/ppermute | solution.py:794
  10.2 2.9 %collective-permute-done.1.refs_3_ = f32[4,2048]{1,0:T(4,128)S(1)} collective-permute-done((f32[4,2048]{1,0:T(4,128)S(1)}, f32[4,2048]{1,0:T(4,128)S(1)}, u32[]{:S(2)}, u32[]{:S(2)}) %collective-permute-start.1) | collective-permute-done | bytes 32800 | tf_op jit(solution)/shard_map/ppermute | solution.py:794
  13.1 0.7 %arrange.1.refs_2_ = f32[4,64,128]{2,1,0:T(8,128)S(1)} custom-call(s32[9]{0:T(128)S(1)} %get-tuple-element.17.refs_0_, bf16[2,128,256]{2,1,0:T(8,128)(2,1)S(1)} %get-tuple-element.18.refs_1_.refs_14_, f32[4,2048]{1,0:T(4,128)S(1)} %collective-permute-done.refs_2_, f32[4,2048]{1,0:T(4,128)S(1)} %collective-permute-done.1.refs_3_, ...), custom_call_target="tpu_custom_call" | custom-call | bytes 262144 | tf_op jit(solution)/shard_map/arrange/pallas_call | solution.py:843
  13.9 2.5 %collective-permute-start.7 = (f32[4,64,128]{2,1,0:T(8,128)S(1)}, f32[4,64,128]{2,1,0:T(8,128)S(1)}, u32[]{:S(2)}, u32[]{:S(2)}) collective-permute-start(f32[4,64,128]{2,1,0:T(8,128)S(1)} %arrange.1.refs_2_), channel_id=1, source_target_pairs={{0,5},{1,4},{2,7},{3,6},{4,1},{5,0},{6,3},{7,2},{8,13},{9,12},{10,... | collective-permute-start | bytes 393224 | tf_op jit(solution)/shard_map/ppermute | solution.py:794
  16.4 0.5 %collective-permute-start.6 = (f32[4,64,128]{2,1,0:T(8,128)S(1)}, f32[4,64,128]{2,1,0:T(8,128)S(1)}, u32[]{:S(2)}, u32[]{:S(2)}) collective-permute-start(f32[4,64,128]{2,1,0:T(8,128)S(1)} %arrange.1.refs_2_), channel_id=1, source_target_pairs={{0,4},{1,5},{2,6},{3,7},{4,0},{5,1},{6,2},{7,3},{8,12},{9,13},{10,... | collective-permute-start | bytes 393224 | tf_op jit(solution)/shard_map/ppermute | solution.py:794
  16.9 0.5 %collective-permute-start.3 = (f32[4,64,128]{2,1,0:T(8,128)S(1)}, f32[4,64,128]{2,1,0:T(8,128)S(1)}, u32[]{:S(2)}, u32[]{:S(2)}) collective-permute-start(f32[4,64,128]{2,1,0:T(8,128)S(1)} %arrange.1.refs_2_), channel_id=1, source_target_pairs={{0,1},{1,0},{2,3},{3,2},{4,5},{5,4},{6,7},{7,6},{8,9},{9,8},{10,11... | collective-permute-start | bytes 393224 | tf_op jit(solution)/shard_map/ppermute | solution.py:794
  17.4 3.8 %collective-permute-done.7.refs_7_ = f32[4,64,128]{2,1,0:T(8,128)S(1)} collective-permute-done((f32[4,64,128]{2,1,0:T(8,128)S(1)}, f32[4,64,128]{2,1,0:T(8,128)S(1)}, u32[]{:S(2)}, u32[]{:S(2)}) %collective-permute-start.7) | collective-permute-done | bytes 131104 | tf_op jit(solution)/shard_map/ppermute | solution.py:794
  21.2 0.8 %collective-permute-done.6.refs_6_ = f32[4,64,128]{2,1,0:T(8,128)S(1)} collective-permute-done((f32[4,64,128]{2,1,0:T(8,128)S(1)}, f32[4,64,128]{2,1,0:T(8,128)S(1)}, u32[]{:S(2)}, u32[]{:S(2)}) %collective-permute-start.6) | collective-permute-done | bytes 131104 | tf_op jit(solution)/shard_map/ppermute | solution.py:794
  22.0 0.5 %collective-permute-start.5 = (f32[4,64,128]{2,1,0:T(8,128)S(1)}, f32[4,64,128]{2,1,0:T(8,128)S(1)}, u32[]{:S(2)}, u32[]{:S(2)}) collective-permute-start(f32[4,64,128]{2,1,0:T(8,128)S(1)} %collective-permute-done.3.refs_3_), channel_id=1, source_target_pairs={{0,2},{1,3},{2,0},{3,1},{4,6},{5,7},{6,4},{7,5},{8,10},{9,11},{10,... | collective-permute-start | bytes 393224 | tf_op jit(solution)/shard_map/ppermute | solution.py:794
  22.5 0.0 collective-permute-done.9.refs_9_
  22.5 0.8 %collective-permute-done.8.refs_8_ = f32[4,64,128]{2,1,0:T(8,128)S(1)} collective-permute-done((f32[4,64,128]{2,1,0:T(8,128)S(1)}, f32[4,64,128]{2,1,0:T(8,128)S(1)}, u32[]{:S(2)}, u32[]{:S(2)}) %collective-permute-start.8) | collective-permute-done | bytes 131104 | tf_op jit(solution)/shard_map/ppermute | solution.py:794
  23.3 0.2 collective-permute-done.5.refs_5_
  23.5 10.2 %solve.1 = (f32[16,256,128]{2,1,0:T(8,128)S(1)}, f32[4,2048]{1,0:T(4,128)S(1)}, f32[4,2048]{1,0:T(4,128)S(1)}, f32[4,2048]{1,0:T(4,128)S(1)}, f32[4,2048]{1,0:T(4,128)S(1)}, /*index=5*/f32[64,4,2048]{2,1,0:T(4,128)}) custom-call(s32[9]{0:T(128)S(1)} %get-tuple-element.17.refs_0_, f32[3,8]{1,0:T(4,128)S(1)} %copy-done.1, f32[4,64,128]{2,1,0:T(8,128)S(1)} %arrange.1.refs_2_, ...), custom_call_target="tpu_custom_call" | custom-call | flops 4294967296 | bytes 8388608 | tf_op jit(solution)/shard_map/solve/pallas_call | solution.py:862
  33.7 1.4 %collective-permute-start.10 = (f32[4,2048]{1,0:T(4,128)S(1)}, f32[4,2048]{1,0:T(4,128)S(1)}, u32[]{:S(2)}, u32[]{:S(2)}) collective-permute-start(f32[4,2048]{1,0:T(4,128)S(1)} %get-tuple-element.26), channel_id=1, source_target_pairs={{0,24},{8,16},{16,8},{24,0},{1,25},{9,17},{17,9},{25,1},{2,26},{10... | collective-permute-start | bytes 98312 | tf_op jit(solution)/shard_map/ppermute | solution.py:794
  35.1 0.8 %collective-permute-start.11 = (f32[4,2048]{1,0:T(4,128)S(1)}, f32[4,2048]{1,0:T(4,128)S(1)}, u32[]{:S(2)}, u32[]{:S(2)}) collective-permute-start(f32[4,2048]{1,0:T(4,128)S(1)} %get-tuple-element.27), channel_id=1, source_target_pairs={{0,16},{8,24},{16,0},{24,8},{1,17},{9,25},{17,1},{25,9},{2,18},{10... | collective-permute-start | bytes 98312 | tf_op jit(solution)/shard_map/ppermute | solution.py:794
  35.9 2.3 %collective-permute-start.12 = (f32[4,2048]{1,0:T(4,128)S(1)}, f32[4,2048]{1,0:T(4,128)S(1)}, u32[]{:S(2)}, u32[]{:S(2)}) collective-permute-start(f32[4,2048]{1,0:T(4,128)S(1)} %get-tuple-element.28), channel_id=1, source_target_pairs={{0,8},{8,0},{16,24},{24,16},{1,9},{9,1},{17,25},{25,17},{2,10},{10... | collective-permute-start | bytes 98312 | tf_op jit(solution)/shard_map/ppermute | solution.py:794
  38.2 4.3 %inverse.1 = f32[256,16,128]{2,1,0:T(8,128)} custom-call(bf16[256,256]{1,0:T(8,128)(2,1)S(1)} %copy-done.5, bf16[512,256]{1,0:T(8,128)(2,1)S(1)} %get-tuple-element.30.mats, f32[16,256,128]{2,1,0:T(8,128)S(1)} %get-tuple-element.31.spectrum), custom_call_target="tpu_custom_call" | custom-call | flops 4294967296 | bytes 4194304 | tf_op jit(solution)/shard_map/inverse/pallas_call | solution.py:901
  42.4 1.2 %patch.1 = f32[64,4,2048]{2,1,0:T(4,128)} custom-call(s32[9]{0:T(128)S(1)} %get-tuple-element.17.refs_0_, f32[64,4,2048]{2,1,0:T(4,128)} %get-tuple-element.25.refs_1_, f32[4,2048]{1,0:T(4,128)S(1)} %collective-permute-done.10.refs_2_, f32[4,2048]{1,0:T(4,128)S(1)} %collective-permute-done.11.refs_3_, ...), custom_call_target="tpu_custom_call", output_to_operand_aliasing={{}: (1, {})} | custom-call | bytes 262144 | tf_op jit(solution)/shard_map/patch/pallas_call | solution.py:916
  (22 shorter events, 0.1 us)
Async XLA Ops:
  0.6 8.3 %copy-start = (f32[832,256]{1,0:T(8,128)S(1)}, f32[832,256]{1,0:T(8,128)}, u32[]{:S(2)}) copy-start(f32[832,256]{1,0:T(8,128)} %constant.17.clone.bank) | copy-start | bytes 2555908
  0.6 22.9 %copy-start.2 = (f32[5,256,128]{2,1,0:T(8,128)S(1)}, f32[5,256,128]{2,1,0:T(8,128)}, u32[]{:S(2)}) copy-start(f32[5,256,128]{2,1,0:T(8,128)} %constant.16.clone.refs_13_) | copy-start | bytes 1966084
  0.7 22.9 %copy-start.6 = (bf16[128,192]{1,0:T(8,128)(2,1)S(1)}, bf16[128,192]{1,0:T(8,128)(2,1)}, u32[]{:S(2)}) copy-start(bf16[128,192]{1,0:T(8,128)(2,1)} %constant.15.clone.refs_10_) | copy-start | bytes 147460
  0.7 22.8 %copy-start.3 = (bf16[2,512,128]{2,1,0:T(8,128)(2,1)S(1)}, bf16[2,512,128]{2,1,0:T(8,128)(2,1)}, u32[]{:S(2)}) copy-start(bf16[2,512,128]{2,1,0:T(8,128)(2,1)} %constant.14.clone.refs_16_) | copy-start | bytes 786436
  0.7 22.8 %copy-start.4 = (bf16[2,512,128]{2,1,0:T(8,128)(2,1)S(1)}, bf16[2,512,128]{2,1,0:T(8,128)(2,1)}, u32[]{:S(2)}) copy-start(bf16[2,512,128]{2,1,0:T(8,128)(2,1)} %constant.13.clone.refs_15_) | copy-start | bytes 786436
  0.7 8.3 %copy-start.1 = (f32[3,8]{1,0:T(4,128)S(1)}, f32[3,8]{1,0:T(4,128)}, u32[]{:S(2)}) copy-start(f32[3,8]{1,0:T(4,128)} %refs_1_.3) | copy-start | bytes 292
  3.2 7.0 %collective-permute-start = (f32[4,2048]{1,0:T(4,128)S(1)}, f32[4,2048]{1,0:T(4,128)S(1)}, u32[]{:S(2)}, u32[]{:S(2)}) collective-permute-start(f32[4,2048]{1,0:T(4,128)S(1)} %get-tuple-element.19), channel_id=1, source_target_pairs={{0,24},{8,16},{16,8},{24,0},{1,25},{9,17},{17,9},{25,1},{2,26},{10... | collective-permute-start | bytes 98312 | tf_op jit(solution)/shard_map/ppermute | solution.py:794
  8.3 4.8 %collective-permute-start.1 = (f32[4,2048]{1,0:T(4,128)S(1)}, f32[4,2048]{1,0:T(4,128)S(1)}, u32[]{:S(2)}, u32[]{:S(2)}) collective-permute-start(f32[4,2048]{1,0:T(4,128)S(1)} %get-tuple-element.20), channel_id=1, source_target_pairs={{0,16},{8,24},{16,0},{24,8},{1,17},{9,25},{17,1},{25,9},{2,18},{10... | collective-permute-start | bytes 98312 | tf_op jit(solution)/shard_map/ppermute | solution.py:794
  8.3 4.8 %collective-permute-start.2 = (f32[4,2048]{1,0:T(4,128)S(1)}, f32[4,2048]{1,0:T(4,128)S(1)}, u32[]{:S(2)}, u32[]{:S(2)}) collective-permute-start(f32[4,2048]{1,0:T(4,128)S(1)} %get-tuple-element.21), channel_id=1, source_target_pairs={{0,8},{8,0},{16,24},{24,16},{1,9},{9,1},{17,25},{25,17},{2,10},{10... | collective-permute-start | bytes 98312 | tf_op jit(solution)/shard_map/ppermute | solution.py:794
  13.9 7.3 %collective-permute-start.7 = (f32[4,64,128]{2,1,0:T(8,128)S(1)}, f32[4,64,128]{2,1,0:T(8,128)S(1)}, u32[]{:S(2)}, u32[]{:S(2)}) collective-permute-start(f32[4,64,128]{2,1,0:T(8,128)S(1)} %arrange.1.refs_2_), channel_id=1, source_target_pairs={{0,5},{1,4},{2,7},{3,6},{4,1},{5,0},{6,3},{7,2},{8,13},{9,12},{10,... | collective-permute-start | bytes 393224 | tf_op jit(solution)/shard_map/ppermute | solution.py:794
  16.4 5.6 %collective-permute-start.6 = (f32[4,64,128]{2,1,0:T(8,128)S(1)}, f32[4,64,128]{2,1,0:T(8,128)S(1)}, u32[]{:S(2)}, u32[]{:S(2)}) collective-permute-start(f32[4,64,128]{2,1,0:T(8,128)S(1)} %arrange.1.refs_2_), channel_id=1, source_target_pairs={{0,4},{1,5},{2,6},{3,7},{4,0},{5,1},{6,2},{7,3},{8,12},{9,13},{10,... | collective-permute-start | bytes 393224 | tf_op jit(solution)/shard_map/ppermute | solution.py:794
  16.9 5.1 %collective-permute-start.3 = (f32[4,64,128]{2,1,0:T(8,128)S(1)}, f32[4,64,128]{2,1,0:T(8,128)S(1)}, u32[]{:S(2)}, u32[]{:S(2)}) collective-permute-start(f32[4,64,128]{2,1,0:T(8,128)S(1)} %arrange.1.refs_2_), channel_id=1, source_target_pairs={{0,1},{1,0},{2,3},{3,2},{4,5},{5,4},{6,7},{7,6},{8,9},{9,8},{10,11... | collective-permute-start | bytes 393224 | tf_op jit(solution)/shard_map/ppermute | solution.py:794
  17.4 5.1 %collective-permute-start.4 = (f32[4,64,128]{2,1,0:T(8,128)S(1)}, f32[4,64,128]{2,1,0:T(8,128)S(1)}, u32[]{:S(2)}, u32[]{:S(2)}) collective-permute-start(f32[4,64,128]{2,1,0:T(8,128)S(1)} %arrange.1.refs_2_), channel_id=1, source_target_pairs={{0,2},{1,3},{2,0},{3,1},{4,6},{5,7},{6,4},{7,5},{8,10},{9,11},{10,... | collective-permute-start | bytes 393224 | tf_op jit(solution)/shard_map/ppermute | solution.py:794
  21.2 1.3 %collective-permute-start.9 = (f32[4,64,128]{2,1,0:T(8,128)S(1)}, f32[4,64,128]{2,1,0:T(8,128)S(1)}, u32[]{:S(2)}, u32[]{:S(2)}) collective-permute-start(f32[4,64,128]{2,1,0:T(8,128)S(1)} %collective-permute-done.7.refs_7_), channel_id=1, source_target_pairs={{0,2},{1,3},{2,0},{3,1},{4,6},{5,7},{6,4},{7,5},{8,10},{9,11},{10,... | collective-permute-start | bytes 393224 | tf_op jit(solution)/shard_map/ppermute | solution.py:794
  22.0 1.3 %collective-permute-start.8 = (f32[4,64,128]{2,1,0:T(8,128)S(1)}, f32[4,64,128]{2,1,0:T(8,128)S(1)}, u32[]{:S(2)}, u32[]{:S(2)}) collective-permute-start(f32[4,64,128]{2,1,0:T(8,128)S(1)} %collective-permute-done.6.refs_6_), channel_id=1, source_target_pairs={{0,2},{1,3},{2,0},{3,1},{4,6},{5,7},{6,4},{7,5},{8,10},{9,11},{10,... | collective-permute-start | bytes 393224 | tf_op jit(solution)/shard_map/ppermute | solution.py:794
  22.0 1.5 %collective-permute-start.5 = (f32[4,64,128]{2,1,0:T(8,128)S(1)}, f32[4,64,128]{2,1,0:T(8,128)S(1)}, u32[]{:S(2)}, u32[]{:S(2)}) collective-permute-start(f32[4,64,128]{2,1,0:T(8,128)S(1)} %collective-permute-done.3.refs_3_), channel_id=1, source_target_pairs={{0,2},{1,3},{2,0},{3,1},{4,6},{5,7},{6,4},{7,5},{8,10},{9,11},{10,... | collective-permute-start | bytes 393224 | tf_op jit(solution)/shard_map/ppermute | solution.py:794
  23.5 14.6 %copy-start.5 = (bf16[256,256]{1,0:T(8,128)(2,1)S(1)}, bf16[256,256]{1,0:T(8,128)(2,1)}, u32[]{:S(2)}) copy-start(bf16[256,256]{1,0:T(8,128)(2,1)} %constant.12.clone.iz) | copy-start | bytes 393220
  33.7 8.7 %collective-permute-start.10 = (f32[4,2048]{1,0:T(4,128)S(1)}, f32[4,2048]{1,0:T(4,128)S(1)}, u32[]{:S(2)}, u32[]{:S(2)}) collective-permute-start(f32[4,2048]{1,0:T(4,128)S(1)} %get-tuple-element.26), channel_id=1, source_target_pairs={{0,24},{8,16},{16,8},{24,0},{1,25},{9,17},{17,9},{25,1},{2,26},{10... | collective-permute-start | bytes 98312 | tf_op jit(solution)/shard_map/ppermute | solution.py:794
  35.1 7.3 %collective-permute-start.11 = (f32[4,2048]{1,0:T(4,128)S(1)}, f32[4,2048]{1,0:T(4,128)S(1)}, u32[]{:S(2)}, u32[]{:S(2)}) collective-permute-start(f32[4,2048]{1,0:T(4,128)S(1)} %get-tuple-element.27), channel_id=1, source_target_pairs={{0,16},{8,24},{16,0},{24,8},{1,17},{9,25},{17,1},{25,9},{2,18},{10... | collective-permute-start | bytes 98312 | tf_op jit(solution)/shard_map/ppermute | solution.py:794
  35.9 6.6 %collective-permute-start.12 = (f32[4,2048]{1,0:T(4,128)S(1)}, f32[4,2048]{1,0:T(4,128)S(1)}, u32[]{:S(2)}, u32[]{:S(2)}) collective-permute-start(f32[4,2048]{1,0:T(4,128)S(1)} %get-tuple-element.28), channel_id=1, source_target_pairs={{0,8},{8,0},{16,24},{24,16},{1,9},{9,1},{17,25},{25,17},{2,10},{10... | collective-permute-start | bytes 98312 | tf_op jit(solution)/shard_map/ppermute | solution.py:794

commit v3 on v2

--- a/solution.py
+++ b/solution.py
@@ -297,10 +297,10 @@
     rz = iz.reshape(nfz, coarse_z, REFINE).mean(2)
     dz = (iz[:, REFINE - 1 :: REFINE] - np.roll(iz, 1, 1)[:, ::REFINE]) / REFINE
     eye = np.eye(rows)
-    for name, mat in (("rz", rz), ("dz", dz)):
-        big = np.einsum("ij,kz->ikjz", eye, mat).reshape(rows * nfz, rows * coarse_z)
-        hi, lo = halves_np(big)
-        out[name] = np.stack([hi, lo])
+    big = [
+        np.einsum("ij,kz->ikjz", eye, mat).reshape(rows * nfz, rows * coarse_z) for mat in (rz, dz)
+    ]
+    out["rz"] = np.stack(halves_np(np.concatenate(big, 1)))
     coarse = np.arange(quarter)
     turns = (coarse[:, None] * coarse[None, :]) % quarter
     angle = turns * 2 * np.pi / quarter
@@ -418,9 +418,8 @@
 def prep_kernel(taps, bank, mats, rmats, wu, ww):
     nfx = mats.shape[1]
     quarter = nfx // REFINE
-    lanes = wu.shape[0] // 3
-    rows = wu.shape[1] // lanes
-    per = lanes // rows
+    lanes = wu.shape[0] // 2
+    duo = lanes // 2
     at_ex = 6 * TAPS
     at_e4 = at_ex + 2 * nfx
     at_gz = at_e4 + 2 * quarter
@@ -445,84 +444,123 @@
         hi, lo = halves(coarse)
         rmats[0, at : at + quarter, :] = hi
         rmats[1, at : at + quarter, :] = lo
-    band = lax.broadcasted_iota(jnp.int32, (lanes, lanes), 0) // per
+    band = lax.broadcasted_iota(jnp.int32, (duo, lanes), 0) // (duo // 2)
     for which, target in ((0, wu), (1, ww)):
         value = weighted(at_gz + which * TAPS, 2) * bank[at_zz : at_zz + lanes, :]
         value = value[:, 0:lanes] + value[:, lanes : 2 * lanes]
-        for row in range(rows):
-            hi, lo = halves(jnp.where(band == row, value, 0.0))
+        for row in range(2):
+            hi, lo = halves(jnp.where(band == row, value[0:duo], 0.0))
             at = row * lanes
-            target[0:lanes, at : at + lanes] = hi
-            target[lanes : 2 * lanes, at : at + lanes] = hi
-            target[2 * lanes : 3 * lanes, at : at + lanes] = lo
+            target[0:duo, at : at + lanes] = hi
+            target[duo:lanes, at : at + lanes] = hi
+            target[lanes : lanes + duo, at : at + lanes] = lo
+            target[lanes + duo : 2 * lanes, at : at + lanes] = jnp.zeros_like(lo)
 
 
 def solve_kernel(farm_count, pairs, groups, info, taps, *refs):
     pieces = refs[:groups]
-    (fx, wu_any, ww_any, planes_any, rmats, rz, dz, tiles, spectrum) = refs[groups : groups + 9]
-    outs = refs[groups + 9 : groups + 9 + farm_count]
-    base = refs[groups + 9 + farm_count]
-    (data, wu, ww, planes, left, field, mean_p, step_p, fresh, out_stage, zero_add, shelf, sems) = refs[
-        groups + 10 + farm_count :
+    (fx, wu, ww, planes, rmats, rz, tiles, spectrum) = refs[groups : groups + 8]
+    outs = refs[groups + 8 : groups + 8 + farm_count]
+    base = refs[groups + 8 + farm_count]
+    (left, field, mean_p, step_p, fresh, out_stage, zero_add, shelf, sems) = refs[
+        groups + 9 + farm_count :
     ]
-    take = pltpu.make_async_copy(tiles, shelf, sems.at[groups + 3])
+    take = pltpu.make_async_copy(tiles, shelf, sems.at[0])
     take.start()
     group = info[farm_count + pairs]
-    copies = []
-    for shift in range(groups):
-        copies.append(
-            pltpu.make_async_copy(pieces[shift], data.at[group ^ shift], sems.at[shift])
-        )
-    weights = [
-        pltpu.make_async_copy(wu_any, wu, sems.at[groups]),
-        pltpu.make_async_copy(ww_any, ww, sems.at[groups + 1]),
-        pltpu.make_async_copy(planes_any, planes, sems.at[groups + 2]),
-    ]
-    for copy in copies + weights:
-        copy.start()
-    for copy in copies:
-        copy.wait()
-    channels, width_x, lanes = data.shape[1:]
-    rows = wu.shape[1] // lanes
+    channels, width_x, lanes = pieces[0].shape
+    rows = mean_p.shape[0]
     per = lanes // rows
     coarse_y = groups * rows
     fine_y = coarse_y * REFINE
     own_fine = rows * REFINE
     coarse_rows = fx.shape[0]
 
+    def band(axis):
+        quarter = 1.0 / REFINE
+        return (
+            (taps[axis, 6] + taps[axis, 7]) * quarter,
+            (taps[axis, 2] + taps[axis, 3] + taps[axis, 4] + taps[axis, 5]) * quarter,
+            (taps[axis, 0] + taps[axis, 1]) * quarter,
+        )
+
+    lane = lax.broadcasted_iota(jnp.int32, (width_x, lanes), 1)
+    previous = group ^ ((group + groups - 1) & (groups - 1))
+    following = group ^ ((group + 1) & (groups - 1))
+
+    def beside(shift, channel):
+        value = pieces[1][channel]
+        mark = 3
+        while mark < groups:
+            value = jnp.where(shift == mark, pieces[mark][channel], value)
+            mark = 2 * mark + 1
+        return value
+
+    for channel in range(channels):
+        here = pieces[0][channel]
+        before, after = beside(previous, channel), beside(following, channel)
+        lag, mid, lead = band(1)
+        low = jnp.where(lane < per, pltpu.roll(before, per, 1), pltpu.roll(here, per, 1))
+        high = jnp.where(
+            lane >= lanes - per, pltpu.roll(after, lanes - per, 1), pltpu.roll(here, lanes - per, 1)
+        )
+        value = mid * here + lag * low + lead * high
+        lag, mid, lead = band(2)
+        spot = lane % per
+        low = jnp.where(spot == 0, pltpu.roll(value, lanes - per + 1, 1), pltpu.roll(value, 1, 1))
+        high = jnp.where(
+            spot == per - 1, pltpu.roll(value, per - 1, 1), pltpu.roll(value, lanes - 1, 1)
+        )
+        value = mid * value + lag * low + lead * high
+        lag, mid, lead = band(0)
+        value = (
+            mid * value
+            + lag * pltpu.roll(value, 1, 0)
+            + lead * pltpu.roll(value, width_x - 1, 0)
+        )
+        fresh[channel] = value
+    duo = lanes // 2
+    front = lax.broadcasted_iota(jnp.int32, (width_x, lanes), 1) < duo
+    ahead_half = lax.broadcasted_iota(jnp.int32, (coarse_rows, lanes), 1) < duo
     for block in range(groups):
-        hi_lo = [halves(data[block, channel]) for channel in range(3)]
-        hi = jnp.concatenate([pair[0] for pair in hi_lo], 1)
-        lo = jnp.concatenate([pair[1] for pair in hi_lo], 1)
+        doubled = []
+        for channel in range(3):
+            value = pieces[block][channel]
+            turned = pltpu.roll(value, duo, 1)
+            doubled += [jnp.where(front, value, turned), jnp.where(front, turned, value)]
+        hi, lo = halves(jnp.concatenate(doubled, 1))
         turned = mm(fx[...], jnp.concatenate([hi, lo, hi], 0))
         for channel in range(3):
-            hi, lo = halves(turned[:, channel * lanes : (channel + 1) * lanes])
-            at = block * coarse_rows
-            left[channel, at : at + coarse_rows, :] = jnp.concatenate([hi, lo, hi], 1)
-    for copy in weights:
-        copy.wait()
+            for pair in range(2):
+                at = (2 * channel + pair) * lanes
+                value = turned[:, at : at + lanes]
+                hi = value.astype(BF)
+                rest = jnp.where(ahead_half, value, value - hi.astype(F32)).astype(BF)
+                at = (2 * block + pair) * coarse_rows
+                left[channel, at : at + coarse_rows, :] = jnp.concatenate([rest, hi], 1)
     chunk = min(groups, 4)
     for channel in range(3):
         weight = ww if channel == 2 else wu
         for block in range(0, groups, chunk):
-            at = block * coarse_rows
-            value = mm(left[channel, at : at + chunk * coarse_rows, :], weight[...])
+            at = 2 * block * coarse_rows
+            value = mm(left[channel, at : at + 2 * chunk * coarse_rows, :], weight[...])
             for inner in range(chunk):
                 for row in range(rows):
-                    field[channel, (block + inner) * rows + row] = value[
-                        inner * coarse_rows : (inner + 1) * coarse_rows,
-                        row * lanes : (row + 1) * lanes,
+                    at_y = (((group ^ (block + inner)) - group) * rows + row) & (coarse_y - 1)
+                    at = (2 * inner + row // 2) * coarse_rows
+                    field[channel, at_y] = value[
+                        at : at + coarse_rows, (row % 2) * lanes : (row % 2 + 1) * lanes
                     ]
 
     sums = jnp.concatenate(
-        [jnp.sum(data[block, 1], axis=0, keepdims=True) for block in range(groups)], 0
+        [jnp.sum(pieces[block][1], axis=0, keepdims=True) for block in range(groups)], 0
     )
     total_z = taps[2, 0]
     for tap in range(1, TAPS):
         total_z = total_z + taps[2, tap]
     sums = sums * total_z
     shape = (groups, lanes)
-    coarse_id = rows * lax.broadcasted_iota(jnp.int32, shape, 0)
+    coarse_id = rows * (lax.broadcasted_iota(jnp.int32, shape, 0) ^ group)
     coarse_id = coarse_id + lax.broadcasted_iota(jnp.int32, shape, 1) // per
     corner = (lax.broadcasted_iota(jnp.int32, (8, lanes), 0) == 0) & (
         lax.broadcasted_iota(jnp.int32, (8, lanes), 1) == 0
@@ -538,12 +576,11 @@
         zero_add[index] = jnp.where(corner, value, 0.0)
 
     take.wait()
-    give = pltpu.make_async_copy(shelf, base, sems.at[groups + 4])
+    give = pltpu.make_async_copy(shelf, base, sems.at[1])
     give.start()
-    first = rows * group
 
     def at_row(offset):
-        return (first + offset) & (coarse_y - 1)
+        return offset % coarse_y
 
     def tap_y(offset):
         return taps[1, offset + 2]
@@ -565,21 +602,23 @@
         quad = [value * value for value in root]
         quad = [value * value for value in quad]
 
-        def horner(offset, sign):
-            def body(i, acc):
+        def horner(i, acc):
+            spread = []
+            for way, (offset, sign) in enumerate(((-2, -1), (rows + 1, 1))):
                 row = at_row(offset + sign * (coarse_y - 1 - i))
                 loaded = [[coarse(c, row, side) for side in range(2)] for c in range(3)]
-                return tuple(
-                    acc[c * 4 + part] * quad[part] + loaded[c][part % 2]
+                spread += [
+                    acc[12 * way + c * 4 + part] * quad[part] + loaded[c][part % 2]
                     for c in range(3)
                     for part in range(4)
-                )
-
-            zeros = tuple(jnp.zeros((8, lanes), F32) for _ in range(12))
-            return lax.fori_loop(0, coarse_y, body, zeros, unroll=4)
-
-        below = horner(-2, -1)
-        above = horner(rows + 1, 1)
+                ]
+            return tuple(spread)
+
+        sums_far = tuple(jnp.zeros((8, lanes), F32) for _ in range(24))
+        for i in range(coarse_y):
+            sums_far = horner(i, sums_far)
+        below, above = sums_far[:12], sums_far[12:]
+        opening = jnp.where(step == 0, 1.0, 0.0)
         near = list(range(-1, rows + 1))
         near_u = {m: [coarse(0, at_row(m), side) for side in range(2)] for m in near}
         near_v = {m: [coarse(1, at_row(m), side) for side in range(2)] for m in near}
@@ -637,6 +676,8 @@
             for j in range(own_fine - 1, -1, -1):
                 back = r * (back + source[j])
                 pressure[j] = kappa * (ahead[j] + back)
+            if part == 0:
+                pressure = [pressure[j] + opening * zero_add[j] for j in range(own_fine + 1)]
             spot = pl.ds(slots[part], 8)
             for j in range(own_fine):
                 spectrum[j, spot, :] = pressure[j + 1]
@@ -650,17 +691,6 @@
         return carry
 
     lax.fori_loop(0, half_rows // 8, sweep, 0)
-    for j in range(own_fine):
-        spectrum[j, 0:8, :] = spectrum[j, 0:8, :] + zero_add[j + 1]
-    for m in range(rows):
-        at = REFINE * m
-        total = zero_add[at + 1]
-        for q in range(1, REFINE):
-            total = total + zero_add[at + 1 + q]
-        mean_p[m, 0:8, :] = mean_p[m, 0:8, :] + total * (1.0 / REFINE)
-        step = (zero_add[at + REFINE] - zero_add[at]) * (1.0 / REFINE)
-        step_p[m, 0:8, :] = step_p[m, 0:8, :] + step
-
     def left_three(count, stacked):
         hi, lo = halves(stacked)
         value = mm(rmats[0, 0:count, :], hi) + mm(rmats[0, 0:count, :], lo)
@@ -674,7 +704,8 @@
     slope = left_three(width_x, jnp.concatenate([step_p[m] for m in range(rows)], 1))
     mean_x, step_x = smooth[0:width_x], smooth[width_x : 2 * width_x]
     through = right_three(jnp.concatenate([step_x, slope, mean_x], 0), rz)
-    part_w = right_three(mean_x, dz)
+    part_w = through[2 * width_x : 3 * width_x, lanes:]
+    through = through[:, 0:lanes]
     change = [
         -through[0:width_x],
         -through[width_x : 2 * width_x],
@@ -682,40 +713,8 @@
         through[2 * width_x : 3 * width_x],
     ]
 
-    def band(axis):
-        quarter = 1.0 / REFINE
-        return (
-            (taps[axis, 6] + taps[axis, 7]) * quarter,
-            (taps[axis, 2] + taps[axis, 3] + taps[axis, 4] + taps[axis, 5]) * quarter,
-            (taps[axis, 0] + taps[axis, 1]) * quarter,
-        )
-
-    lane = lax.broadcasted_iota(jnp.int32, (width_x, lanes), 1)
-    previous = (group + groups - 1) & (groups - 1)
-    following = (group + 1) & (groups - 1)
     for channel in range(channels):
-        here = data[group, channel]
-        before, after = data[previous, channel], data[following, channel]
-        lag, mid, lead = band(1)
-        low = jnp.where(lane < per, pltpu.roll(before, per, 1), pltpu.roll(here, per, 1))
-        high = jnp.where(
-            lane >= lanes - per, pltpu.roll(after, lanes - per, 1), pltpu.roll(here, lanes - per, 1)
-        )
-        value = mid * here + lag * low + lead * high
-        lag, mid, lead = band(2)
-        spot = lane % per
-        low = jnp.where(spot == 0, pltpu.roll(value, lanes - per + 1, 1), pltpu.roll(value, 1, 1))
-        high = jnp.where(
-            spot == per - 1, pltpu.roll(value, per - 1, 1), pltpu.roll(value, lanes - 1, 1)
-        )
-        value = mid * value + lag * low + lead * high
-        lag, mid, lead = band(0)
-        value = (
-            mid * value
-            + lag * pltpu.roll(value, 1, 0)
-            + lead * pltpu.roll(value, width_x - 1, 0)
-        )
-        fresh[channel] = value + change[channel]
+        fresh[channel] = fresh[channel] + change[channel]
     shifts = [info[farm_count + pair] for pair in range(pairs)]
     edge = width_x // pairs
     row_lanes = edge * per
@@ -732,15 +731,14 @@
     give.wait()
 
 
-def inverse_kernel(iz, mats, spectrum, out):
+def inverse_kernel(iz, mats, spectrum, out, middle):
     count, nfx, lanes = spectrum.shape
+    for at in range(0, count, 4):
+        hi, lo = halves(spectrum[at : at + 4].reshape(4 * nfx, lanes))
+        both = mm(jnp.concatenate([hi, lo], 1), iz[...])
+        middle[at : at + 4] = (both[:, 0:lanes] + both[:, lanes : 2 * lanes]).reshape(4, nfx, lanes)
     for at in range(0, count, 2):
-        value = []
-        for row in (at, at + 1):
-            hi, lo = halves(spectrum[row])
-            both = mm(jnp.concatenate([hi, lo], 1), iz[...])
-            value.append(both[:, 0:lanes] + both[:, lanes : 2 * lanes])
-        hi, lo = halves(jnp.concatenate(value, 1))
+        hi, lo = halves(jnp.concatenate([middle[at], middle[at + 1]], 1))
         upper = mm(mats[...], hi)
         final = upper[0:nfx] + upper[nfx : 2 * nfx] + mm(mats[0:nfx, :], lo)
         for row in range(2):
@@ -831,8 +829,8 @@
         out_shape=[
             jax.ShapeDtypeStruct((2 * NFX, NFX), BF),
             jax.ShapeDtypeStruct((2, 2 * width_x, NFX), BF),
-            jax.ShapeDtypeStruct((3 * lanes, rows * NFZ), BF),
-            jax.ShapeDtypeStruct((3 * lanes, rows * NFZ), BF),
+            jax.ShapeDtypeStruct((2 * lanes, 2 * NFZ), BF),
+            jax.ShapeDtypeStruct((2 * lanes, 2 * NFZ), BF),
         ],
         in_specs=[in_smem(), in_vmem()],
         out_specs=[in_vmem()] * 4,
@@ -866,18 +864,11 @@
         + [tile_shape] * farm_count
         + [jax.ShapeDtypeStruct(coarse_tiles.shape, F32)],
         in_specs=[in_smem()] * 2
-        + [anywhere()] * groups
-        + [in_vmem()]
-        + [anywhere()] * 3
-        + [in_vmem()] * 3
+        + [in_vmem()] * (groups + 6)
         + [in_hbm()],
         out_specs=[in_vmem()] * (farm_count + 1) + [in_hbm()],
         scratch_shapes=[
-            pltpu.VMEM((groups, CH, width_x, lanes), F32),
-            pltpu.VMEM((3 * lanes, rows * NFZ), BF),
-            pltpu.VMEM((3 * lanes, rows * NFZ), BF),
-            pltpu.VMEM(const["planes"].shape, F32),
-            pltpu.VMEM((3, groups * coarse_rows, 3 * lanes), BF),
+            pltpu.VMEM((3, 2 * groups * coarse_rows, 2 * lanes), BF),
             pltpu.VMEM((3, coarse_y, coarse_rows, NFZ), F32),
             pltpu.VMEM((rows, NFX, NFZ), F32),
             pltpu.VMEM((rows, NFX, NFZ), F32),
@@ -885,14 +876,14 @@
             pltpu.VMEM((farm_count, rows, row_width), F32),
             pltpu.VMEM((own_fine + 1, 8, lanes), F32),
             pltpu.VMEM(coarse_tiles.shape, F32),
-            pltpu.SemaphoreType.DMA((groups + 5,)),
+            pltpu.SemaphoreType.DMA((2,)),
         ],
         compiler_params=limit(40),
         cost_estimate=cost(4 << 30, 8 << 20),
     )(
         info, prolong_taps,
         *[held[s] for s in range(groups)],
-        const["fx"], wu, ww, const["planes"], rmats, const["rz"], const["dz"],
+        const["fx"], wu, ww, const["planes"], rmats, const["rz"],
         keep_hbm(coarse_tiles),
     )
     returned = [fresh[0]] + [flip(fresh[s], "farm", s) for s in range(1, farm_count)]
@@ -909,6 +900,7 @@
             pl.BlockSpec((half, NFX, NFZ), lambda i: (i, 0, 0)),
         ],
         out_specs=pl.BlockSpec((NFX, half, NFZ), lambda i: (0, i, 0)),
+        scratch_shapes=[pltpu.VMEM((half, NFX, NFZ), F32)],
         compiler_params=limit(24),
         cost_estimate=cost(4 << 30, 4 << 20),
     )(const["iz"], mats, spectrum)

time: 43.8 us -> 41.5 us (0.947)
  Pallas kernels: 19.6 us -> 17.2 us
    pallas_call x1, Pallas kernels: 10.2 us -> 8.66 us  [fast_local(): pl.pallas_call(bind(solve_kernel, farm_count, pairs, groups), name='solve...]
    pallas_call x1, Pallas kernels: 4.25 us -> 3.36 us  [fast_local(): pl.pallas_call(inverse_kernel, name='inverse', out_shape=jax.ShapeDtypeSt...]
  transfers between devices with their start and end apart: 13 -> 13, of which waited for: 6 -> 6; matrix products, arithmetic and copies ran while one was open for 0% -> 0% of each run, Pallas kernels for 12% -> 10%
where the time goes in v3:
time: 41.5 us; the launch traced here: 41.3 us
  Pallas kernels  17.2 us (41%)
  starting transfers between devices  14.3 us (34%)
  waiting for transfers between devices  9.02 us (22%)
  between operations  0.73 us (2%)
    ppermute x13, starting transfers between devices, flip(): return lax.ppermute(value, axis, [(i, i ^ bits) for i in range(count)])  14.3 us
    ppermute x13, waiting for transfers between devices, flip(): return lax.ppermute(value, axis, [(i, i ^ bits) for i in range(count)])  9.02 us
    pallas_call x1, Pallas kernels, fast_local(): pl.pallas_call(bind(solve_kernel, farm_count, pairs, groups), name='solve...  8.66 us
    pallas_call x1, Pallas kernels, fast_local(): pl.pallas_call(inverse_kernel, name='inverse', out_shape=jax.ShapeDtypeSt...  3.36 us
    pallas_call x1, Pallas kernels, fast_local(): pl.pallas_call(bind(pick_kernel, local_tiles, farm_count, pairs), name='p...  2.46 us
    pallas_call x1, Pallas kernels, fast_local(): pl.pallas_call(bind(patch_kernel, farm_count), name='patch', out_shape=ja...  1.23 us
  transfers between devices with their start and end apart: 13, of which 6 were waited for; matrix products, arithmetic and copies ran while one was open for 0% of the time, Pallas kernels for 10%

profile of v3, /device:TPU:0, one launch (start us, length us, event | category | flops | bytes accessed | tf_op | source)
XLA Modules:
  0.0 41.3 jit_solution(6567110702883448229)
XLA Ops:
  0.6 0.0 copy-start
  0.6 0.0 copy-start.2
  0.7 2.5 %pick.1 = (s32[9]{0:T(128)S(1)}, f32[4,2048]{1,0:T(4,128)S(1)}, f32[4,2048]{1,0:T(4,128)S(1)}, f32[4,2048]{1,0:T(4,128)S(1)}, f32[4,2048]{1,0:T(4,128)S(1)}) custom-call(s32[4,4]{1,0:T(4,128)} %refs_0_.1, s32[4]{0:T(128)} %refs_1_.2, f32[64,4,2048]{2,1,0:T(4,128)} %refs_16_.1), custom_call_target="tpu_custom_call" | custom-call | bytes 262144 | tf_op jit(solution)/shard_map/pick/pallas_call | solution.py:809
  3.2 5.1 %collective-permute-start = (f32[4,2048]{1,0:T(4,128)S(1)}, f32[4,2048]{1,0:T(4,128)S(1)}, u32[]{:S(2)}, u32[]{:S(2)}) collective-permute-start(f32[4,2048]{1,0:T(4,128)S(1)} %get-tuple-element.19), channel_id=1, source_target_pairs={{0,24},{8,16},{16,8},{24,0},{1,25},{9,17},{17,9},{25,1},{2,26},{10... | collective-permute-start | bytes 98312 | tf_op jit(solution)/shard_map/ppermute | solution.py:792
  8.3 0.6 %collective-permute-start.2 = (f32[4,2048]{1,0:T(4,128)S(1)}, f32[4,2048]{1,0:T(4,128)S(1)}, u32[]{:S(2)}, u32[]{:S(2)}) collective-permute-start(f32[4,2048]{1,0:T(4,128)S(1)} %get-tuple-element.21), channel_id=1, source_target_pairs={{0,8},{8,0},{16,24},{24,16},{1,9},{9,1},{17,25},{25,17},{2,10},{10... | collective-permute-start | bytes 98312 | tf_op jit(solution)/shard_map/ppermute | solution.py:792
  8.9 0.7 %prep.1 = (bf16[512,256]{1,0:T(8,128)(2,1)S(1)}, bf16[2,128,256]{2,1,0:T(8,128)(2,1)S(1)}, bf16[256,256]{1,0:T(8,128)(2,1)S(1)}, bf16[256,256]{1,0:T(8,128)(2,1)S(1)}) custom-call(f32[3,8]{1,0:T(4,128)S(1)} %copy-done.1, f32[832,256]{1,0:T(8,128)S(1)} %copy-done), custom_call_target="tpu_custom_call" | custom-call | bytes 6291456 | tf_op jit(solution)/shard_map/prep/pallas_call | solution.py:826
  9.7 0.5 %collective-permute-done.refs_2_ = f32[4,2048]{1,0:T(4,128)S(1)} collective-permute-done((f32[4,2048]{1,0:T(4,128)S(1)}, f32[4,2048]{1,0:T(4,128)S(1)}, u32[]{:S(2)}, u32[]{:S(2)}) %collective-permute-start) | collective-permute-done | bytes 32800 | tf_op jit(solution)/shard_map/ppermute | solution.py:792
  10.2 2.9 %collective-permute-done.1.refs_3_ = f32[4,2048]{1,0:T(4,128)S(1)} collective-permute-done((f32[4,2048]{1,0:T(4,128)S(1)}, f32[4,2048]{1,0:T(4,128)S(1)}, u32[]{:S(2)}, u32[]{:S(2)}) %collective-permute-start.1) | collective-permute-done | bytes 32800 | tf_op jit(solution)/shard_map/ppermute | solution.py:792
  13.1 0.7 %arrange.1.refs_2_ = f32[4,64,128]{2,1,0:T(8,128)S(1)} custom-call(s32[9]{0:T(128)S(1)} %get-tuple-element.17.refs_0_, bf16[2,128,256]{2,1,0:T(8,128)(2,1)S(1)} %get-tuple-element.18.refs_1_.refs_14_, f32[4,2048]{1,0:T(4,128)S(1)} %collective-permute-done.refs_2_, f32[4,2048]{1,0:T(4,128)S(1)} %collective-permute-done.1.refs_3_, ...), custom_call_target="tpu_custom_call" | custom-call | bytes 262144 | tf_op jit(solution)/shard_map/arrange/pallas_call | solution.py:841
  13.8 2.5 %collective-permute-start.7 = (f32[4,64,128]{2,1,0:T(8,128)S(1)}, f32[4,64,128]{2,1,0:T(8,128)S(1)}, u32[]{:S(2)}, u32[]{:S(2)}) collective-permute-start(f32[4,64,128]{2,1,0:T(8,128)S(1)} %arrange.1.refs_2_), channel_id=1, source_target_pairs={{0,5},{1,4},{2,7},{3,6},{4,1},{5,0},{6,3},{7,2},{8,13},{9,12},{10,... | collective-permute-start | bytes 393224 | tf_op jit(solution)/shard_map/ppermute | solution.py:792
  16.4 0.5 %collective-permute-start.6 = (f32[4,64,128]{2,1,0:T(8,128)S(1)}, f32[4,64,128]{2,1,0:T(8,128)S(1)}, u32[]{:S(2)}, u32[]{:S(2)}) collective-permute-start(f32[4,64,128]{2,1,0:T(8,128)S(1)} %arrange.1.refs_2_), channel_id=1, source_target_pairs={{0,4},{1,5},{2,6},{3,7},{4,0},{5,1},{6,2},{7,3},{8,12},{9,13},{10,... | collective-permute-start | bytes 393224 | tf_op jit(solution)/shard_map/ppermute | solution.py:792
  16.9 0.5 %collective-permute-start.3 = (f32[4,64,128]{2,1,0:T(8,128)S(1)}, f32[4,64,128]{2,1,0:T(8,128)S(1)}, u32[]{:S(2)}, u32[]{:S(2)}) collective-permute-start(f32[4,64,128]{2,1,0:T(8,128)S(1)} %arrange.1.refs_2_), channel_id=1, source_target_pairs={{0,1},{1,0},{2,3},{3,2},{4,5},{5,4},{6,7},{7,6},{8,9},{9,8},{10,11... | collective-permute-start | bytes 393224 | tf_op jit(solution)/shard_map/ppermute | solution.py:792
  17.4 3.8 %collective-permute-done.7.refs_7_ = f32[4,64,128]{2,1,0:T(8,128)S(1)} collective-permute-done((f32[4,64,128]{2,1,0:T(8,128)S(1)}, f32[4,64,128]{2,1,0:T(8,128)S(1)}, u32[]{:S(2)}, u32[]{:S(2)}) %collective-permute-start.7) | collective-permute-done | bytes 131104 | tf_op jit(solution)/shard_map/ppermute | solution.py:792
  21.2 0.8 %collective-permute-done.6.refs_6_ = f32[4,64,128]{2,1,0:T(8,128)S(1)} collective-permute-done((f32[4,64,128]{2,1,0:T(8,128)S(1)}, f32[4,64,128]{2,1,0:T(8,128)S(1)}, u32[]{:S(2)}, u32[]{:S(2)}) %collective-permute-start.6) | collective-permute-done | bytes 131104 | tf_op jit(solution)/shard_map/ppermute | solution.py:792
  22.0 0.5 %collective-permute-start.5 = (f32[4,64,128]{2,1,0:T(8,128)S(1)}, f32[4,64,128]{2,1,0:T(8,128)S(1)}, u32[]{:S(2)}, u32[]{:S(2)}) collective-permute-start(f32[4,64,128]{2,1,0:T(8,128)S(1)} %collective-permute-done.3.refs_3_), channel_id=1, source_target_pairs={{0,2},{1,3},{2,0},{3,1},{4,6},{5,7},{6,4},{7,5},{8,10},{9,11},{10,... | collective-permute-start | bytes 393224 | tf_op jit(solution)/shard_map/ppermute | solution.py:792
  22.5 0.0 collective-permute-done.9.refs_9_
  22.5 0.8 %collective-permute-done.8.refs_8_ = f32[4,64,128]{2,1,0:T(8,128)S(1)} collective-permute-done((f32[4,64,128]{2,1,0:T(8,128)S(1)}, f32[4,64,128]{2,1,0:T(8,128)S(1)}, u32[]{:S(2)}, u32[]{:S(2)}) %collective-permute-start.8) | collective-permute-done | bytes 131104 | tf_op jit(solution)/shard_map/ppermute | solution.py:792
  23.3 0.2 collective-permute-done.5.refs_5_
  23.5 8.7 %solve.1 = (f32[16,256,128]{2,1,0:T(8,128)S(1)}, f32[4,2048]{1,0:T(4,128)S(1)}, f32[4,2048]{1,0:T(4,128)S(1)}, f32[4,2048]{1,0:T(4,128)S(1)}, f32[4,2048]{1,0:T(4,128)S(1)}, /*index=5*/f32[64,4,2048]{2,1,0:T(4,128)}) custom-call(s32[9]{0:T(128)S(1)} %get-tuple-element.17.refs_0_, f32[3,8]{1,0:T(4,128)S(1)} %copy-done.1, f32[4,64,128]{2,1,0:T(8,128)S(1)} %arrange.1.refs_2_, ...), custom_call_target="tpu_custom_call" | custom-call | flops 4294967296 | bytes 8388608 | tf_op jit(solution)/shard_map/solve/pallas_call | solution.py:860
  32.2 1.4 %collective-permute-start.10 = (f32[4,2048]{1,0:T(4,128)S(1)}, f32[4,2048]{1,0:T(4,128)S(1)}, u32[]{:S(2)}, u32[]{:S(2)}) collective-permute-start(f32[4,2048]{1,0:T(4,128)S(1)} %get-tuple-element.26), channel_id=1, source_target_pairs={{0,24},{8,16},{16,8},{24,0},{1,25},{9,17},{17,9},{25,1},{2,26},{10... | collective-permute-start | bytes 98312 | tf_op jit(solution)/shard_map/ppermute | solution.py:792
  33.6 0.8 %collective-permute-start.11 = (f32[4,2048]{1,0:T(4,128)S(1)}, f32[4,2048]{1,0:T(4,128)S(1)}, u32[]{:S(2)}, u32[]{:S(2)}) collective-permute-start(f32[4,2048]{1,0:T(4,128)S(1)} %get-tuple-element.27), channel_id=1, source_target_pairs={{0,16},{8,24},{16,0},{24,8},{1,17},{9,25},{17,1},{25,9},{2,18},{10... | collective-permute-start | bytes 98312 | tf_op jit(solution)/shard_map/ppermute | solution.py:792
  34.4 2.3 %collective-permute-start.12 = (f32[4,2048]{1,0:T(4,128)S(1)}, f32[4,2048]{1,0:T(4,128)S(1)}, u32[]{:S(2)}, u32[]{:S(2)}) collective-permute-start(f32[4,2048]{1,0:T(4,128)S(1)} %get-tuple-element.28), channel_id=1, source_target_pairs={{0,8},{8,0},{16,24},{24,16},{1,9},{9,1},{17,25},{25,17},{2,10},{10... | collective-permute-start | bytes 98312 | tf_op jit(solution)/shard_map/ppermute | solution.py:792
  36.6 3.4 %inverse.1 = f32[256,16,128]{2,1,0:T(8,128)} custom-call(bf16[256,256]{1,0:T(8,128)(2,1)S(1)} %copy-done.4, bf16[512,256]{1,0:T(8,128)(2,1)S(1)} %get-tuple-element.30.mats, f32[16,256,128]{2,1,0:T(8,128)S(1)} %get-tuple-element.31.spectrum), custom_call_target="tpu_custom_call" | custom-call | flops 4294967296 | bytes 4194304 | tf_op jit(solution)/shard_map/inverse/pallas_call | solution.py:892
  40.0 1.2 %patch.1 = f32[64,4,2048]{2,1,0:T(4,128)} custom-call(s32[9]{0:T(128)S(1)} %get-tuple-element.17.refs_0_, f32[64,4,2048]{2,1,0:T(4,128)} %get-tuple-element.25.refs_1_, f32[4,2048]{1,0:T(4,128)S(1)} %collective-permute-done.10.refs_2_, f32[4,2048]{1,0:T(4,128)S(1)} %collective-permute-done.11.refs_3_, ...), custom_call_target="tpu_custom_call", output_to_operand_aliasing={{}: (1, {})} | custom-call | bytes 262144 | tf_op jit(solution)/shard_map/patch/pallas_call | solution.py:908
  (20 shorter events, 0.1 us)
Async XLA Ops:
  0.6 8.3 %copy-start = (f32[832,256]{1,0:T(8,128)S(1)}, f32[832,256]{1,0:T(8,128)}, u32[]{:S(2)}) copy-start(f32[832,256]{1,0:T(8,128)} %constant.14.clone.bank) | copy-start | bytes 2555908
  0.6 22.9 %copy-start.2 = (f32[5,256,128]{2,1,0:T(8,128)S(1)}, f32[5,256,128]{2,1,0:T(8,128)}, u32[]{:S(2)}) copy-start(f32[5,256,128]{2,1,0:T(8,128)} %constant.13.clone.refs_13_) | copy-start | bytes 1966084
  0.7 22.8 %copy-start.5 = (bf16[128,192]{1,0:T(8,128)(2,1)S(1)}, bf16[128,192]{1,0:T(8,128)(2,1)}, u32[]{:S(2)}) copy-start(bf16[128,192]{1,0:T(8,128)(2,1)} %constant.12.clone.refs_10_) | copy-start | bytes 147460
  0.7 22.8 %copy-start.3 = (bf16[2,512,256]{2,1,0:T(8,128)(2,1)S(1)}, bf16[2,512,256]{2,1,0:T(8,128)(2,1)}, u32[]{:S(2)}) copy-start(bf16[2,512,256]{2,1,0:T(8,128)(2,1)} %constant.11.clone.refs_15_) | copy-start | bytes 1572868
  0.7 8.3 %copy-start.1 = (f32[3,8]{1,0:T(4,128)S(1)}, f32[3,8]{1,0:T(4,128)}, u32[]{:S(2)}) copy-start(f32[3,8]{1,0:T(4,128)} %refs_1_.3) | copy-start | bytes 292
  3.2 7.0 %collective-permute-start = (f32[4,2048]{1,0:T(4,128)S(1)}, f32[4,2048]{1,0:T(4,128)S(1)}, u32[]{:S(2)}, u32[]{:S(2)}) collective-permute-start(f32[4,2048]{1,0:T(4,128)S(1)} %get-tuple-element.19), channel_id=1, source_target_pairs={{0,24},{8,16},{16,8},{24,0},{1,25},{9,17},{17,9},{25,1},{2,26},{10... | collective-permute-start | bytes 98312 | tf_op jit(solution)/shard_map/ppermute | solution.py:792
  8.3 4.8 %collective-permute-start.1 = (f32[4,2048]{1,0:T(4,128)S(1)}, f32[4,2048]{1,0:T(4,128)S(1)}, u32[]{:S(2)}, u32[]{:S(2)}) collective-permute-start(f32[4,2048]{1,0:T(4,128)S(1)} %get-tuple-element.20), channel_id=1, source_target_pairs={{0,16},{8,24},{16,0},{24,8},{1,17},{9,25},{17,1},{25,9},{2,18},{10... | collective-permute-start | bytes 98312 | tf_op jit(solution)/shard_map/ppermute | solution.py:792
  8.3 4.8 %collective-permute-start.2 = (f32[4,2048]{1,0:T(4,128)S(1)}, f32[4,2048]{1,0:T(4,128)S(1)}, u32[]{:S(2)}, u32[]{:S(2)}) collective-permute-start(f32[4,2048]{1,0:T(4,128)S(1)} %get-tuple-element.21), channel_id=1, source_target_pairs={{0,8},{8,0},{16,24},{24,16},{1,9},{9,1},{17,25},{25,17},{2,10},{10... | collective-permute-start | bytes 98312 | tf_op jit(solution)/shard_map/ppermute | solution.py:792
  13.8 7.3 %collective-permute-start.7 = (f32[4,64,128]{2,1,0:T(8,128)S(1)}, f32[4,64,128]{2,1,0:T(8,128)S(1)}, u32[]{:S(2)}, u32[]{:S(2)}) collective-permute-start(f32[4,64,128]{2,1,0:T(8,128)S(1)} %arrange.1.refs_2_), channel_id=1, source_target_pairs={{0,5},{1,4},{2,7},{3,6},{4,1},{5,0},{6,3},{7,2},{8,13},{9,12},{10,... | collective-permute-start | bytes 393224 | tf_op jit(solution)/shard_map/ppermute | solution.py:792
  16.4 5.6 %collective-permute-start.6 = (f32[4,64,128]{2,1,0:T(8,128)S(1)}, f32[4,64,128]{2,1,0:T(8,128)S(1)}, u32[]{:S(2)}, u32[]{:S(2)}) collective-permute-start(f32[4,64,128]{2,1,0:T(8,128)S(1)} %arrange.1.refs_2_), channel_id=1, source_target_pairs={{0,4},{1,5},{2,6},{3,7},{4,0},{5,1},{6,2},{7,3},{8,12},{9,13},{10,... | collective-permute-start | bytes 393224 | tf_op jit(solution)/shard_map/ppermute | solution.py:792
  16.9 5.1 %collective-permute-start.3 = (f32[4,64,128]{2,1,0:T(8,128)S(1)}, f32[4,64,128]{2,1,0:T(8,128)S(1)}, u32[]{:S(2)}, u32[]{:S(2)}) collective-permute-start(f32[4,64,128]{2,1,0:T(8,128)S(1)} %arrange.1.refs_2_), channel_id=1, source_target_pairs={{0,1},{1,0},{2,3},{3,2},{4,5},{5,4},{6,7},{7,6},{8,9},{9,8},{10,11... | collective-permute-start | bytes 393224 | tf_op jit(solution)/shard_map/ppermute | solution.py:792
  17.4 5.1 %collective-permute-start.4 = (f32[4,64,128]{2,1,0:T(8,128)S(1)}, f32[4,64,128]{2,1,0:T(8,128)S(1)}, u32[]{:S(2)}, u32[]{:S(2)}) collective-permute-start(f32[4,64,128]{2,1,0:T(8,128)S(1)} %arrange.1.refs_2_), channel_id=1, source_target_pairs={{0,2},{1,3},{2,0},{3,1},{4,6},{5,7},{6,4},{7,5},{8,10},{9,11},{10,... | collective-permute-start | bytes 393224 | tf_op jit(solution)/shard_map/ppermute | solution.py:792
  21.2 1.3 %collective-permute-start.9 = (f32[4,64,128]{2,1,0:T(8,128)S(1)}, f32[4,64,128]{2,1,0:T(8,128)S(1)}, u32[]{:S(2)}, u32[]{:S(2)}) collective-permute-start(f32[4,64,128]{2,1,0:T(8,128)S(1)} %collective-permute-done.7.refs_7_), channel_id=1, source_target_pairs={{0,2},{1,3},{2,0},{3,1},{4,6},{5,7},{6,4},{7,5},{8,10},{9,11},{10,... | collective-permute-start | bytes 393224 | tf_op jit(solution)/shard_map/ppermute | solution.py:792
  22.0 1.3 %collective-permute-start.8 = (f32[4,64,128]{2,1,0:T(8,128)S(1)}, f32[4,64,128]{2,1,0:T(8,128)S(1)}, u32[]{:S(2)}, u32[]{:S(2)}) collective-permute-start(f32[4,64,128]{2,1,0:T(8,128)S(1)} %collective-permute-done.6.refs_6_), channel_id=1, source_target_pairs={{0,2},{1,3},{2,0},{3,1},{4,6},{5,7},{6,4},{7,5},{8,10},{9,11},{10,... | collective-permute-start | bytes 393224 | tf_op jit(solution)/shard_map/ppermute | solution.py:792
  22.0 1.5 %collective-permute-start.5 = (f32[4,64,128]{2,1,0:T(8,128)S(1)}, f32[4,64,128]{2,1,0:T(8,128)S(1)}, u32[]{:S(2)}, u32[]{:S(2)}) collective-permute-start(f32[4,64,128]{2,1,0:T(8,128)S(1)} %collective-permute-done.3.refs_3_), channel_id=1, source_target_pairs={{0,2},{1,3},{2,0},{3,1},{4,6},{5,7},{6,4},{7,5},{8,10},{9,11},{10,... | collective-permute-start | bytes 393224 | tf_op jit(solution)/shard_map/ppermute | solution.py:792
  23.5 13.1 %copy-start.4 = (bf16[256,256]{1,0:T(8,128)(2,1)S(1)}, bf16[256,256]{1,0:T(8,128)(2,1)}, u32[]{:S(2)}) copy-start(bf16[256,256]{1,0:T(8,128)(2,1)} %constant.10.clone.iz) | copy-start | bytes 393220
  32.2 7.8 %collective-permute-start.10 = (f32[4,2048]{1,0:T(4,128)S(1)}, f32[4,2048]{1,0:T(4,128)S(1)}, u32[]{:S(2)}, u32[]{:S(2)}) collective-permute-start(f32[4,2048]{1,0:T(4,128)S(1)} %get-tuple-element.26), channel_id=1, source_target_pairs={{0,24},{8,16},{16,8},{24,0},{1,25},{9,17},{17,9},{25,1},{2,26},{10... | collective-permute-start | bytes 98312 | tf_op jit(solution)/shard_map/ppermute | solution.py:792
  33.6 6.4 %collective-permute-start.11 = (f32[4,2048]{1,0:T(4,128)S(1)}, f32[4,2048]{1,0:T(4,128)S(1)}, u32[]{:S(2)}, u32[]{:S(2)}) collective-permute-start(f32[4,2048]{1,0:T(4,128)S(1)} %get-tuple-element.27), channel_id=1, source_target_pairs={{0,16},{8,24},{16,0},{24,8},{1,17},{9,25},{17,1},{25,9},{2,18},{10... | collective-permute-start | bytes 98312 | tf_op jit(solution)/shard_map/ppermute | solution.py:792
  34.4 5.7 %collective-permute-start.12 = (f32[4,2048]{1,0:T(4,128)S(1)}, f32[4,2048]{1,0:T(4,128)S(1)}, u32[]{:S(2)}, u32[]{:S(2)}) collective-permute-start(f32[4,2048]{1,0:T(4,128)S(1)} %get-tuple-element.28), channel_id=1, source_target_pairs={{0,8},{8,0},{16,24},{24,16},{1,9},{9,1},{17,25},{25,17},{2,10},{10... | collective-permute-start | bytes 98312 | tf_op jit(solution)/shard_map/ppermute | solution.py:792

commit v4 on v3

--- a/solution.py
+++ b/solution.py
@@ -395,11 +395,13 @@
 
 
 def arrange_kernel(farm_count, pairs, info, gate, *refs):
-    tiles, out, stage = refs[:farm_count], refs[farm_count], refs[farm_count + 1]
+    tiles = refs[:farm_count]
+    piece, own, stage = refs[farm_count:]
     for shift in range(farm_count):
         stage[shift] = tiles[farm_count - 1 - shift][...]
     rows = stage.shape[1]
-    channels, width_x, lanes = out.shape
+    width_x, lanes = own.shape
+    channels = stage.shape[2] * pairs // (width_x * (lanes // rows))
     edge = width_x // pairs
     per = lanes // rows
     row_lanes = edge * per
@@ -412,7 +414,16 @@
                     [tile[:, base : base + lanes], tile[:, base + lanes : base + 2 * lanes]], 0
                 )
                 at = pair * edge + 2 * part * rows
-                out[channel, at : at + 2 * rows, :] = swap_blocks(block, rows, per)
+                if channel < channels - 1:
+                    at = channel * width_x + at
+                    piece[at : at + 2 * rows, :] = swap_blocks(block, rows, per)
+                else:
+                    own[at : at + 2 * rows, :] = swap_blocks(block, rows, per)
+    rolled = pltpu.roll(own[...], per, 1)
+    half = width_x // 2
+    front = lax.broadcasted_iota(jnp.int32, (half, lanes), 1) < lanes // 2
+    edges = jnp.where(front, rolled[0:half], pltpu.roll(rolled[half:], lanes // 2, 1))
+    piece[(channels - 1) * width_x :, :] = edges
 
 
 def prep_kernel(taps, bank, mats, rmats, wu, ww):
@@ -458,7 +469,8 @@
 
 
 def solve_kernel(farm_count, pairs, groups, info, taps, *refs):
-    pieces = refs[:groups]
+    blocks, own_q = refs[:groups], refs[groups]
+    refs = refs[:groups] + refs[groups + 1 :]
     (fx, wu, ww, planes, rmats, rz, tiles, spectrum) = refs[groups : groups + 8]
     outs = refs[groups + 8 : groups + 8 + farm_count]
     base = refs[groups + 8 + farm_count]
@@ -468,7 +480,13 @@
     take = pltpu.make_async_copy(tiles, shelf, sems.at[0])
     take.start()
     group = info[farm_count + pairs]
-    channels, width_x, lanes = pieces[0].shape
+    width_x, lanes = own_q.shape
+    channels = fresh.shape[0]
+    pieces = [
+        [block.at[pl.ds(channel * width_x, width_x)] for channel in range(channels - 1)]
+        + [block.at[pl.ds((channels - 1) * width_x, width_x // 2)]]
+        for block in blocks
+    ]
     rows = mean_p.shape[0]
     per = lanes // rows
     coarse_y = groups * rows
@@ -489,91 +507,103 @@
     following = group ^ ((group + 1) & (groups - 1))
 
     def beside(shift, channel):
-        value = pieces[1][channel]
+        value = pieces[1][channel][...]
         mark = 3
         while mark < groups:
-            value = jnp.where(shift == mark, pieces[mark][channel], value)
+            value = jnp.where(shift == mark, pieces[mark][channel][...], value)
             mark = 2 * mark + 1
         return value
 
-    for channel in range(channels):
-        here = pieces[0][channel]
-        before, after = beside(previous, channel), beside(following, channel)
-        lag, mid, lead = band(1)
-        low = jnp.where(lane < per, pltpu.roll(before, per, 1), pltpu.roll(here, per, 1))
-        high = jnp.where(
-            lane >= lanes - per, pltpu.roll(after, lanes - per, 1), pltpu.roll(here, lanes - per, 1)
-        )
-        value = mid * here + lag * low + lead * high
-        lag, mid, lead = band(2)
-        spot = lane % per
-        low = jnp.where(spot == 0, pltpu.roll(value, lanes - per + 1, 1), pltpu.roll(value, 1, 1))
-        high = jnp.where(
-            spot == per - 1, pltpu.roll(value, per - 1, 1), pltpu.roll(value, lanes - 1, 1)
-        )
-        value = mid * value + lag * low + lead * high
-        lag, mid, lead = band(0)
-        value = (
-            mid * value
-            + lag * pltpu.roll(value, 1, 0)
-            + lead * pltpu.roll(value, width_x - 1, 0)
-        )
-        fresh[channel] = value
+    @pl.when(group >= 0)
+    def _():
+        for channel in range(channels):
+            lag, mid, lead = band(1)
+            if channel < channels - 1:
+                here = pieces[0][channel][...]
+                before = pltpu.roll(beside(previous, channel), per, 1)
+                after = pltpu.roll(beside(following, channel), lanes - per, 1)
+            else:
+                here = own_q[...]
+                prior, later = beside(previous, channel), beside(following, channel)
+                before = jnp.concatenate([prior, pltpu.roll(prior, lanes // 2, 1)], 0)
+                after = jnp.concatenate([pltpu.roll(later, lanes // 2, 1), later], 0)
+            low = jnp.where(lane < per, before, pltpu.roll(here, per, 1))
+            high = jnp.where(lane >= lanes - per, after, pltpu.roll(here, lanes - per, 1))
+            value = mid * here + lag * low + lead * high
+            lag, mid, lead = band(2)
+            spot = lane % per
+            low = jnp.where(spot == 0, pltpu.roll(value, lanes - per + 1, 1), pltpu.roll(value, 1, 1))
+            high = jnp.where(
+                spot == per - 1, pltpu.roll(value, per - 1, 1), pltpu.roll(value, lanes - 1, 1)
+            )
+            value = mid * value + lag * low + lead * high
+            lag, mid, lead = band(0)
+            value = (
+                mid * value
+                + lag * pltpu.roll(value, 1, 0)
+                + lead * pltpu.roll(value, width_x - 1, 0)
+            )
+            fresh[channel] = value
     duo = lanes // 2
-    front = lax.broadcasted_iota(jnp.int32, (width_x, lanes), 1) < duo
     ahead_half = lax.broadcasted_iota(jnp.int32, (coarse_rows, lanes), 1) < duo
     for block in range(groups):
-        doubled = []
-        for channel in range(3):
-            value = pieces[block][channel]
-            turned = pltpu.roll(value, duo, 1)
-            doubled += [jnp.where(front, value, turned), jnp.where(front, turned, value)]
-        hi, lo = halves(jnp.concatenate(doubled, 1))
-        turned = mm(fx[...], jnp.concatenate([hi, lo, hi], 0))
-        for channel in range(3):
-            for pair in range(2):
-                at = (2 * channel + pair) * lanes
-                value = turned[:, at : at + lanes]
-                hi = value.astype(BF)
-                rest = jnp.where(ahead_half, value, value - hi.astype(F32)).astype(BF)
-                at = (2 * block + pair) * coarse_rows
-                left[channel, at : at + coarse_rows, :] = jnp.concatenate([rest, hi], 1)
+        @pl.when(group >= 0)
+        def _():
+            hi, lo = halves(jnp.concatenate([pieces[block][channel][...] for channel in range(3)], 1))
+            turned = mm(fx[...], jnp.concatenate([hi, lo, hi], 0))
+            for channel in range(3):
+                value = turned[:, channel * lanes : (channel + 1) * lanes]
+                moved = pltpu.roll(value, duo, 1)
+                twins = (
+                    jnp.where(ahead_half, value, moved),
+                    jnp.where(ahead_half, moved, value),
+                )
+                for pair in range(2):
+                    value = twins[pair]
+                    hi = value.astype(BF)
+                    rest = jnp.where(ahead_half, value, value - hi.astype(F32)).astype(BF)
+                    at = (2 * block + pair) * coarse_rows
+                    left[channel, at : at + coarse_rows, :] = jnp.concatenate([rest, hi], 1)
     chunk = min(groups, 4)
     for channel in range(3):
-        weight = ww if channel == 2 else wu
-        for block in range(0, groups, chunk):
-            at = 2 * block * coarse_rows
-            value = mm(left[channel, at : at + 2 * chunk * coarse_rows, :], weight[...])
-            for inner in range(chunk):
-                for row in range(rows):
-                    at_y = (((group ^ (block + inner)) - group) * rows + row) & (coarse_y - 1)
-                    at = (2 * inner + row // 2) * coarse_rows
-                    field[channel, at_y] = value[
-                        at : at + coarse_rows, (row % 2) * lanes : (row % 2 + 1) * lanes
-                    ]
-
-    sums = jnp.concatenate(
-        [jnp.sum(pieces[block][1], axis=0, keepdims=True) for block in range(groups)], 0
-    )
-    total_z = taps[2, 0]
-    for tap in range(1, TAPS):
-        total_z = total_z + taps[2, tap]
-    sums = sums * total_z
-    shape = (groups, lanes)
-    coarse_id = rows * (lax.broadcasted_iota(jnp.int32, shape, 0) ^ group)
-    coarse_id = coarse_id + lax.broadcasted_iota(jnp.int32, shape, 1) // per
-    corner = (lax.broadcasted_iota(jnp.int32, (8, lanes), 0) == 0) & (
-        lax.broadcasted_iota(jnp.int32, (8, lanes), 1) == 0
-    )
-    for index in range(own_fine + 1):
-        at = own_fine * group - 1 + index
-        weight = jnp.zeros(shape, F32)
-        for tap in range(TAPS):
-            gap = (at - REFINE * coarse_id + 2 - tap) & (fine_y - 1)
-            saw = 0.5 - (2 * gap + 1).astype(F32) * (0.5 / fine_y)
-            weight = weight + taps[1, tap] * saw
-        value = jnp.sum(jnp.sum(weight * sums, axis=1, keepdims=True), axis=0, keepdims=True)
-        zero_add[index] = jnp.where(corner, value, 0.0)
+        @pl.when(group >= 0)
+        def _():
+            weight = ww if channel == 2 else wu
+            for block in range(0, groups, chunk):
+                at = 2 * block * coarse_rows
+                value = mm(left[channel, at : at + 2 * chunk * coarse_rows, :], weight[...])
+                for inner in range(chunk):
+                    for row in range(rows):
+                        at_y = (((group ^ (block + inner)) - group) * rows + row) & (coarse_y - 1)
+                        at = (2 * inner + row // 2) * coarse_rows
+                        field[channel, at_y] = value[
+                            at : at + coarse_rows, (row % 2) * lanes : (row % 2 + 1) * lanes
+                        ]
+
+    @pl.when(group >= 0)
+    def _():
+        sums = jnp.concatenate(
+            [jnp.sum(pieces[block][1][...], axis=0, keepdims=True) for block in range(groups)], 0
+        )
+        total_z = taps[2, 0]
+        for tap in range(1, TAPS):
+            total_z = total_z + taps[2, tap]
+        sums = sums * total_z
+        shape = (groups, lanes)
+        coarse_id = rows * (lax.broadcasted_iota(jnp.int32, shape, 0) ^ group)
+        coarse_id = coarse_id + lax.broadcasted_iota(jnp.int32, shape, 1) // per
+        corner = (lax.broadcasted_iota(jnp.int32, (8, lanes), 0) == 0) & (
+            lax.broadcasted_iota(jnp.int32, (8, lanes), 1) == 0
+        )
+        for index in range(own_fine + 1):
+            at = own_fine * group - 1 + index
+            weight = jnp.zeros(shape, F32)
+            for tap in range(TAPS):
+                gap = (at - REFINE * coarse_id + 2 - tap) & (fine_y - 1)
+                saw = 0.5 - (2 * gap + 1).astype(F32) * (0.5 / fine_y)
+                weight = weight + taps[1, tap] * saw
+            value = jnp.sum(jnp.sum(weight * sums, axis=1, keepdims=True), axis=0, keepdims=True)
+            zero_add[index] = jnp.where(corner, value, 0.0)
 
     take.wait()
     give = pltpu.make_async_copy(shelf, base, sems.at[1])
@@ -715,19 +745,21 @@
 
     for channel in range(channels):
         fresh[channel] = fresh[channel] + change[channel]
-    shifts = [info[farm_count + pair] for pair in range(pairs)]
-    edge = width_x // pairs
-    row_lanes = edge * per
-    for pair in range(pairs):
-        for channel in range(channels):
-            for part in range(row_lanes // (2 * lanes)):
-                at = pair * edge + 2 * part * rows
-                block = swap_blocks(fresh[channel, at : at + 2 * rows, :], rows, per)
-                base = channel * row_lanes + 2 * part * lanes
-                out_stage[shifts[pair], :, base : base + lanes] = block[0:rows]
-                out_stage[shifts[pair], :, base + lanes : base + 2 * lanes] = block[rows:]
-    for shift in range(farm_count):
-        outs[shift][...] = out_stage[shift]
+    @pl.when(group >= 0)
+    def _():
+        shifts = [info[farm_count + pair] for pair in range(pairs)]
+        edge = width_x // pairs
+        row_lanes = edge * per
+        for pair in range(pairs):
+            for channel in range(channels):
+                for part in range(row_lanes // (2 * lanes)):
+                    at = pair * edge + 2 * part * rows
+                    block = swap_blocks(fresh[channel, at : at + 2 * rows, :], rows, per)
+                    base = channel * row_lanes + 2 * part * lanes
+                    out_stage[shifts[pair], :, base : base + lanes] = block[0:rows]
+                    out_stage[shifts[pair], :, base + lanes : base + 2 * lanes] = block[rows:]
+        for shift in range(farm_count):
+            outs[shift][...] = out_stage[shift]
     give.wait()
 
 
@@ -838,12 +870,15 @@
         cost_estimate=cost(0, 6 << 20),
     )(prolong_taps, const["bank"])
 
-    piece = pl.pallas_call(
+    piece, own = pl.pallas_call(
         bind(arrange_kernel, farm_count, pairs),
         name="arrange",
-        out_shape=jax.ShapeDtypeStruct((CH, width_x, lanes), F32),
+        out_shape=[
+            jax.ShapeDtypeStruct(((CH - 1) * width_x + width_x // 2, lanes), F32),
+            jax.ShapeDtypeStruct((width_x, lanes), F32),
+        ],
         in_specs=[in_smem(), anywhere()] + [in_vmem()] * farm_count,
-        out_specs=in_vmem(),
+        out_specs=[in_vmem()] * 2,
         scratch_shapes=[pltpu.VMEM((farm_count, rows, row_width), F32)],
         compiler_params=limit(8),
         cost_estimate=cost(0, 1 << 18),
@@ -864,7 +899,7 @@
         + [tile_shape] * farm_count
         + [jax.ShapeDtypeStruct(coarse_tiles.shape, F32)],
         in_specs=[in_smem()] * 2
-        + [in_vmem()] * (groups + 6)
+        + [in_vmem()] * (groups + 7)
         + [in_hbm()],
         out_specs=[in_vmem()] * (farm_count + 1) + [in_hbm()],
         scratch_shapes=[
@@ -883,6 +918,7 @@
     )(
         info, prolong_taps,
         *[held[s] for s in range(groups)],
+        own,
         const["fx"], wu, ww, const["planes"], rmats, const["rz"],
         keep_hbm(coarse_tiles),
     )

time: 41.5 us -> 39.8 us (0.959)
  Pallas kernels: 17.2 us -> 15.9 us
    pallas_call x1, Pallas kernels: 8.66 us -> 7.38 us  [fast_local(): pl.pallas_call(bind(solve_kernel, farm_count, pairs, groups), name='solve...]
where the time goes in v4:
time: 39.8 us; the launch traced here: 39.6 us
  Pallas kernels  15.9 us (40%)
  starting transfers between devices  14.2 us (36%)
  waiting for transfers between devices  8.67 us (22%)
  between operations  0.72 us (2%)
    ppermute x13, starting transfers between devices, flip(): return lax.ppermute(value, axis, [(i, i ^ bits) for i in range(count)])  14.2 us
    ppermute x13, waiting for transfers between devices, flip(): return lax.ppermute(value, axis, [(i, i ^ bits) for i in range(count)])  8.67 us
    pallas_call x1, Pallas kernels, fast_local(): pl.pallas_call(bind(solve_kernel, farm_count, pairs, groups), name='solve...  7.38 us
    pallas_call x1, Pallas kernels, fast_local(): pl.pallas_call(inverse_kernel, name='inverse', out_shape=jax.ShapeDtypeSt...  3.36 us
    pallas_call x1, Pallas kernels, fast_local(): pl.pallas_call(bind(pick_kernel, local_tiles, farm_count, pairs), name='p...  2.46 us
    pallas_call x1, Pallas kernels, fast_local(): pl.pallas_call(bind(patch_kernel, farm_count), name='patch', out_shape=ja...  1.23 us
  transfers between devices with their start and end apart: 13, of which 6 were waited for; matrix products, arithmetic and copies ran while one was open for 0% of the time, Pallas kernels for 10%

profile of v4, /device:TPU:0, one launch (start us, length us, event | category | flops | bytes accessed | tf_op | source)
XLA Modules:
  0.0 39.6 jit_solution(12452215860025082482)
XLA Ops:
  0.6 0.0 copy-start
  0.7 2.5 %pick.1 = (s32[9]{0:T(128)S(1)}, f32[4,2048]{1,0:T(4,128)S(1)}, f32[4,2048]{1,0:T(4,128)S(1)}, f32[4,2048]{1,0:T(4,128)S(1)}, f32[4,2048]{1,0:T(4,128)S(1)}) custom-call(s32[4,4]{1,0:T(4,128)} %refs_0_.1, s32[4]{0:T(128)} %refs_1_.2, f32[64,4,2048]{2,1,0:T(4,128)} %refs_17_.1), custom_call_target="tpu_custom_call" | custom-call | bytes 262144 | tf_op jit(solution)/shard_map/pick/pallas_call | solution.py:841
  3.2 5.1 %collective-permute-start = (f32[4,2048]{1,0:T(4,128)S(1)}, f32[4,2048]{1,0:T(4,128)S(1)}, u32[]{:S(2)}, u32[]{:S(2)}) collective-permute-start(f32[4,2048]{1,0:T(4,128)S(1)} %get-tuple-element.21), channel_id=1, source_target_pairs={{0,24},{8,16},{16,8},{24,0},{1,25},{9,17},{17,9},{25,1},{2,26},{10... | collective-permute-start | bytes 98312 | tf_op jit(solution)/shard_map/ppermute | solution.py:824
  8.3 0.6 %collective-permute-start.2 = (f32[4,2048]{1,0:T(4,128)S(1)}, f32[4,2048]{1,0:T(4,128)S(1)}, u32[]{:S(2)}, u32[]{:S(2)}) collective-permute-start(f32[4,2048]{1,0:T(4,128)S(1)} %get-tuple-element.23), channel_id=1, source_target_pairs={{0,8},{8,0},{16,24},{24,16},{1,9},{9,1},{17,25},{25,17},{2,10},{10... | collective-permute-start | bytes 98312 | tf_op jit(solution)/shard_map/ppermute | solution.py:824
  8.9 0.7 %prep.1 = (bf16[512,256]{1,0:T(8,128)(2,1)S(1)}, bf16[2,128,256]{2,1,0:T(8,128)(2,1)S(1)}, bf16[256,256]{1,0:T(8,128)(2,1)S(1)}, bf16[256,256]{1,0:T(8,128)(2,1)S(1)}) custom-call(f32[3,8]{1,0:T(4,128)S(1)} %copy-done.1, f32[832,256]{1,0:T(8,128)S(1)} %copy-done), custom_call_target="tpu_custom_call" | custom-call | bytes 6291456 | tf_op jit(solution)/shard_map/prep/pallas_call | solution.py:858
  9.7 0.5 %collective-permute-done.refs_2_ = f32[4,2048]{1,0:T(4,128)S(1)} collective-permute-done((f32[4,2048]{1,0:T(4,128)S(1)}, f32[4,2048]{1,0:T(4,128)S(1)}, u32[]{:S(2)}, u32[]{:S(2)}) %collective-permute-start) | collective-permute-done | bytes 32800 | tf_op jit(solution)/shard_map/ppermute | solution.py:824
  10.2 2.9 %collective-permute-done.1.refs_3_ = f32[4,2048]{1,0:T(4,128)S(1)} collective-permute-done((f32[4,2048]{1,0:T(4,128)S(1)}, f32[4,2048]{1,0:T(4,128)S(1)}, u32[]{:S(2)}, u32[]{:S(2)}) %collective-permute-start.1) | collective-permute-done | bytes 32800 | tf_op jit(solution)/shard_map/ppermute | solution.py:824
  13.1 0.8 %arrange.1 = (f32[224,128]{1,0:T(8,128)S(1)}, f32[64,128]{1,0:T(8,128)S(1)}) custom-call(s32[9]{0:T(128)S(1)} %get-tuple-element.19.refs_0_, bf16[2,128,256]{2,1,0:T(8,128)(2,1)S(1)} %get-tuple-element.20.refs_1_.refs_15_, f32[4,2048]{1,0:T(4,128)S(1)} %collective-permute-done.refs_2_, f32[4,2048]{1,0:T(4,128)S(1)} %collective-permute-done.1.refs_3_, ...), custom_call_target="tpu_custom_call" | custom-call | bytes 262144 | tf_op jit(solution)/shard_map/arrange/pallas_call | solution.py:873
  13.9 2.5 %collective-permute-start.7 = (f32[224,128]{1,0:T(8,128)S(1)}, f32[224,128]{1,0:T(8,128)S(1)}, u32[]{:S(2)}, u32[]{:S(2)}) collective-permute-start(f32[224,128]{1,0:T(8,128)S(1)} %get-tuple-element.25.refs_2_), channel_id=1, source_target_pairs={{0,5},{1,4},{2,7},{3,6},{4,1},{5,0},{6,3},{7,2},{8,13},{9,12},{10,... | collective-permute-start | bytes 344072 | tf_op jit(solution)/shard_map/ppermute | solution.py:824
  16.4 0.5 %collective-permute-start.6 = (f32[224,128]{1,0:T(8,128)S(1)}, f32[224,128]{1,0:T(8,128)S(1)}, u32[]{:S(2)}, u32[]{:S(2)}) collective-permute-start(f32[224,128]{1,0:T(8,128)S(1)} %get-tuple-element.25.refs_2_), channel_id=1, source_target_pairs={{0,4},{1,5},{2,6},{3,7},{4,0},{5,1},{6,2},{7,3},{8,12},{9,13},{10,... | collective-permute-start | bytes 344072 | tf_op jit(solution)/shard_map/ppermute | solution.py:824
  16.9 0.5 %collective-permute-start.3 = (f32[224,128]{1,0:T(8,128)S(1)}, f32[224,128]{1,0:T(8,128)S(1)}, u32[]{:S(2)}, u32[]{:S(2)}) collective-permute-start(f32[224,128]{1,0:T(8,128)S(1)} %get-tuple-element.25.refs_2_), channel_id=1, source_target_pairs={{0,1},{1,0},{2,3},{3,2},{4,5},{5,4},{6,7},{7,6},{8,9},{9,8},{10,11... | collective-permute-start | bytes 344072 | tf_op jit(solution)/shard_map/ppermute | solution.py:824
  17.4 3.4 %collective-permute-done.7.refs_7_ = f32[224,128]{1,0:T(8,128)S(1)} collective-permute-done((f32[224,128]{1,0:T(8,128)S(1)}, f32[224,128]{1,0:T(8,128)S(1)}, u32[]{:S(2)}, u32[]{:S(2)}) %collective-permute-start.7) | collective-permute-done | bytes 114720 | tf_op jit(solution)/shard_map/ppermute | solution.py:824
  20.8 0.8 %collective-permute-done.6.refs_6_ = f32[224,128]{1,0:T(8,128)S(1)} collective-permute-done((f32[224,128]{1,0:T(8,128)S(1)}, f32[224,128]{1,0:T(8,128)S(1)}, u32[]{:S(2)}, u32[]{:S(2)}) %collective-permute-start.6) | collective-permute-done | bytes 114720 | tf_op jit(solution)/shard_map/ppermute | solution.py:824
  21.6 0.0 collective-permute-done.3.refs_3_
  21.7 0.5 %collective-permute-start.5 = (f32[224,128]{1,0:T(8,128)S(1)}, f32[224,128]{1,0:T(8,128)S(1)}, u32[]{:S(2)}, u32[]{:S(2)}) collective-permute-start(f32[224,128]{1,0:T(8,128)S(1)} %collective-permute-done.3.refs_3_), channel_id=1, source_target_pairs={{0,2},{1,3},{2,0},{3,1},{4,6},{5,7},{6,4},{7,5},{8,10},{9,11},{10,... | collective-permute-start | bytes 344072 | tf_op jit(solution)/shard_map/ppermute | solution.py:824
  22.1 0.0 collective-permute-done.9.refs_9_
  22.2 0.8 %collective-permute-done.8.refs_8_ = f32[224,128]{1,0:T(8,128)S(1)} collective-permute-done((f32[224,128]{1,0:T(8,128)S(1)}, f32[224,128]{1,0:T(8,128)S(1)}, u32[]{:S(2)}, u32[]{:S(2)}) %collective-permute-start.8) | collective-permute-done | bytes 114720 | tf_op jit(solution)/shard_map/ppermute | solution.py:824
  23.0 0.2 collective-permute-done.5.refs_5_
  23.1 7.4 %solve.1 = (f32[16,256,128]{2,1,0:T(8,128)S(1)}, f32[4,2048]{1,0:T(4,128)S(1)}, f32[4,2048]{1,0:T(4,128)S(1)}, f32[4,2048]{1,0:T(4,128)S(1)}, f32[4,2048]{1,0:T(4,128)S(1)}, /*index=5*/f32[64,4,2048]{2,1,0:T(4,128)}) custom-call(s32[9]{0:T(128)S(1)} %get-tuple-element.19.refs_0_, f32[3,8]{1,0:T(4,128)S(1)} %copy-done.1, ...), custom_call_target="tpu_custom_call" | custom-call | flops 4294967296 | bytes 8388608 | tf_op jit(solution)/shard_map/solve/pallas_call | solution.py:895
  30.5 1.4 %collective-permute-start.10 = (f32[4,2048]{1,0:T(4,128)S(1)}, f32[4,2048]{1,0:T(4,128)S(1)}, u32[]{:S(2)}, u32[]{:S(2)}) collective-permute-start(f32[4,2048]{1,0:T(4,128)S(1)} %get-tuple-element.30), channel_id=1, source_target_pairs={{0,24},{8,16},{16,8},{24,0},{1,25},{9,17},{17,9},{25,1},{2,26},{10... | collective-permute-start | bytes 98312 | tf_op jit(solution)/shard_map/ppermute | solution.py:824
  31.9 0.8 %collective-permute-start.11 = (f32[4,2048]{1,0:T(4,128)S(1)}, f32[4,2048]{1,0:T(4,128)S(1)}, u32[]{:S(2)}, u32[]{:S(2)}) collective-permute-start(f32[4,2048]{1,0:T(4,128)S(1)} %get-tuple-element.31), channel_id=1, source_target_pairs={{0,16},{8,24},{16,0},{24,8},{1,17},{9,25},{17,1},{25,9},{2,18},{10... | collective-permute-start | bytes 98312 | tf_op jit(solution)/shard_map/ppermute | solution.py:824
  32.7 2.3 %collective-permute-start.12 = (f32[4,2048]{1,0:T(4,128)S(1)}, f32[4,2048]{1,0:T(4,128)S(1)}, u32[]{:S(2)}, u32[]{:S(2)}) collective-permute-start(f32[4,2048]{1,0:T(4,128)S(1)} %get-tuple-element.32), channel_id=1, source_target_pairs={{0,8},{8,0},{16,24},{24,16},{1,9},{9,1},{17,25},{25,17},{2,10},{10... | collective-permute-start | bytes 98312 | tf_op jit(solution)/shard_map/ppermute | solution.py:824
  35.0 3.4 %inverse.1 = f32[256,16,128]{2,1,0:T(8,128)} custom-call(bf16[256,256]{1,0:T(8,128)(2,1)S(1)} %copy-done.4, bf16[512,256]{1,0:T(8,128)(2,1)S(1)} %get-tuple-element.34.mats, f32[16,256,128]{2,1,0:T(8,128)S(1)} %get-tuple-element.35.spectrum), custom_call_target="tpu_custom_call" | custom-call | flops 4294967296 | bytes 4194304 | tf_op jit(solution)/shard_map/inverse/pallas_call | solution.py:928
  38.4 1.2 %patch.1 = f32[64,4,2048]{2,1,0:T(4,128)} custom-call(s32[9]{0:T(128)S(1)} %get-tuple-element.19.refs_0_, f32[64,4,2048]{2,1,0:T(4,128)} %get-tuple-element.29.refs_1_, f32[4,2048]{1,0:T(4,128)S(1)} %collective-permute-done.10.refs_2_, f32[4,2048]{1,0:T(4,128)S(1)} %collective-permute-done.11.refs_3_, ...), custom_call_target="tpu_custom_call", output_to_operand_aliasing={{}: (1, {})} | custom-call | bytes 262144 | tf_op jit(solution)/shard_map/patch/pallas_call | solution.py:944
  (20 shorter events, 0.1 us)
Async XLA Ops:
  0.6 8.3 %copy-start = (f32[832,256]{1,0:T(8,128)S(1)}, f32[832,256]{1,0:T(8,128)}, u32[]{:S(2)}) copy-start(f32[832,256]{1,0:T(8,128)} %constant.14.clone.bank) | copy-start | bytes 2555908
  0.6 22.5 %copy-start.2 = (f32[5,256,128]{2,1,0:T(8,128)S(1)}, f32[5,256,128]{2,1,0:T(8,128)}, u32[]{:S(2)}) copy-start(f32[5,256,128]{2,1,0:T(8,128)} %constant.13.clone.refs_14_) | copy-start | bytes 1966084
  0.7 22.5 %copy-start.5 = (bf16[128,192]{1,0:T(8,128)(2,1)S(1)}, bf16[128,192]{1,0:T(8,128)(2,1)}, u32[]{:S(2)}) copy-start(bf16[128,192]{1,0:T(8,128)(2,1)} %constant.12.clone.refs_11_) | copy-start | bytes 147460
  0.7 22.5 %copy-start.3 = (bf16[2,512,256]{2,1,0:T(8,128)(2,1)S(1)}, bf16[2,512,256]{2,1,0:T(8,128)(2,1)}, u32[]{:S(2)}) copy-start(bf16[2,512,256]{2,1,0:T(8,128)(2,1)} %constant.11.clone.refs_16_) | copy-start | bytes 1572868
  0.7 8.3 %copy-start.1 = (f32[3,8]{1,0:T(4,128)S(1)}, f32[3,8]{1,0:T(4,128)}, u32[]{:S(2)}) copy-start(f32[3,8]{1,0:T(4,128)} %refs_1_.3) | copy-start | bytes 292
  3.2 7.0 %collective-permute-start = (f32[4,2048]{1,0:T(4,128)S(1)}, f32[4,2048]{1,0:T(4,128)S(1)}, u32[]{:S(2)}, u32[]{:S(2)}) collective-permute-start(f32[4,2048]{1,0:T(4,128)S(1)} %get-tuple-element.21), channel_id=1, source_target_pairs={{0,24},{8,16},{16,8},{24,0},{1,25},{9,17},{17,9},{25,1},{2,26},{10... | collective-permute-start | bytes 98312 | tf_op jit(solution)/shard_map/ppermute | solution.py:824
  8.3 4.8 %collective-permute-start.1 = (f32[4,2048]{1,0:T(4,128)S(1)}, f32[4,2048]{1,0:T(4,128)S(1)}, u32[]{:S(2)}, u32[]{:S(2)}) collective-permute-start(f32[4,2048]{1,0:T(4,128)S(1)} %get-tuple-element.22), channel_id=1, source_target_pairs={{0,16},{8,24},{16,0},{24,8},{1,17},{9,25},{17,1},{25,9},{2,18},{10... | collective-permute-start | bytes 98312 | tf_op jit(solution)/shard_map/ppermute | solution.py:824
  8.3 4.8 %collective-permute-start.2 = (f32[4,2048]{1,0:T(4,128)S(1)}, f32[4,2048]{1,0:T(4,128)S(1)}, u32[]{:S(2)}, u32[]{:S(2)}) collective-permute-start(f32[4,2048]{1,0:T(4,128)S(1)} %get-tuple-element.23), channel_id=1, source_target_pairs={{0,8},{8,0},{16,24},{24,16},{1,9},{9,1},{17,25},{25,17},{2,10},{10... | collective-permute-start | bytes 98312 | tf_op jit(solution)/shard_map/ppermute | solution.py:824
  13.9 7.0 %collective-permute-start.7 = (f32[224,128]{1,0:T(8,128)S(1)}, f32[224,128]{1,0:T(8,128)S(1)}, u32[]{:S(2)}, u32[]{:S(2)}) collective-permute-start(f32[224,128]{1,0:T(8,128)S(1)} %get-tuple-element.25.refs_2_), channel_id=1, source_target_pairs={{0,5},{1,4},{2,7},{3,6},{4,1},{5,0},{6,3},{7,2},{8,13},{9,12},{10,... | collective-permute-start | bytes 344072 | tf_op jit(solution)/shard_map/ppermute | solution.py:824
  16.4 5.2 %collective-permute-start.6 = (f32[224,128]{1,0:T(8,128)S(1)}, f32[224,128]{1,0:T(8,128)S(1)}, u32[]{:S(2)}, u32[]{:S(2)}) collective-permute-start(f32[224,128]{1,0:T(8,128)S(1)} %get-tuple-element.25.refs_2_), channel_id=1, source_target_pairs={{0,4},{1,5},{2,6},{3,7},{4,0},{5,1},{6,2},{7,3},{8,12},{9,13},{10,... | collective-permute-start | bytes 344072 | tf_op jit(solution)/shard_map/ppermute | solution.py:824
  16.9 4.8 %collective-permute-start.3 = (f32[224,128]{1,0:T(8,128)S(1)}, f32[224,128]{1,0:T(8,128)S(1)}, u32[]{:S(2)}, u32[]{:S(2)}) collective-permute-start(f32[224,128]{1,0:T(8,128)S(1)} %get-tuple-element.25.refs_2_), channel_id=1, source_target_pairs={{0,1},{1,0},{2,3},{3,2},{4,5},{5,4},{6,7},{7,6},{8,9},{9,8},{10,11... | collective-permute-start | bytes 344072 | tf_op jit(solution)/shard_map/ppermute | solution.py:824
  17.4 4.7 %collective-permute-start.4 = (f32[224,128]{1,0:T(8,128)S(1)}, f32[224,128]{1,0:T(8,128)S(1)}, u32[]{:S(2)}, u32[]{:S(2)}) collective-permute-start(f32[224,128]{1,0:T(8,128)S(1)} %get-tuple-element.25.refs_2_), channel_id=1, source_target_pairs={{0,2},{1,3},{2,0},{3,1},{4,6},{5,7},{6,4},{7,5},{8,10},{9,11},{10,... | collective-permute-start | bytes 344072 | tf_op jit(solution)/shard_map/ppermute | solution.py:824
  20.8 1.3 %collective-permute-start.9 = (f32[224,128]{1,0:T(8,128)S(1)}, f32[224,128]{1,0:T(8,128)S(1)}, u32[]{:S(2)}, u32[]{:S(2)}) collective-permute-start(f32[224,128]{1,0:T(8,128)S(1)} %collective-permute-done.7.refs_7_), channel_id=1, source_target_pairs={{0,2},{1,3},{2,0},{3,1},{4,6},{5,7},{6,4},{7,5},{8,10},{9,11},{10,... | collective-permute-start | bytes 344072 | tf_op jit(solution)/shard_map/ppermute | solution.py:824
  21.6 1.3 %collective-permute-start.8 = (f32[224,128]{1,0:T(8,128)S(1)}, f32[224,128]{1,0:T(8,128)S(1)}, u32[]{:S(2)}, u32[]{:S(2)}) collective-permute-start(f32[224,128]{1,0:T(8,128)S(1)} %collective-permute-done.6.refs_6_), channel_id=1, source_target_pairs={{0,2},{1,3},{2,0},{3,1},{4,6},{5,7},{6,4},{7,5},{8,10},{9,11},{10,... | collective-permute-start | bytes 344072 | tf_op jit(solution)/shard_map/ppermute | solution.py:824
  21.7 1.4 %collective-permute-start.5 = (f32[224,128]{1,0:T(8,128)S(1)}, f32[224,128]{1,0:T(8,128)S(1)}, u32[]{:S(2)}, u32[]{:S(2)}) collective-permute-start(f32[224,128]{1,0:T(8,128)S(1)} %collective-permute-done.3.refs_3_), channel_id=1, source_target_pairs={{0,2},{1,3},{2,0},{3,1},{4,6},{5,7},{6,4},{7,5},{8,10},{9,11},{10,... | collective-permute-start | bytes 344072 | tf_op jit(solution)/shard_map/ppermute | solution.py:824
  23.1 11.9 %copy-start.4 = (bf16[256,256]{1,0:T(8,128)(2,1)S(1)}, bf16[256,256]{1,0:T(8,128)(2,1)}, u32[]{:S(2)}) copy-start(bf16[256,256]{1,0:T(8,128)(2,1)} %constant.10.clone.iz) | copy-start | bytes 393220
  30.5 7.8 %collective-permute-start.10 = (f32[4,2048]{1,0:T(4,128)S(1)}, f32[4,2048]{1,0:T(4,128)S(1)}, u32[]{:S(2)}, u32[]{:S(2)}) collective-permute-start(f32[4,2048]{1,0:T(4,128)S(1)} %get-tuple-element.30), channel_id=1, source_target_pairs={{0,24},{8,16},{16,8},{24,0},{1,25},{9,17},{17,9},{25,1},{2,26},{10... | collective-permute-start | bytes 98312 | tf_op jit(solution)/shard_map/ppermute | solution.py:824
  31.9 6.4 %collective-permute-start.11 = (f32[4,2048]{1,0:T(4,128)S(1)}, f32[4,2048]{1,0:T(4,128)S(1)}, u32[]{:S(2)}, u32[]{:S(2)}) collective-permute-start(f32[4,2048]{1,0:T(4,128)S(1)} %get-tuple-element.31), channel_id=1, source_target_pairs={{0,16},{8,24},{16,0},{24,8},{1,17},{9,25},{17,1},{25,9},{2,18},{10... | collective-permute-start | bytes 98312 | tf_op jit(solution)/shard_map/ppermute | solution.py:824
  32.7 5.7 %collective-permute-start.12 = (f32[4,2048]{1,0:T(4,128)S(1)}, f32[4,2048]{1,0:T(4,128)S(1)}, u32[]{:S(2)}, u32[]{:S(2)}) collective-permute-start(f32[4,2048]{1,0:T(4,128)S(1)} %get-tuple-element.32), channel_id=1, source_target_pairs={{0,8},{8,0},{16,24},{24,16},{1,9},{9,1},{17,25},{25,17},{2,10},{10... | collective-permute-start | bytes 98312 | tf_op jit(solution)/shard_map/ppermute | solution.py:824

commit v5 on v4

--- a/solution.py
+++ b/solution.py
@@ -332,21 +332,25 @@
 
 
 def find_tiles(me, lists, owner, local_tiles, farm_count, pairs):
-    found, shifts = [], []
+    found, shifts, held = [], [], []
+    size = jnp.int32(local_tiles)
+    for nest in range(farm_count):
+        tile = jnp.int32(0)
+        for pair in range(pairs):
+            entry = lists[nest, pair]
+            tile = jnp.where(lax.div(entry, size) == me, entry, tile)
+        held.append(tile)
     for shift in range(farm_count):
         target = me ^ shift
-        tile = jnp.int32(0)
-        for nest in range(farm_count):
-            for pair in range(pairs):
-                entry = lists[nest, pair]
-                hit = (owner[nest] == target) & (entry // local_tiles == me)
-                tile = jnp.where(hit, entry, tile)
+        tile = held[0]
+        for nest in range(1, farm_count):
+            tile = jnp.where(owner[nest] == target, held[nest], tile)
         found.append(tile - me * local_tiles)
     for pair in range(pairs):
         tile = jnp.int32(0)
         for nest in range(farm_count):
             tile = jnp.where(owner[nest] == me, lists[nest, pair], tile)
-        shifts.append((tile // local_tiles) ^ me)
+        shifts.append(lax.div(tile, size) ^ me)
     return found, shifts
 
 

time: 39.8 us -> 39.6 us (level)
  no operation moved by 1% of the time
where the time goes in v5:
time: 39.6 us; the launch traced here: 39.5 us
  Pallas kernels  15.8 us (40%)
  starting transfers between devices  14.2 us (36%)
  waiting for transfers between devices  8.67 us (22%)
  between operations  0.72 us (2%)
    ppermute x13, starting transfers between devices, flip(): return lax.ppermute(value, axis, [(i, i ^ bits) for i in range(count)])  14.2 us
    ppermute x13, waiting for transfers between devices, flip(): return lax.ppermute(value, axis, [(i, i ^ bits) for i in range(count)])  8.67 us
    pallas_call x1, Pallas kernels, fast_local(): pl.pallas_call(bind(solve_kernel, farm_count, pairs, groups), name='solve...  7.38 us
    pallas_call x1, Pallas kernels, fast_local(): pl.pallas_call(inverse_kernel, name='inverse', out_shape=jax.ShapeDtypeSt...  3.36 us
    pallas_call x1, Pallas kernels, fast_local(): pl.pallas_call(bind(pick_kernel, local_tiles, farm_count, pairs), name='p...  2.35 us
    pallas_call x1, Pallas kernels, fast_local(): pl.pallas_call(bind(patch_kernel, farm_count), name='patch', out_shape=ja...  1.23 us
  transfers between devices with their start and end apart: 13, of which 6 were waited for; matrix products, arithmetic and copies ran while one was open for 0% of the time, Pallas kernels for 10%

profile of v5, /device:TPU:0, one launch (start us, length us, event | category | flops | bytes accessed | tf_op | source)
XLA Modules:
  0.0 39.5 jit_solution(9211992567814110652)
XLA Ops:
  0.6 0.0 copy-start
  0.7 2.4 %pick.1 = (s32[9]{0:T(128)S(1)}, f32[4,2048]{1,0:T(4,128)S(1)}, f32[4,2048]{1,0:T(4,128)S(1)}, f32[4,2048]{1,0:T(4,128)S(1)}, f32[4,2048]{1,0:T(4,128)S(1)}) custom-call(s32[4,4]{1,0:T(4,128)} %refs_0_.1, s32[4]{0:T(128)} %refs_1_.2, f32[64,4,2048]{2,1,0:T(4,128)} %refs_17_.1), custom_call_target="tpu_custom_call" | custom-call | bytes 262144 | tf_op jit(solution)/shard_map/pick/pallas_call | solution.py:845
  3.1 5.1 %collective-permute-start = (f32[4,2048]{1,0:T(4,128)S(1)}, f32[4,2048]{1,0:T(4,128)S(1)}, u32[]{:S(2)}, u32[]{:S(2)}) collective-permute-start(f32[4,2048]{1,0:T(4,128)S(1)} %get-tuple-element.21), channel_id=1, source_target_pairs={{0,24},{8,16},{16,8},{24,0},{1,25},{9,17},{17,9},{25,1},{2,26},{10... | collective-permute-start | bytes 98312 | tf_op jit(solution)/shard_map/ppermute | solution.py:828
  8.2 0.6 %collective-permute-start.2 = (f32[4,2048]{1,0:T(4,128)S(1)}, f32[4,2048]{1,0:T(4,128)S(1)}, u32[]{:S(2)}, u32[]{:S(2)}) collective-permute-start(f32[4,2048]{1,0:T(4,128)S(1)} %get-tuple-element.23), channel_id=1, source_target_pairs={{0,8},{8,0},{16,24},{24,16},{1,9},{9,1},{17,25},{25,17},{2,10},{10... | collective-permute-start | bytes 98312 | tf_op jit(solution)/shard_map/ppermute | solution.py:828
  8.8 0.7 %prep.1 = (bf16[512,256]{1,0:T(8,128)(2,1)S(1)}, bf16[2,128,256]{2,1,0:T(8,128)(2,1)S(1)}, bf16[256,256]{1,0:T(8,128)(2,1)S(1)}, bf16[256,256]{1,0:T(8,128)(2,1)S(1)}) custom-call(f32[3,8]{1,0:T(4,128)S(1)} %copy-done.1, f32[832,256]{1,0:T(8,128)S(1)} %copy-done), custom_call_target="tpu_custom_call" | custom-call | bytes 6291456 | tf_op jit(solution)/shard_map/prep/pallas_call | solution.py:862
  9.6 0.5 %collective-permute-done.refs_2_ = f32[4,2048]{1,0:T(4,128)S(1)} collective-permute-done((f32[4,2048]{1,0:T(4,128)S(1)}, f32[4,2048]{1,0:T(4,128)S(1)}, u32[]{:S(2)}, u32[]{:S(2)}) %collective-permute-start) | collective-permute-done | bytes 32800 | tf_op jit(solution)/shard_map/ppermute | solution.py:828
  10.1 2.9 %collective-permute-done.1.refs_3_ = f32[4,2048]{1,0:T(4,128)S(1)} collective-permute-done((f32[4,2048]{1,0:T(4,128)S(1)}, f32[4,2048]{1,0:T(4,128)S(1)}, u32[]{:S(2)}, u32[]{:S(2)}) %collective-permute-start.1) | collective-permute-done | bytes 32800 | tf_op jit(solution)/shard_map/ppermute | solution.py:828
  13.0 0.8 %arrange.1 = (f32[224,128]{1,0:T(8,128)S(1)}, f32[64,128]{1,0:T(8,128)S(1)}) custom-call(s32[9]{0:T(128)S(1)} %get-tuple-element.19.refs_0_, bf16[2,128,256]{2,1,0:T(8,128)(2,1)S(1)} %get-tuple-element.20.refs_1_.refs_15_, f32[4,2048]{1,0:T(4,128)S(1)} %collective-permute-done.refs_2_, f32[4,2048]{1,0:T(4,128)S(1)} %collective-permute-done.1.refs_3_, ...), custom_call_target="tpu_custom_call" | custom-call | bytes 262144 | tf_op jit(solution)/shard_map/arrange/pallas_call | solution.py:877
  13.8 2.5 %collective-permute-start.7 = (f32[224,128]{1,0:T(8,128)S(1)}, f32[224,128]{1,0:T(8,128)S(1)}, u32[]{:S(2)}, u32[]{:S(2)}) collective-permute-start(f32[224,128]{1,0:T(8,128)S(1)} %get-tuple-element.25.refs_2_), channel_id=1, source_target_pairs={{0,5},{1,4},{2,7},{3,6},{4,1},{5,0},{6,3},{7,2},{8,13},{9,12},{10,... | collective-permute-start | bytes 344072 | tf_op jit(solution)/shard_map/ppermute | solution.py:828
  16.3 0.5 %collective-permute-start.6 = (f32[224,128]{1,0:T(8,128)S(1)}, f32[224,128]{1,0:T(8,128)S(1)}, u32[]{:S(2)}, u32[]{:S(2)}) collective-permute-start(f32[224,128]{1,0:T(8,128)S(1)} %get-tuple-element.25.refs_2_), channel_id=1, source_target_pairs={{0,4},{1,5},{2,6},{3,7},{4,0},{5,1},{6,2},{7,3},{8,12},{9,13},{10,... | collective-permute-start | bytes 344072 | tf_op jit(solution)/shard_map/ppermute | solution.py:828
  16.8 0.5 %collective-permute-start.3 = (f32[224,128]{1,0:T(8,128)S(1)}, f32[224,128]{1,0:T(8,128)S(1)}, u32[]{:S(2)}, u32[]{:S(2)}) collective-permute-start(f32[224,128]{1,0:T(8,128)S(1)} %get-tuple-element.25.refs_2_), channel_id=1, source_target_pairs={{0,1},{1,0},{2,3},{3,2},{4,5},{5,4},{6,7},{7,6},{8,9},{9,8},{10,11... | collective-permute-start | bytes 344072 | tf_op jit(solution)/shard_map/ppermute | solution.py:828
  17.3 3.4 %collective-permute-done.7.refs_7_ = f32[224,128]{1,0:T(8,128)S(1)} collective-permute-done((f32[224,128]{1,0:T(8,128)S(1)}, f32[224,128]{1,0:T(8,128)S(1)}, u32[]{:S(2)}, u32[]{:S(2)}) %collective-permute-start.7) | collective-permute-done | bytes 114720 | tf_op jit(solution)/shard_map/ppermute | solution.py:828
  20.7 0.8 %collective-permute-done.6.refs_6_ = f32[224,128]{1,0:T(8,128)S(1)} collective-permute-done((f32[224,128]{1,0:T(8,128)S(1)}, f32[224,128]{1,0:T(8,128)S(1)}, u32[]{:S(2)}, u32[]{:S(2)}) %collective-permute-start.6) | collective-permute-done | bytes 114720 | tf_op jit(solution)/shard_map/ppermute | solution.py:828
  21.5 0.0 collective-permute-done.3.refs_3_
  21.6 0.5 %collective-permute-start.5 = (f32[224,128]{1,0:T(8,128)S(1)}, f32[224,128]{1,0:T(8,128)S(1)}, u32[]{:S(2)}, u32[]{:S(2)}) collective-permute-start(f32[224,128]{1,0:T(8,128)S(1)} %collective-permute-done.3.refs_3_), channel_id=1, source_target_pairs={{0,2},{1,3},{2,0},{3,1},{4,6},{5,7},{6,4},{7,5},{8,10},{9,11},{10,... | collective-permute-start | bytes 344072 | tf_op jit(solution)/shard_map/ppermute | solution.py:828
  22.0 0.0 collective-permute-done.9.refs_9_
  22.1 0.8 %collective-permute-done.8.refs_8_ = f32[224,128]{1,0:T(8,128)S(1)} collective-permute-done((f32[224,128]{1,0:T(8,128)S(1)}, f32[224,128]{1,0:T(8,128)S(1)}, u32[]{:S(2)}, u32[]{:S(2)}) %collective-permute-start.8) | collective-permute-done | bytes 114720 | tf_op jit(solution)/shard_map/ppermute | solution.py:828
  22.8 0.2 collective-permute-done.5.refs_5_
  23.0 7.4 %solve.1 = (f32[16,256,128]{2,1,0:T(8,128)S(1)}, f32[4,2048]{1,0:T(4,128)S(1)}, f32[4,2048]{1,0:T(4,128)S(1)}, f32[4,2048]{1,0:T(4,128)S(1)}, f32[4,2048]{1,0:T(4,128)S(1)}, /*index=5*/f32[64,4,2048]{2,1,0:T(4,128)}) custom-call(s32[9]{0:T(128)S(1)} %get-tuple-element.19.refs_0_, f32[3,8]{1,0:T(4,128)S(1)} %copy-done.1, ...), custom_call_target="tpu_custom_call" | custom-call | flops 4294967296 | bytes 8388608 | tf_op jit(solution)/shard_map/solve/pallas_call | solution.py:899
  30.4 1.4 %collective-permute-start.10 = (f32[4,2048]{1,0:T(4,128)S(1)}, f32[4,2048]{1,0:T(4,128)S(1)}, u32[]{:S(2)}, u32[]{:S(2)}) collective-permute-start(f32[4,2048]{1,0:T(4,128)S(1)} %get-tuple-element.30), channel_id=1, source_target_pairs={{0,24},{8,16},{16,8},{24,0},{1,25},{9,17},{17,9},{25,1},{2,26},{10... | collective-permute-start | bytes 98312 | tf_op jit(solution)/shard_map/ppermute | solution.py:828
  31.8 0.8 %collective-permute-start.11 = (f32[4,2048]{1,0:T(4,128)S(1)}, f32[4,2048]{1,0:T(4,128)S(1)}, u32[]{:S(2)}, u32[]{:S(2)}) collective-permute-start(f32[4,2048]{1,0:T(4,128)S(1)} %get-tuple-element.31), channel_id=1, source_target_pairs={{0,16},{8,24},{16,0},{24,8},{1,17},{9,25},{17,1},{25,9},{2,18},{10... | collective-permute-start | bytes 98312 | tf_op jit(solution)/shard_map/ppermute | solution.py:828
  32.6 2.3 %collective-permute-start.12 = (f32[4,2048]{1,0:T(4,128)S(1)}, f32[4,2048]{1,0:T(4,128)S(1)}, u32[]{:S(2)}, u32[]{:S(2)}) collective-permute-start(f32[4,2048]{1,0:T(4,128)S(1)} %get-tuple-element.32), channel_id=1, source_target_pairs={{0,8},{8,0},{16,24},{24,16},{1,9},{9,1},{17,25},{25,17},{2,10},{10... | collective-permute-start | bytes 98312 | tf_op jit(solution)/shard_map/ppermute | solution.py:828
  34.9 3.4 %inverse.1 = f32[256,16,128]{2,1,0:T(8,128)} custom-call(bf16[256,256]{1,0:T(8,128)(2,1)S(1)} %copy-done.4, bf16[512,256]{1,0:T(8,128)(2,1)S(1)} %get-tuple-element.34.mats, f32[16,256,128]{2,1,0:T(8,128)S(1)} %get-tuple-element.35.spectrum), custom_call_target="tpu_custom_call" | custom-call | flops 4294967296 | bytes 4194304 | tf_op jit(solution)/shard_map/inverse/pallas_call | solution.py:932
  38.2 1.2 %patch.1 = f32[64,4,2048]{2,1,0:T(4,128)} custom-call(s32[9]{0:T(128)S(1)} %get-tuple-element.19.refs_0_, f32[64,4,2048]{2,1,0:T(4,128)} %get-tuple-element.29.refs_1_, f32[4,2048]{1,0:T(4,128)S(1)} %collective-permute-done.10.refs_2_, f32[4,2048]{1,0:T(4,128)S(1)} %collective-permute-done.11.refs_3_, ...), custom_call_target="tpu_custom_call", output_to_operand_aliasing={{}: (1, {})} | custom-call | bytes 262144 | tf_op jit(solution)/shard_map/patch/pallas_call | solution.py:948
  (20 shorter events, 0.1 us)
Async XLA Ops:
  0.6 8.2 %copy-start = (f32[832,256]{1,0:T(8,128)S(1)}, f32[832,256]{1,0:T(8,128)}, u32[]{:S(2)}) copy-start(f32[832,256]{1,0:T(8,128)} %constant.14.clone.bank) | copy-start | bytes 2555908
  0.6 22.4 %copy-start.2 = (f32[5,256,128]{2,1,0:T(8,128)S(1)}, f32[5,256,128]{2,1,0:T(8,128)}, u32[]{:S(2)}) copy-start(f32[5,256,128]{2,1,0:T(8,128)} %constant.13.clone.refs_14_) | copy-start | bytes 1966084
  0.7 22.4 %copy-start.5 = (bf16[128,192]{1,0:T(8,128)(2,1)S(1)}, bf16[128,192]{1,0:T(8,128)(2,1)}, u32[]{:S(2)}) copy-start(bf16[128,192]{1,0:T(8,128)(2,1)} %constant.12.clone.refs_11_) | copy-start | bytes 147460
  0.7 22.3 %copy-start.3 = (bf16[2,512,256]{2,1,0:T(8,128)(2,1)S(1)}, bf16[2,512,256]{2,1,0:T(8,128)(2,1)}, u32[]{:S(2)}) copy-start(bf16[2,512,256]{2,1,0:T(8,128)(2,1)} %constant.11.clone.refs_16_) | copy-start | bytes 1572868
  0.7 8.2 %copy-start.1 = (f32[3,8]{1,0:T(4,128)S(1)}, f32[3,8]{1,0:T(4,128)}, u32[]{:S(2)}) copy-start(f32[3,8]{1,0:T(4,128)} %refs_1_.3) | copy-start | bytes 292
  3.1 7.0 %collective-permute-start = (f32[4,2048]{1,0:T(4,128)S(1)}, f32[4,2048]{1,0:T(4,128)S(1)}, u32[]{:S(2)}, u32[]{:S(2)}) collective-permute-start(f32[4,2048]{1,0:T(4,128)S(1)} %get-tuple-element.21), channel_id=1, source_target_pairs={{0,24},{8,16},{16,8},{24,0},{1,25},{9,17},{17,9},{25,1},{2,26},{10... | collective-permute-start | bytes 98312 | tf_op jit(solution)/shard_map/ppermute | solution.py:828
  8.2 4.8 %collective-permute-start.1 = (f32[4,2048]{1,0:T(4,128)S(1)}, f32[4,2048]{1,0:T(4,128)S(1)}, u32[]{:S(2)}, u32[]{:S(2)}) collective-permute-start(f32[4,2048]{1,0:T(4,128)S(1)} %get-tuple-element.22), channel_id=1, source_target_pairs={{0,16},{8,24},{16,0},{24,8},{1,17},{9,25},{17,1},{25,9},{2,18},{10... | collective-permute-start | bytes 98312 | tf_op jit(solution)/shard_map/ppermute | solution.py:828
  8.2 4.8 %collective-permute-start.2 = (f32[4,2048]{1,0:T(4,128)S(1)}, f32[4,2048]{1,0:T(4,128)S(1)}, u32[]{:S(2)}, u32[]{:S(2)}) collective-permute-start(f32[4,2048]{1,0:T(4,128)S(1)} %get-tuple-element.23), channel_id=1, source_target_pairs={{0,8},{8,0},{16,24},{24,16},{1,9},{9,1},{17,25},{25,17},{2,10},{10... | collective-permute-start | bytes 98312 | tf_op jit(solution)/shard_map/ppermute | solution.py:828
  13.8 7.0 %collective-permute-start.7 = (f32[224,128]{1,0:T(8,128)S(1)}, f32[224,128]{1,0:T(8,128)S(1)}, u32[]{:S(2)}, u32[]{:S(2)}) collective-permute-start(f32[224,128]{1,0:T(8,128)S(1)} %get-tuple-element.25.refs_2_), channel_id=1, source_target_pairs={{0,5},{1,4},{2,7},{3,6},{4,1},{5,0},{6,3},{7,2},{8,13},{9,12},{10,... | collective-permute-start | bytes 344072 | tf_op jit(solution)/shard_map/ppermute | solution.py:828
  16.3 5.2 %collective-permute-start.6 = (f32[224,128]{1,0:T(8,128)S(1)}, f32[224,128]{1,0:T(8,128)S(1)}, u32[]{:S(2)}, u32[]{:S(2)}) collective-permute-start(f32[224,128]{1,0:T(8,128)S(1)} %get-tuple-element.25.refs_2_), channel_id=1, source_target_pairs={{0,4},{1,5},{2,6},{3,7},{4,0},{5,1},{6,2},{7,3},{8,12},{9,13},{10,... | collective-permute-start | bytes 344072 | tf_op jit(solution)/shard_map/ppermute | solution.py:828
  16.8 4.8 %collective-permute-start.3 = (f32[224,128]{1,0:T(8,128)S(1)}, f32[224,128]{1,0:T(8,128)S(1)}, u32[]{:S(2)}, u32[]{:S(2)}) collective-permute-start(f32[224,128]{1,0:T(8,128)S(1)} %get-tuple-element.25.refs_2_), channel_id=1, source_target_pairs={{0,1},{1,0},{2,3},{3,2},{4,5},{5,4},{6,7},{7,6},{8,9},{9,8},{10,11... | collective-permute-start | bytes 344072 | tf_op jit(solution)/shard_map/ppermute | solution.py:828
  17.3 4.7 %collective-permute-start.4 = (f32[224,128]{1,0:T(8,128)S(1)}, f32[224,128]{1,0:T(8,128)S(1)}, u32[]{:S(2)}, u32[]{:S(2)}) collective-permute-start(f32[224,128]{1,0:T(8,128)S(1)} %get-tuple-element.25.refs_2_), channel_id=1, source_target_pairs={{0,2},{1,3},{2,0},{3,1},{4,6},{5,7},{6,4},{7,5},{8,10},{9,11},{10,... | collective-permute-start | bytes 344072 | tf_op jit(solution)/shard_map/ppermute | solution.py:828
  20.7 1.3 %collective-permute-start.9 = (f32[224,128]{1,0:T(8,128)S(1)}, f32[224,128]{1,0:T(8,128)S(1)}, u32[]{:S(2)}, u32[]{:S(2)}) collective-permute-start(f32[224,128]{1,0:T(8,128)S(1)} %collective-permute-done.7.refs_7_), channel_id=1, source_target_pairs={{0,2},{1,3},{2,0},{3,1},{4,6},{5,7},{6,4},{7,5},{8,10},{9,11},{10,... | collective-permute-start | bytes 344072 | tf_op jit(solution)/shard_map/ppermute | solution.py:828
  21.5 1.3 %collective-permute-start.8 = (f32[224,128]{1,0:T(8,128)S(1)}, f32[224,128]{1,0:T(8,128)S(1)}, u32[]{:S(2)}, u32[]{:S(2)}) collective-permute-start(f32[224,128]{1,0:T(8,128)S(1)} %collective-permute-done.6.refs_6_), channel_id=1, source_target_pairs={{0,2},{1,3},{2,0},{3,1},{4,6},{5,7},{6,4},{7,5},{8,10},{9,11},{10,... | collective-permute-start | bytes 344072 | tf_op jit(solution)/shard_map/ppermute | solution.py:828
  21.6 1.4 %collective-permute-start.5 = (f32[224,128]{1,0:T(8,128)S(1)}, f32[224,128]{1,0:T(8,128)S(1)}, u32[]{:S(2)}, u32[]{:S(2)}) collective-permute-start(f32[224,128]{1,0:T(8,128)S(1)} %collective-permute-done.3.refs_3_), channel_id=1, source_target_pairs={{0,2},{1,3},{2,0},{3,1},{4,6},{5,7},{6,4},{7,5},{8,10},{9,11},{10,... | collective-permute-start | bytes 344072 | tf_op jit(solution)/shard_map/ppermute | solution.py:828
  23.0 11.9 %copy-start.4 = (bf16[256,256]{1,0:T(8,128)(2,1)S(1)}, bf16[256,256]{1,0:T(8,128)(2,1)}, u32[]{:S(2)}) copy-start(bf16[256,256]{1,0:T(8,128)(2,1)} %constant.10.clone.iz) | copy-start | bytes 393220
  30.4 7.8 %collective-permute-start.10 = (f32[4,2048]{1,0:T(4,128)S(1)}, f32[4,2048]{1,0:T(4,128)S(1)}, u32[]{:S(2)}, u32[]{:S(2)}) collective-permute-start(f32[4,2048]{1,0:T(4,128)S(1)} %get-tuple-element.30), channel_id=1, source_target_pairs={{0,24},{8,16},{16,8},{24,0},{1,25},{9,17},{17,9},{25,1},{2,26},{10... | collective-permute-start | bytes 98312 | tf_op jit(solution)/shard_map/ppermute | solution.py:828
  31.8 6.4 %collective-permute-start.11 = (f32[4,2048]{1,0:T(4,128)S(1)}, f32[4,2048]{1,0:T(4,128)S(1)}, u32[]{:S(2)}, u32[]{:S(2)}) collective-permute-start(f32[4,2048]{1,0:T(4,128)S(1)} %get-tuple-element.31), channel_id=1, source_target_pairs={{0,16},{8,24},{16,0},{24,8},{1,17},{9,25},{17,1},{25,9},{2,18},{10... | collective-permute-start | bytes 98312 | tf_op jit(solution)/shard_map/ppermute | solution.py:828
  32.6 5.7 %collective-permute-start.12 = (f32[4,2048]{1,0:T(4,128)S(1)}, f32[4,2048]{1,0:T(4,128)S(1)}, u32[]{:S(2)}, u32[]{:S(2)}) collective-permute-start(f32[4,2048]{1,0:T(4,128)S(1)} %get-tuple-element.32), channel_id=1, source_target_pairs={{0,8},{8,0},{16,24},{24,16},{1,9},{9,1},{17,25},{25,17},{2,10},{10... | collective-permute-start | bytes 98312 | tf_op jit(solution)/shard_map/ppermute | solution.py:828
